TPU v7x, 256 devices: a whole 4x4x8 slice. The times are simulated.
256 devices in a mesh: section: 8 (over z), expert: 32 (over y, x, core).
Axes of the slice: x: 4, y: 4, z: 8, core: 2. Of those that a mesh axis runs over, the one named last changes fastest.
Arguments:
- features: bfloat16 [2, 2048, 2048], P(None, 'expert'), may hold values from -6 to 6
- labels: int32 [2, 2048], P(None, 'expert'), may hold values 0 or 1
- routes: int32 [8, 2, 2048, 1], P('section', None, 'expert'), may hold values from 0 to 31; in each aligned block of 64 rows (0 to 63, 64 to 127, ..., all dimensions but the last counted through in order) at most 3 rows name the same one
- route_gates: float32 [8, 2, 2048], P('section', None, 'expert'), may hold values from 0.25 to 1
- gate_weight: bfloat16 [8, 32, 2048, 256], P('section', 'expert'), may hold values from -0.125 to 0.125
- up_weight: bfloat16 [8, 32, 2048, 256], P('section', 'expert'), may hold values from -0.125 to 0.125
- down_weight: bfloat16 [8, 32, 256, 2048], P('section', 'expert'), may hold values from -0.375 to 0.375
- lowrank_in: bfloat16 [8, 2048, 128], P('section'), may hold values from -0.125 to 0.125
- lowrank_out: bfloat16 [8, 128, 2048], P('section'), may hold values from -0.5 to 0.5
- head_weight: float32 [2048], replicated, may hold values from -0.5 to 0.5
Outputs:
- grad_gate: float32 [8, 32, 2048, 256], P('section', 'expert')
- grad_up: float32 [8, 32, 2048, 256], P('section', 'expert')
- grad_down: float32 [8, 32, 256, 2048], P('section', 'expert')
- grad_lowrank_in: float32 [8, 2048, 128], P('section', 'expert')
- grad_lowrank_out: float32 [8, 128, 2048], P('section', None, 'expert')
Inputs may be any that keep to these rules, and one draw needn't show every extreme that they name: `routes`: in each layer and micro-batch the 64 rows of one device name one expert at most 3 times, and 3 is reached in every draw.
All inputs are finite; a program needn't handle non-finite values. No bound on the sum of `labels` on one device may be relied on, other than what follows from the above.
Results may differ from a plain program's by a relative error of at most 0.04.
Values may be sent and summed in bfloat16 or wider, within the bound.
No kernel may reach another device: no remote copies, remote signals or barrier semaphores. Data moves between devices by JAX's collectives and lax.ppermute only.
A program may use at most 128 MiB of HBM per device.

v0:
```python
import jax
import jax.numpy as jnp
from jax import lax
from jax.sharding import PartitionSpec as P

epsilon = 1e-06


def shifted(value, axis, steps):
    count = lax.axis_size(axis)
    first, last = (max(0, -steps), min(count, count - steps))
    return lax.ppermute(value, axis, [(source, source + steps) for source in range(first, last)])


def rms_scale(values):
    widened = values.astype(jnp.float32)
    return lax.rsqrt(jnp.mean(widened * widened, axis=-1, keepdims=True) + epsilon)


def norm_back(values, row_scale, grad_norm):
    widened = values.astype(jnp.float32)
    inner_mean = jnp.mean(grad_norm * widened, axis=-1, keepdims=True)
    return row_scale * grad_norm - widened * (row_scale * row_scale * row_scale) * inner_mean


def expert_forward(slot_rows, gate_mat, up_mat, down_mat):
    gate_pre = jnp.dot(slot_rows, gate_mat, preferred_element_type=jnp.float32)
    up_pre = jnp.dot(slot_rows, up_mat, preferred_element_type=jnp.float32)
    hidden = (gate_pre * jax.nn.sigmoid(gate_pre) * up_pre).astype(jnp.bfloat16)
    return jnp.dot(hidden, down_mat, preferred_element_type=jnp.float32).astype(jnp.bfloat16)


def expert_backward(slot_rows, grad_out, gate_mat, up_mat, down_mat):
    gate_pre = jnp.dot(slot_rows, gate_mat, preferred_element_type=jnp.float32)
    up_pre = jnp.dot(slot_rows, up_mat, preferred_element_type=jnp.float32)
    gate_sig = jax.nn.sigmoid(gate_pre)
    gate_act = gate_pre * gate_sig
    hidden = (gate_act * up_pre).astype(jnp.bfloat16)
    grad_hidden = jnp.dot(grad_out, down_mat.T, preferred_element_type=jnp.float32)
    grad_gate = (grad_hidden * up_pre * (gate_sig * (1.0 + gate_pre * (1.0 - gate_sig)))).astype(
        jnp.bfloat16
    )
    grad_up = (grad_hidden * gate_act).astype(jnp.bfloat16)
    grad_slots = (
        jnp.dot(grad_gate, gate_mat.T, preferred_element_type=jnp.float32)
        + jnp.dot(grad_up, up_mat.T, preferred_element_type=jnp.float32)
    ).astype(jnp.bfloat16)
    part_gate = jnp.dot(slot_rows.T, grad_gate, preferred_element_type=jnp.float32)
    part_up = jnp.dot(slot_rows.T, grad_up, preferred_element_type=jnp.float32)
    part_down = jnp.dot(hidden.T, grad_out, preferred_element_type=jnp.float32)
    return (grad_slots, part_gate, part_up, part_down)


def lowrank_parts(values, matrix_in):
    row_scale = rms_scale(values)
    normed = (values.astype(jnp.float32) * row_scale).astype(jnp.bfloat16)
    inner_pre = jnp.dot(normed, matrix_in, preferred_element_type=jnp.float32)
    inner_sig = jax.nn.sigmoid(inner_pre)
    inner_act = (inner_pre * inner_sig).astype(jnp.bfloat16)
    return (row_scale, normed, inner_pre, inner_sig, inner_act)


def lowrank_forward(values, matrix_in, matrix_out):
    row_scale, normed, inner_pre, inner_sig, inner_act = lowrank_parts(values, matrix_in)
    return (
        values.astype(jnp.float32)
        + jnp.dot(inner_act, matrix_out, preferred_element_type=jnp.float32)
    ).astype(jnp.bfloat16)


def lowrank_backward(values, grad_rows, matrix_in, matrix_out):
    row_scale, normed, inner_pre, inner_sig, inner_act = lowrank_parts(values, matrix_in)
    grad_act = jnp.dot(grad_rows, matrix_out.T, preferred_element_type=jnp.float32)
    grad_pre = (grad_act * (inner_sig * (1.0 + inner_pre * (1.0 - inner_sig)))).astype(jnp.bfloat16)
    grad_norm = jnp.dot(grad_pre, matrix_in.T, preferred_element_type=jnp.float32)
    grad_input = (grad_rows.astype(jnp.float32) + norm_back(values, row_scale, grad_norm)).astype(
        jnp.bfloat16
    )
    part_in = jnp.dot(normed.T, grad_pre, preferred_element_type=jnp.float32)
    part_out = jnp.dot(inner_act.T, grad_rows, preferred_element_type=jnp.float32)
    return (grad_input, part_in, part_out)


def head_grad(values, targets, head_weight):
    row_scale = rms_scale(values)
    logits = row_scale[:, 0] * jnp.sum(values.astype(jnp.float32) * head_weight[None, :], axis=1)
    grad_logit = jax.nn.sigmoid(logits) - targets.astype(jnp.float32)
    return norm_back(values, row_scale, grad_logit[:, None] * head_weight[None, :]).astype(
        jnp.bfloat16
    )


def route_table(expert_ids, expert_count, capacity):
    chosen = (expert_ids[:, None] == jnp.arange(expert_count, dtype=jnp.int32)[None, :]).astype(
        jnp.int32
    )
    ranking = jnp.cumsum(chosen, axis=0) - 1
    slot_index = jnp.sum(chosen * ranking, axis=1)
    target_slot = expert_ids * capacity + slot_index
    slot_grid = jnp.arange(expert_count * capacity, dtype=jnp.int32)
    return (slot_grid[:, None] == target_slot[None, :]).astype(jnp.bfloat16)


def spread_rows(table, values, expert_count, capacity):
    placed = jnp.dot(table, values, preferred_element_type=jnp.float32).astype(jnp.bfloat16)
    return placed.reshape(expert_count, capacity, values.shape[1])


def gather_rows(table, buffer):
    flat_rows = buffer.reshape(-1, buffer.shape[-1])
    return lax.dot_general(
        table, flat_rows, (((0,), (0,)), ((), ())), preferred_element_type=jnp.float32
    )


def local(
    features,
    labels,
    routes,
    route_gates,
    gate_weight,
    up_weight,
    down_weight,
    lowrank_in,
    lowrank_out,
    head_weight,
):
    section_count = lax.axis_size("section")
    section_index = lax.axis_index("section")
    expert_count = lax.axis_size("expert")
    micro_count, row_count, feature_width = features.shape
    capacity = min(row_count, max(2, 3 * row_count // (2 * expert_count)))
    last_section = section_count - 1
    gate_mat = gate_weight[0, 0]
    up_mat = up_weight[0, 0]
    down_mat = down_weight[0, 0]
    inner_in = lowrank_in[0]
    inner_out = lowrank_out[0]
    route_ids = routes[0, :, :, 0]
    gate_values = route_gates[0]
    zero_rows = jnp.zeros((row_count, feature_width), jnp.bfloat16)
    zero_store = jnp.zeros((micro_count, row_count, feature_width), jnp.bfloat16)
    zero_slots = jnp.zeros((micro_count, expert_count, capacity, feature_width), jnp.bfloat16)

    def window_slot(tick_id, offset):
        micro_id = tick_id - offset
        active = (micro_id >= 0) & (micro_id < micro_count)
        return (jnp.clip(micro_id, 0, micro_count - 1), active)

    def pick_micro(stored, micro_id):
        return lax.dynamic_index_in_dim(stored, micro_id, 0, keepdims=False)

    def store_micro(stored, micro_id, active, values):
        previous = pick_micro(stored, micro_id)
        return lax.dynamic_update_index_in_dim(
            stored, jnp.where(active, values, previous), micro_id, 0
        )

    def send_down(values):
        return shifted(values, "section", 1)

    def send_up(values):
        return shifted(values, "section", -1)

    def grads_forward(values):
        return shifted(values, "section", 1)

    def grads_backward(values):
        return shifted(values, "section", -1)

    def expert_layer(values, expert_ids, gate_row):
        row_scale = rms_scale(values)
        normed = (values.astype(jnp.float32) * row_scale).astype(jnp.bfloat16)
        table = route_table(expert_ids, expert_count, capacity)
        outgoing = spread_rows(table, normed, expert_count, capacity)
        received = lax.all_to_all(outgoing, "expert", split_axis=0, concat_axis=0, tiled=True)
        flat_rows = received.reshape(-1, feature_width)
        served = expert_forward(flat_rows, gate_mat, up_mat, down_mat)
        returned = lax.all_to_all(
            served.reshape(received.shape), "expert", split_axis=0, concat_axis=0, tiled=True
        )
        returned, kept_slots = (returned, received)
        layer_out = values.astype(jnp.float32) + gate_row[:, None] * gather_rows(table, returned)
        return (layer_out.astype(jnp.bfloat16), kept_slots)

    def expert_layer_back(values, grad_rows, expert_ids, gate_row, kept_slots, active):
        row_scale = rms_scale(values)
        table = route_table(expert_ids, expert_count, capacity)
        grad_out = (gate_row[:, None] * grad_rows.astype(jnp.float32)).astype(jnp.bfloat16)
        grad_buffer = spread_rows(table, grad_out, expert_count, capacity)
        slot_grads = lax.all_to_all(grad_buffer, "expert", split_axis=0, concat_axis=0, tiled=True)
        operands = (kept_slots.reshape(-1, feature_width), slot_grads.reshape(-1, feature_width))
        grad_slots, part_gate, part_up, part_down = expert_backward(
            operands[0], operands[1], gate_mat, up_mat, down_mat
        )
        factor = active.astype(jnp.float32)
        part_gate = part_gate * factor
        part_up = part_up * factor
        part_down = part_down * factor
        returned = lax.all_to_all(
            grad_slots.reshape(kept_slots.shape), "expert", split_axis=0, concat_axis=0, tiled=True
        )
        grad_norm = gather_rows(table, returned)
        grad_input = (
            grad_rows.astype(jnp.float32) + norm_back(values, row_scale, grad_norm)
        ).astype(jnp.bfloat16)
        return (grad_input, part_gate, part_up, part_down)

    def expert_tick(tick_id, down_input, saved_down, saved_slots):
        micro_id, active = window_slot(tick_id, section_index)
        entering = pick_micro(features, jnp.clip(tick_id, 0, micro_count - 1))
        rows_in = jnp.where(section_index == 0, entering, down_input)
        layer_out, kept_slots = expert_layer(
            rows_in, pick_micro(route_ids, micro_id), pick_micro(gate_values, micro_id)
        )
        saved_down = store_micro(saved_down, micro_id, active, rows_in)
        saved_slots = store_micro(saved_slots, micro_id, active, kept_slots)
        return (layer_out, saved_down, saved_slots)

    def lowrank_tick(tick_id, up_input, saved_up, final_rows):
        micro_id, active = window_slot(tick_id, 2 * section_count - 1 - section_index)
        layer_out = lowrank_forward(up_input, inner_in, inner_out)
        saved_up = store_micro(saved_up, micro_id, active, up_input)
        final_rows = store_micro(final_rows, micro_id, active & (section_index == 0), layer_out)
        return (layer_out, saved_up, final_rows)

    def first_leg(tick_id, loop_state):
        down_input, up_input, saved_down, saved_slots = loop_state
        layer_out, saved_down, saved_slots = expert_tick(
            tick_id, down_input, saved_down, saved_slots
        )
        return (send_down(layer_out), layer_out, saved_down, saved_slots)

    down_input, up_input, saved_down, saved_slots = lax.fori_loop(
        0, section_count, first_leg, (zero_rows, zero_rows, zero_store, zero_slots)
    )
    saved_up = zero_store
    final_rows = zero_store
    tick_id = 8
    expert_out, saved_down, saved_slots = expert_tick(tick_id, down_input, saved_down, saved_slots)
    lowrank_out_rows, saved_up, final_rows = lowrank_tick(tick_id, up_input, saved_up, final_rows)
    down_input = send_down(expert_out)
    up_input = jnp.where(section_index == last_section, expert_out, send_up(lowrank_out_rows))

    def second_leg(tick_id, loop_state):
        up_input, saved_up, final_rows = loop_state
        layer_out, saved_up, final_rows = lowrank_tick(tick_id, up_input, saved_up, final_rows)
        return (send_up(layer_out), saved_up, final_rows)

    up_input, saved_up, final_rows = lax.fori_loop(
        section_count + micro_count - 1,
        2 * section_count + micro_count - 1,
        second_leg,
        (up_input, saved_up, final_rows),
    )
    top_grads = head_grad(
        final_rows.reshape(-1, feature_width), labels.reshape(-1), head_weight
    ).reshape(micro_count, row_count, feature_width)

    def lowrank_back_tick(tick_id, grad_input, sum_in, sum_out):
        micro_id, active = window_slot(tick_id, section_index)
        entering = pick_micro(top_grads, jnp.clip(tick_id, 0, micro_count - 1))
        grad_rows = jnp.where(section_index == 0, entering, grad_input)
        grad_next, part_in, part_out = lowrank_backward(
            pick_micro(saved_up, micro_id), grad_rows, inner_in, inner_out
        )
        factor = active.astype(jnp.float32)
        return (grad_next, sum_in + factor * part_in, sum_out + factor * part_out)

    def expert_back_tick(tick_id, grad_input, grad_sums):
        micro_id, active = window_slot(tick_id, 2 * section_count - 1 - section_index)
        grad_next, part_gate, part_up, part_down = expert_layer_back(
            pick_micro(saved_down, micro_id),
            grad_input,
            pick_micro(route_ids, micro_id),
            pick_micro(gate_values, micro_id),
            pick_micro(saved_slots, micro_id),
            active,
        )
        return (
            grad_next,
            (grad_sums[0] + part_gate, grad_sums[1] + part_up, grad_sums[2] + part_down),
        )

    zero_in = jnp.zeros(inner_in.shape, jnp.float32)
    zero_out = jnp.zeros(inner_out.shape, jnp.float32)

    def back_first(tick_id, loop_state):
        grad_up_rows, grad_down_rows, sum_in, sum_out = loop_state
        grad_next, sum_in, sum_out = lowrank_back_tick(tick_id, grad_up_rows, sum_in, sum_out)
        return (grads_forward(grad_next), grad_next, sum_in, sum_out)

    grad_up_rows, grad_down_rows, sum_in, sum_out = lax.fori_loop(
        0, section_count, back_first, (zero_rows, zero_rows, zero_in, zero_out)
    )
    grad_sums = (
        jnp.zeros(gate_mat.shape, jnp.float32),
        jnp.zeros(up_mat.shape, jnp.float32),
        jnp.zeros(down_mat.shape, jnp.float32),
    )
    tick_id = 8
    expert_grad, grad_sums = expert_back_tick(tick_id, grad_down_rows, grad_sums)
    lowrank_grad, sum_in, sum_out = lowrank_back_tick(tick_id, grad_up_rows, sum_in, sum_out)
    grad_up_rows = grads_forward(lowrank_grad)
    grad_down_rows = jnp.where(
        section_index == last_section, lowrank_grad, grads_backward(expert_grad)
    )

    def back_second(tick_id, loop_state):
        grad_next, grad_sums = expert_back_tick(tick_id, loop_state[0], loop_state[1:])
        return (grads_backward(grad_next),) + grad_sums

    loop_result = lax.fori_loop(
        section_count + micro_count - 1,
        2 * section_count + micro_count - 1,
        back_second,
        (grad_down_rows,) + grad_sums,
    )
    sum_gate, sum_up, sum_down = (loop_result[1], loop_result[2], loop_result[3])
    share_in, share_out = (
        lax.psum_scatter(
            sum_in.astype(jnp.bfloat16), "expert", scatter_dimension=0, tiled=True
        ).astype(jnp.float32),
        lax.psum_scatter(
            sum_out.astype(jnp.bfloat16), "expert", scatter_dimension=1, tiled=True
        ).astype(jnp.float32),
    )
    return (
        sum_gate[None, None],
        sum_up[None, None],
        sum_down[None, None],
        share_in[None],
        share_out[None],
    )


def solution(mesh):
    return jax.shard_map(
        local,
        mesh=mesh,
        in_specs=(
            P(None, "expert", None),
            P(None, "expert"),
            P("section", None, "expert", None),
            P("section", None, "expert"),
            P("section", "expert", None, None),
            P("section", "expert", None, None),
            P("section", "expert", None, None),
            P("section", None, None),
            P("section", None, None),
            P(),
        ),
        out_specs=(
            P("section", "expert", None, None),
            P("section", "expert", None, None),
            P("section", "expert", None, None),
            P("section", "expert", None),
            P("section", None, "expert"),
        ),
        check_vma=False,
    )
```

profile of v0, /device:TPU:1, one launch (start us, length us, event | category | flops | bytes accessed | tf_op | source)
XLA Modules:
  0.0 1395.3 jit_solution(13711304845578169861)
XLA Ops:
  11.0 468.3 %while.82 = (s32[]{:T(128)}, bf16[64,2048]{1,0:T(8,128)(2,1)}, bf16[64,2048]{1,0:T(8,128)(2,1)}, bf16[2,64,2048]{2,1,0:T(8,128)(2,1)}, bf16[2,32,3,2048]{3,2,1,0...) while((s32[]{:T(128)}, bf16[64,2048]{1,0:T(8,128)(2,1)}, ...), condition=%wide.region_4.5_spmd, body=%wide.region_0.4_spmd.sunk | while | flops 354785408 | bytes 17929328 | solution.py:234
  15.7 20.1 %all_to_all.72 = bf16[32,3,2048]{2,1,0:T(4,128)(2,1)S(1)} all-to-all(bf16[32,3,2048]{2,1,0:T(4,128)(2,1)} %reshape.435), channel_id=1, replica_groups=mesh['section'=8,'expert'=32] {'expert'}, dimensions={0} | all-to-all | bytes 786432 | tf_op jit(solution)/shard_map/while/body/eval_jaxpr/all_to_all | solution.py:176
  49.9 9.6 all-to-all-done.1
  76.4 16.5 %all_to_all.72 = bf16[32,3,2048]{2,1,0:T(4,128)(2,1)S(1)} all-to-all(bf16[32,3,2048]{2,1,0:T(4,128)(2,1)} %reshape.435), channel_id=1, replica_groups=mesh['section'=8,'expert'=32] {'expert'}, dimensions={0} | all-to-all | bytes 786432 | tf_op jit(solution)/shard_map/while/body/eval_jaxpr/all_to_all | solution.py:176
  106.9 9.6 all-to-all-done.1
  134.0 16.5 %all_to_all.72 = bf16[32,3,2048]{2,1,0:T(4,128)(2,1)S(1)} all-to-all(bf16[32,3,2048]{2,1,0:T(4,128)(2,1)} %reshape.435), channel_id=1, replica_groups=mesh['section'=8,'expert'=32] {'expert'}, dimensions={0} | all-to-all | bytes 786432 | tf_op jit(solution)/shard_map/while/body/eval_jaxpr/all_to_all | solution.py:176
  164.6 9.6 all-to-all-done.1
  191.7 16.5 %all_to_all.72 = bf16[32,3,2048]{2,1,0:T(4,128)(2,1)S(1)} all-to-all(bf16[32,3,2048]{2,1,0:T(4,128)(2,1)} %reshape.435), channel_id=1, replica_groups=mesh['section'=8,'expert'=32] {'expert'}, dimensions={0} | all-to-all | bytes 786432 | tf_op jit(solution)/shard_map/while/body/eval_jaxpr/all_to_all | solution.py:176
  222.2 9.6 all-to-all-done.1
  249.4 16.5 %all_to_all.72 = bf16[32,3,2048]{2,1,0:T(4,128)(2,1)S(1)} all-to-all(bf16[32,3,2048]{2,1,0:T(4,128)(2,1)} %reshape.435), channel_id=1, replica_groups=mesh['section'=8,'expert'=32] {'expert'}, dimensions={0} | all-to-all | bytes 786432 | tf_op jit(solution)/shard_map/while/body/eval_jaxpr/all_to_all | solution.py:176
  279.9 9.6 all-to-all-done.1
  307.4 16.5 %all_to_all.72 = bf16[32,3,2048]{2,1,0:T(4,128)(2,1)S(1)} all-to-all(bf16[32,3,2048]{2,1,0:T(4,128)(2,1)} %reshape.435), channel_id=1, replica_groups=mesh['section'=8,'expert'=32] {'expert'}, dimensions={0} | all-to-all | bytes 786432 | tf_op jit(solution)/shard_map/while/body/eval_jaxpr/all_to_all | solution.py:176
  366.3 16.5 %all_to_all.72 = bf16[32,3,2048]{2,1,0:T(4,128)(2,1)S(1)} all-to-all(bf16[32,3,2048]{2,1,0:T(4,128)(2,1)} %reshape.435), channel_id=1, replica_groups=mesh['section'=8,'expert'=32] {'expert'}, dimensions={0} | all-to-all | bytes 786432 | tf_op jit(solution)/shard_map/while/body/eval_jaxpr/all_to_all | solution.py:176
  425.2 16.5 %all_to_all.72 = bf16[32,3,2048]{2,1,0:T(4,128)(2,1)S(1)} all-to-all(bf16[32,3,2048]{2,1,0:T(4,128)(2,1)} %reshape.435), channel_id=1, replica_groups=mesh['section'=8,'expert'=32] {'expert'}, dimensions={0} | all-to-all | bytes 786432 | tf_op jit(solution)/shard_map/while/body/eval_jaxpr/all_to_all | solution.py:176
  499.3 11.6 all-to-all-done.4
  540.1 119.7 %while.83 = (s32[]{:T(128)}, bf16[64,2048]{1,0:T(8,128)(2,1)S(1)}, bf16[2,64,2048]{2,1,0:T(8,128)(2,1)S(1)}, bf16[2,64,2048]{2,1,0:T(8,128)(2,1)}, bf16[2048,128...) while((s32[]{:T(128)}, bf16[64,2048]{1,0:T(8,128)(2,1)S(1)}, ...), condition=%wide.region_11.12_spmd, body=%wide.region_9.11_spmd.sunk | while | flops 68591688 | bytes 6030839 | solution.py:250
  545.8 11.3 collective-permute-done.1
  563.7 10.0 collective-permute-done.1
  666.7 106.6 %while.85 = (s32[]{:T(128)}, bf16[64,2048]{1,0:T(8,128)(2,1)}, bf16[64,2048]{1,0:T(8,128)(2,1)}, f32[2048,128]{1,0:T(8,128)}, f32[128,2048]{1,0:T(8,128)}, /*ind...) while((s32[]{:T(128)}, bf16[64,2048]{1,0:T(8,128)(2,1)}, ...), condition=%wide.region_18.19_spmd.clone, body=%wide.region_15.18_spmd.clone.sunk | while | flops 172212416 | bytes 19550060 | solution.py:293
  789.0 20.7 %all-to-all-start.6 = ((bf16[32,3,2048]{2,1,0:T(4,128)(2,1)}), bf16[32,3,2048]{2,1,0:T(4,128)(2,1)}, u32[]{:S(2)}, u32[]{:S(2)}) async-start(bf16[32,3,2048]{2,1,0:T(4,128)(2,1)} %reshape.414), calls=%async_computation.6 | async-start | bytes 1048576 | tf_op jit(solution)/shard_map/all_to_all | solution.py:191
  811.6 9.9 all-to-all-done.6
  852.2 31.9 %reduce-scatter.5.cloned.1.call-done = bf16[128,64]{0,1:T(8,128)(2,1)} async-done(((bf16[128,2048]{0,1:T(8,128)(2,1)}), bf16[128,64]{0,1:T(8,128)(2,1)}) %reduce-scatter.5.cloned.1.call-update) | async-done | bytes 16400 | tf_op jit(solution)/shard_map/reduce_scatter | solution.py:324
  885.5 86.4 %reduce-scatter.3.cloned.1.call-done = bf16[64,128]{1,0:T(8,128)(2,1)} async-done(((bf16[2048,128]{1,0:T(8,128)(2,1)}), bf16[64,128]{1,0:T(8,128)(2,1)}) %reduce-scatter.3.cloned.1.call-update) | async-done | bytes 16400 | tf_op jit(solution)/shard_map/reduce_scatter | solution.py:321
  975.4 413.1 %while.84 = (s32[]{:T(128)}, bf16[64,2048]{1,0:T(8,128)(2,1)S(1)}, f32[2048,256]{1,0:T(8,128)}, f32[2048,256]{1,0:T(8,128)}, f32[256,2048]{1,0:T(8,128)}, /*inde...) while((s32[]{:T(128)}, bf16[64,2048]{1,0:T(8,128)(2,1)S(1)}, ...), condition=%wide.region_30.31_spmd, body=%wide.region_25.30_spmd.sunk | while | flops 862091520 | bytes 53680440 | solution.py:313
  (892 shorter events, 1012.5 us)
Async XLA Ops:
  43.2 16.4 %all-to-all-start.1 = ((bf16[32,3,2048]{2,1,0:T(4,128)(2,1)}), bf16[32,3,2048]{2,1,0:T(4,128)(2,1)}, u32[]{:S(2)}, u32[]{:S(2)}) async-start(bf16[32,3,2048]{2,1,0:T(4,128)(2,1)} %reshape.437), calls=%async_computation.1 | async-start | bytes 1048576 | tf_op jit(solution)/shard_map/while/body/eval_jaxpr/all_to_all | solution.py:179
  100.2 16.4 %all-to-all-start.1 = ((bf16[32,3,2048]{2,1,0:T(4,128)(2,1)}), bf16[32,3,2048]{2,1,0:T(4,128)(2,1)}, u32[]{:S(2)}, u32[]{:S(2)}) async-start(bf16[32,3,2048]{2,1,0:T(4,128)(2,1)} %reshape.437), calls=%async_computation.1 | async-start | bytes 1048576 | tf_op jit(solution)/shard_map/while/body/eval_jaxpr/all_to_all | solution.py:179
  157.8 16.4 %all-to-all-start.1 = ((bf16[32,3,2048]{2,1,0:T(4,128)(2,1)}), bf16[32,3,2048]{2,1,0:T(4,128)(2,1)}, u32[]{:S(2)}, u32[]{:S(2)}) async-start(bf16[32,3,2048]{2,1,0:T(4,128)(2,1)} %reshape.437), calls=%async_computation.1 | async-start | bytes 1048576 | tf_op jit(solution)/shard_map/while/body/eval_jaxpr/all_to_all | solution.py:179
  215.5 16.4 %all-to-all-start.1 = ((bf16[32,3,2048]{2,1,0:T(4,128)(2,1)}), bf16[32,3,2048]{2,1,0:T(4,128)(2,1)}, u32[]{:S(2)}, u32[]{:S(2)}) async-start(bf16[32,3,2048]{2,1,0:T(4,128)(2,1)} %reshape.437), calls=%async_computation.1 | async-start | bytes 1048576 | tf_op jit(solution)/shard_map/while/body/eval_jaxpr/all_to_all | solution.py:179
  273.2 16.4 %all-to-all-start.1 = ((bf16[32,3,2048]{2,1,0:T(4,128)(2,1)}), bf16[32,3,2048]{2,1,0:T(4,128)(2,1)}, u32[]{:S(2)}, u32[]{:S(2)}) async-start(bf16[32,3,2048]{2,1,0:T(4,128)(2,1)} %reshape.437), calls=%async_computation.1 | async-start | bytes 1048576 | tf_op jit(solution)/shard_map/while/body/eval_jaxpr/all_to_all | solution.py:179
  331.2 16.4 %all-to-all-start.1 = ((bf16[32,3,2048]{2,1,0:T(4,128)(2,1)}), bf16[32,3,2048]{2,1,0:T(4,128)(2,1)}, u32[]{:S(2)}, u32[]{:S(2)}) async-start(bf16[32,3,2048]{2,1,0:T(4,128)(2,1)} %reshape.437), calls=%async_computation.1 | async-start | bytes 1048576 | tf_op jit(solution)/shard_map/while/body/eval_jaxpr/all_to_all | solution.py:179
  390.1 16.4 %all-to-all-start.1 = ((bf16[32,3,2048]{2,1,0:T(4,128)(2,1)}), bf16[32,3,2048]{2,1,0:T(4,128)(2,1)}, u32[]{:S(2)}, u32[]{:S(2)}) async-start(bf16[32,3,2048]{2,1,0:T(4,128)(2,1)} %reshape.437), calls=%async_computation.1 | async-start | bytes 1048576 | tf_op jit(solution)/shard_map/while/body/eval_jaxpr/all_to_all | solution.py:179
  449.0 16.4 %all-to-all-start.1 = ((bf16[32,3,2048]{2,1,0:T(4,128)(2,1)}), bf16[32,3,2048]{2,1,0:T(4,128)(2,1)}, u32[]{:S(2)}, u32[]{:S(2)}) async-start(bf16[32,3,2048]{2,1,0:T(4,128)(2,1)} %reshape.437), calls=%async_computation.1 | async-start | bytes 1048576 | tf_op jit(solution)/shard_map/while/body/eval_jaxpr/all_to_all | solution.py:179
  482.9 55.7 %collective-permute-start.4 = (bf16[64,2048]{1,0:T(8,128)(2,1)}, bf16[64,2048]{1,0:T(8,128)(2,1)}, u32[]{:S(2)}, u32[]{:S(2)}) collective-permute-start(bf16[64,2048]{1,0:T(8,128)(2,1)} %get-tuple-element.1165), channel_id=1, source_target_pairs={{32,0},{64,32},{96,64},{128,96},{160,128},{192,160},{224,192},{33,... | collective-permute-start | bytes 786440 | tf_op jit(solution)/shard_map/ppermute | solution.py:12
  493.6 17.2 %all-to-all-start.4 = ((bf16[32,3,2048]{2,1,0:T(4,128)(2,1)}), bf16[32,3,2048]{2,1,0:T(4,128)(2,1)}, u32[]{:S(2)}, u32[]{:S(2)}) async-start(bf16[32,3,2048]{2,1,0:T(4,128)(2,1)} %reshape.410), calls=%async_computation.4 | async-start | bytes 1048576 | tf_op jit(solution)/shard_map/all_to_all | solution.py:176
  520.3 16.4 %all-to-all-start.5 = ((bf16[32,3,2048]{2,1,0:T(4,128)(2,1)}), bf16[32,3,2048]{2,1,0:T(4,128)(2,1)}, u32[]{:S(2)}, u32[]{:S(2)}) async-start(bf16[32,3,2048]{2,1,0:T(4,128)(2,1)} %reshape.412), calls=%async_computation.5 | async-start | bytes 1048576 | tf_op jit(solution)/shard_map/all_to_all | solution.py:179
  524.9 359.2 %reduce-scatter.5.cloned.1.call-start = ((), (), s32[]{:S(2)}) async-start(), calls=%async_computation.11 | async-start | bytes 540672 | tf_op jit(solution)/shard_map/reduce_scatter | solution.py:324
  780.0 191.9 %reduce-scatter.3.cloned.1.call-start = ((), (), s32[]{:S(2)}) async-start(), calls=%async_computation.10 | async-start | bytes 540672 | tf_op jit(solution)/shard_map/reduce_scatter | solution.py:321
  789.0 32.5 %all-to-all-start.6 = ((bf16[32,3,2048]{2,1,0:T(4,128)(2,1)}), bf16[32,3,2048]{2,1,0:T(4,128)(2,1)}, u32[]{:S(2)}, u32[]{:S(2)}) async-start(bf16[32,3,2048]{2,1,0:T(4,128)(2,1)} %reshape.414), calls=%async_computation.6 | async-start | bytes 1048576 | tf_op jit(solution)/shard_map/all_to_all | solution.py:191
  830.1 16.5 %all-to-all-start.7 = ((bf16[32,3,2048]{2,1,0:T(4,128)(2,1)}), bf16[32,3,2048]{2,1,0:T(4,128)(2,1)}, u32[]{:S(2)}, u32[]{:S(2)}) async-start(bf16[32,3,2048]{2,1,0:T(4,128)(2,1)} %reshape.417), calls=%async_computation.7 | async-start | bytes 1048576 | tf_op jit(solution)/shard_map/all_to_all | solution.py:200
  850.7 122.5 %collective-permute-start.5 = (bf16[64,2048]{1,0:T(8,128)(2,1)S(1)}, bf16[64,2048]{1,0:T(8,128)(2,1)S(1)}, u32[]{:S(2)}, u32[]{:S(2)}) collective-permute-start(bf16[64,2048]{1,0:T(8,128)(2,1)S(1)} %fusion.93), channel_id=1, source_target_pairs={{32,0},{64,32},{96,64},{128,96},{160,128},{192,160},{224,192},{33,... | collective-permute-start | bytes 786440 | tf_op jit(solution)/shard_map/ppermute | solution.py:12
  977.2 18.8 %all-to-all-start.2 = ((bf16[32,3,2048]{2,1,0:T(4,128)(2,1)}), bf16[32,3,2048]{2,1,0:T(4,128)(2,1)S(1)}, u32[]{:S(2)}, u32[]{:S(2)}) async-start(bf16[32,3,2048]{2,1,0:T(4,128)(2,1)} %reshape.440), calls=%async_computation.2 | async-start | bytes 1048576 | tf_op jit(solution)/shard_map/while/body/eval_jaxpr/all_to_all | solution.py:191
  1030.2 16.5 %all-to-all-start.2 = ((bf16[32,3,2048]{2,1,0:T(4,128)(2,1)}), bf16[32,3,2048]{2,1,0:T(4,128)(2,1)S(1)}, u32[]{:S(2)}, u32[]{:S(2)}) async-start(bf16[32,3,2048]{2,1,0:T(4,128)(2,1)} %reshape.440), calls=%async_computation.2 | async-start | bytes 1048576 | tf_op jit(solution)/shard_map/while/body/eval_jaxpr/all_to_all | solution.py:191
  1080.8 16.5 %all-to-all-start.2 = ((bf16[32,3,2048]{2,1,0:T(4,128)(2,1)}), bf16[32,3,2048]{2,1,0:T(4,128)(2,1)S(1)}, u32[]{:S(2)}, u32[]{:S(2)}) async-start(bf16[32,3,2048]{2,1,0:T(4,128)(2,1)} %reshape.440), calls=%async_computation.2 | async-start | bytes 1048576 | tf_op jit(solution)/shard_map/while/body/eval_jaxpr/all_to_all | solution.py:191
  1131.4 16.5 %all-to-all-start.2 = ((bf16[32,3,2048]{2,1,0:T(4,128)(2,1)}), bf16[32,3,2048]{2,1,0:T(4,128)(2,1)S(1)}, u32[]{:S(2)}, u32[]{:S(2)}) async-start(bf16[32,3,2048]{2,1,0:T(4,128)(2,1)} %reshape.440), calls=%async_computation.2 | async-start | bytes 1048576 | tf_op jit(solution)/shard_map/while/body/eval_jaxpr/all_to_all | solution.py:191
  1183.0 16.2 %all-to-all-start.2 = ((bf16[32,3,2048]{2,1,0:T(4,128)(2,1)}), bf16[32,3,2048]{2,1,0:T(4,128)(2,1)S(1)}, u32[]{:S(2)}, u32[]{:S(2)}) async-start(bf16[32,3,2048]{2,1,0:T(4,128)(2,1)} %reshape.440), calls=%async_computation.2 | async-start | bytes 1048576 | tf_op jit(solution)/shard_map/while/body/eval_jaxpr/all_to_all | solution.py:191
  1234.8 16.2 %all-to-all-start.2 = ((bf16[32,3,2048]{2,1,0:T(4,128)(2,1)}), bf16[32,3,2048]{2,1,0:T(4,128)(2,1)S(1)}, u32[]{:S(2)}, u32[]{:S(2)}) async-start(bf16[32,3,2048]{2,1,0:T(4,128)(2,1)} %reshape.440), calls=%async_computation.2 | async-start | bytes 1048576 | tf_op jit(solution)/shard_map/while/body/eval_jaxpr/all_to_all | solution.py:191
  1286.6 16.2 %all-to-all-start.2 = ((bf16[32,3,2048]{2,1,0:T(4,128)(2,1)}), bf16[32,3,2048]{2,1,0:T(4,128)(2,1)S(1)}, u32[]{:S(2)}, u32[]{:S(2)}) async-start(bf16[32,3,2048]{2,1,0:T(4,128)(2,1)} %reshape.440), calls=%async_computation.2 | async-start | bytes 1048576 | tf_op jit(solution)/shard_map/while/body/eval_jaxpr/all_to_all | solution.py:191
  1338.5 16.2 %all-to-all-start.2 = ((bf16[32,3,2048]{2,1,0:T(4,128)(2,1)}), bf16[32,3,2048]{2,1,0:T(4,128)(2,1)S(1)}, u32[]{:S(2)}, u32[]{:S(2)}) async-start(bf16[32,3,2048]{2,1,0:T(4,128)(2,1)} %reshape.440), calls=%async_computation.2 | async-start | bytes 1048576 | tf_op jit(solution)/shard_map/while/body/eval_jaxpr/all_to_all | solution.py:191
  (146 other events, 2523.5 us)
Sparse Core Ops, SparseCore 0:
  780.1 103.9 reduce-scatter.4
  887.9 83.9 reduce-scatter.2
where the time goes:
time: 1410 us; the launch traced here: 1400 us
  waiting for transfers between devices  483 us (34%)
  starting transfers between devices  251 us (18%)
  matrix products  242 us (17%)
  local copies, waits for them, and re-layouts  181 us (13%)
  blocking collectives  136 us (10%)
  other arithmetic  85.2 us (6%)
  between operations  14.5 us (1%)
    ppermute x34, waiting for transfers between devices, shifted(): lax.ppermute(value, axis, [(source, source + steps) for source in range(f...  159 us
    all_to_all x8, blocking collectives, expert_layer(): lax.all_to_all(outgoing, 'expert', split_axis=0, concat_axis=0, tiled=True)  136 us
    ppermute x34, starting transfers between devices, shifted(): lax.ppermute(value, axis, [(source, source + steps) for source in range(f...  106 us
    reduce_scatter x1, waiting for transfers between devices, local(): lax.psum_scatter(sum_in.astype(jnp.bfloat16), 'expert', scatter_dimension...  86.4 us
    all_to_all x9, waiting for transfers between devices, expert_layer(): lax.all_to_all(served.reshape(received.shape), 'expert', split_axis=0, co...  84.1 us
    all_to_all x9, waiting for transfers between devices, expert_layer_back(): lax.all_to_all(grad_buffer, 'expert', split_axis=0, concat_axis=0, tiled=...  65.1 us
    all_to_all x9, starting transfers between devices, expert_layer_back(): lax.all_to_all(grad_buffer, 'expert', split_axis=0, concat_axis=0, tiled=...  60.6 us
    dynamic_slice x43, local copies, waits for them, and re-layouts, pick_micro(): return lax.dynamic_index_in_dim(stored, micro_id, 0, keepdims=False)  59.6 us
  transfers between devices with their start and end apart: 64, of which 59 were waited for; matrix products, arithmetic and copies ran while one was open for 15% of the time, Pallas kernels for 0%

commit v1 on v0

v1 whole, which is shorter than its diff:
```python
import jax
import jax.numpy as jnp
from jax import lax
from jax.sharding import PartitionSpec as P

epsilon = 1e-06
capacity = 3


def dot(left, right):
    return jnp.dot(left, right, preferred_element_type=jnp.float32)


def dot_t(left, right):
    return lax.dot_general(left, right, (((1,), (1,)), ((), ())), preferred_element_type=jnp.float32)


def dot_tn(left, right):
    return lax.dot_general(left, right, (((0,), (0,)), ((), ())), preferred_element_type=jnp.float32)


def rms_scale(values):
    widened = values.astype(jnp.float32)
    return lax.rsqrt(jnp.mean(widened * widened, axis=-1, keepdims=True) + epsilon)


def norm_back(values, row_scale, grad_norm):
    widened = values.astype(jnp.float32)
    inner_mean = jnp.mean(grad_norm * widened, axis=-1, keepdims=True)
    return row_scale * grad_norm - widened * (row_scale * row_scale * row_scale) * inner_mean


def lowrank_parts(values, matrix_in):
    row_scale = rms_scale(values)
    normed = (values.astype(jnp.float32) * row_scale).astype(jnp.bfloat16)
    inner_pre = dot(normed, matrix_in)
    inner_sig = jax.nn.sigmoid(inner_pre)
    inner_act = (inner_pre * inner_sig).astype(jnp.bfloat16)
    return (row_scale, normed, inner_pre, inner_sig, inner_act)


def lowrank_forward(values, matrix_in, matrix_out):
    inner_act = lowrank_parts(values, matrix_in)[4]
    return (values.astype(jnp.float32) + dot(inner_act, matrix_out)).astype(jnp.bfloat16)


def lowrank_backward(values, grad_rows, matrix_in, matrix_out):
    row_scale, normed, inner_pre, inner_sig, inner_act = lowrank_parts(values, matrix_in)
    grad_act = dot_t(grad_rows, matrix_out)
    grad_pre = (grad_act * (inner_sig * (1.0 + inner_pre * (1.0 - inner_sig)))).astype(jnp.bfloat16)
    grad_norm = dot_t(grad_pre, matrix_in)
    grad_input = (grad_rows.astype(jnp.float32) + norm_back(values, row_scale, grad_norm)).astype(
        jnp.bfloat16
    )
    return (grad_input, dot_tn(normed, grad_pre), dot_tn(inner_act, grad_rows))


def head_grad(values, targets, head_weight):
    row_scale = rms_scale(values)
    logits = row_scale[:, 0] * jnp.sum(values.astype(jnp.float32) * head_weight[None, :], axis=1)
    grad_logit = jax.nn.sigmoid(logits) - targets.astype(jnp.float32)
    return norm_back(values, row_scale, grad_logit[:, None] * head_weight[None, :]).astype(
        jnp.bfloat16
    )


def slot_of_rows(expert_ids, expert_count, stride, offset):
    chosen = (expert_ids[:, None] == jnp.arange(expert_count, dtype=jnp.int32)[None, :]).astype(
        jnp.int32
    )
    earlier = jnp.arange(expert_ids.shape[0])[:, None] > jnp.arange(expert_ids.shape[0])[None, :]
    same = expert_ids[:, None] == expert_ids[None, :]
    rank = jnp.sum((same & earlier).astype(jnp.int32), axis=1)
    return expert_ids * stride + offset + rank


def table_of(slots, slot_count):
    grid = jnp.arange(slot_count, dtype=jnp.int32)
    return (grid[:, None] == slots[None, :]).astype(jnp.bfloat16)


def exchange(buffer, expert_count):
    shaped = buffer.reshape(expert_count, -1, buffer.shape[1])
    moved = lax.all_to_all(shaped, "expert", split_axis=0, concat_axis=0, tiled=True)
    return moved.reshape(buffer.shape)


def expert_forward(values, table, gate_row, mats):
    gate_mat, up_mat, down_mat = mats
    expert_count = lax.axis_size("expert")
    row_scale = rms_scale(values)
    normed = (values.astype(jnp.float32) * row_scale).astype(jnp.bfloat16)
    kept = exchange(dot(table, normed).astype(jnp.bfloat16), expert_count)
    gate_pre = dot(kept, gate_mat)
    up_pre = dot(kept, up_mat)
    hidden = (gate_pre * jax.nn.sigmoid(gate_pre) * up_pre).astype(jnp.bfloat16)
    served = dot(hidden, down_mat).astype(jnp.bfloat16)
    returned = exchange(served, expert_count)
    layer_out = values.astype(jnp.float32) + gate_row[:, None] * dot_tn(table, returned)
    return (layer_out.astype(jnp.bfloat16), kept)


def expert_backward(values, grad_rows, table, gate_row, kept, mats):
    gate_mat, up_mat, down_mat = mats
    expert_count = lax.axis_size("expert")
    grad_out = (gate_row[:, None] * grad_rows.astype(jnp.float32)).astype(jnp.bfloat16)
    slot_grads = exchange(dot(table, grad_out).astype(jnp.bfloat16), expert_count)
    gate_pre = dot(kept, gate_mat)
    up_pre = dot(kept, up_mat)
    gate_sig = jax.nn.sigmoid(gate_pre)
    gate_act = gate_pre * gate_sig
    hidden = (gate_act * up_pre).astype(jnp.bfloat16)
    grad_hidden = dot_t(slot_grads, down_mat)
    grad_gate = (grad_hidden * up_pre * (gate_sig * (1.0 + gate_pre * (1.0 - gate_sig)))).astype(
        jnp.bfloat16
    )
    grad_up = (grad_hidden * gate_act).astype(jnp.bfloat16)
    grad_slots = (dot_t(grad_gate, gate_mat) + dot_t(grad_up, up_mat)).astype(jnp.bfloat16)
    returned = exchange(grad_slots, expert_count)
    grad_norm = dot_tn(table, returned)
    row_scale = rms_scale(values)
    grad_input = (grad_rows.astype(jnp.float32) + norm_back(values, row_scale, grad_norm)).astype(
        jnp.bfloat16
    )
    wide = jnp.concatenate([kept, slot_grads], axis=1)
    narrow = jnp.concatenate([hidden, grad_gate, grad_up], axis=1)
    return (grad_input, (wide, narrow))


def local(
    features,
    labels,
    routes,
    route_gates,
    gate_weight,
    up_weight,
    down_weight,
    lowrank_in,
    lowrank_out,
    head_weight,
):
    section_count = lax.axis_size("section")
    section = lax.axis_index("section")
    expert_count = lax.axis_size("expert")
    micro_count, row_count, width = features.shape
    inner = gate_weight.shape[3]
    parity = section % 2
    is_even = parity == 0
    pair = section // 2
    partners = [(s, s ^ 1) for s in range(section_count)]

    def swap(value):
        return lax.ppermute(value, "section", partners)

    def ring(value, steps):
        return lax.ppermute(
            value, "section", [(s, (s + steps) % section_count) for s in range(section_count)]
        )

    own = (gate_weight[0, 0], up_weight[0, 0], down_weight[0, 0])
    other = tuple(swap(mat) for mat in own)
    mats_even = tuple(jnp.where(is_even, a, b) for a, b in zip(own, other))
    mats_odd = tuple(jnp.where(is_even, b, a) for a, b in zip(own, other))

    ids = routes[0, :, :, 0]
    plan = jnp.concatenate([ids.astype(jnp.float32), route_gates[0]], axis=0)
    plan_other = swap(plan)

    def pick(first, second):
        chosen = jnp.where(is_even, first, second)
        mine = jnp.where(is_even, chosen[0::2], chosen[1::2])
        slots = slot_of_rows(mine[0].astype(jnp.int32), expert_count, capacity, 0)
        return (table_of(slots, expert_count * capacity), mine[1])

    table_even, gate_even = pick(plan, plan_other)
    table_odd, gate_odd = pick(plan_other, plan)
    joint_slots = jnp.concatenate(
        [
            slot_of_rows(ids[m], expert_count, capacity * micro_count, capacity * m)
            for m in range(micro_count)
        ]
    )
    table_all = table_of(joint_slots, expert_count * capacity * micro_count)
    gate_all = route_gates[0].reshape(-1)

    first_rows = features.reshape(-1, width)
    second_rows, kept_all = expert_forward(first_rows, table_all, gate_all, own)
    crossing = swap(second_rows[row_count:])
    rows = jnp.where(is_even, second_rows[:row_count], crossing)

    layer_rows = {}
    layer_kept = {}
    for layer in range(1, section_count):
        odd = layer % 2 == 1
        layer_rows[layer] = rows
        rows, layer_kept[layer] = expert_forward(
            rows,
            table_odd if odd else table_even,
            gate_odd if odd else gate_even,
            mats_odd if odd else mats_even,
        )
        if layer == 2:
            low_in, low_out, rows = lax.optimization_barrier((lowrank_in[0], lowrank_out[0], rows))
            all_in = lax.all_gather(low_in, "section")
            all_out = lax.all_gather(low_out, "section")
        if odd and layer < section_count - 1:
            rows = ring(rows, 2)

    low_rows = {}
    for index in reversed(range(section_count)):
        low_rows[index] = rows
        rows = lowrank_forward(rows, all_in[index], all_out[index])
    grads = head_grad(rows, jnp.where(is_even, labels[0], labels[1]), head_weight)
    parts_in = []
    parts_out = []
    for index in range(section_count):
        grads, part_in, part_out = lowrank_backward(
            low_rows[index], grads, all_in[index], all_out[index]
        )
        parts_in.append(part_in.astype(jnp.bfloat16))
        parts_out.append(part_out.astype(jnp.bfloat16))
    valid = pair == section_count // 2 - 1

    def spread_sum(parts, dimension):
        stacked = jnp.stack(parts)
        stacked = jnp.where(valid, stacked, jnp.zeros_like(stacked))
        mine = lax.psum_scatter(stacked, "section", scatter_dimension=0, tiled=False)
        return lax.psum_scatter(mine, "expert", scatter_dimension=dimension, tiled=True).astype(
            jnp.float32
        )

    share_in = spread_sum(parts_in, 0)
    share_out = spread_sum(parts_out, 1)

    saved = {0: None, 1: None}
    for layer in reversed(range(1, section_count)):
        odd = layer % 2 == 1
        grads, record = expert_backward(
            layer_rows[layer],
            grads,
            table_odd if odd else table_even,
            gate_odd if odd else gate_even,
            layer_kept[layer],
            mats_odd if odd else mats_even,
        )
        here = pair == layer // 2
        past = saved[layer % 2]
        saved[layer % 2] = (
            record
            if past is None
            else tuple(jnp.where(here, new, old) for new, old in zip(record, past))
        )
        if not odd:
            grads = ring(grads, -2)

    crossing = swap(grads)
    all_grads = jnp.concatenate([grads, crossing], axis=0)
    sent = tuple(swap(jnp.where(is_even, b, a)) for a, b in zip(saved[0], saved[1]))
    held = tuple(jnp.where(is_even, a, b) for a, b in zip(saved[0], saved[1]))
    _, record = expert_backward(first_rows, all_grads, table_all, gate_all, kept_all, own)
    final_wide, final_narrow = (
        jnp.where(section == 0, joint, jnp.concatenate([mine, theirs], axis=0))
        for joint, mine, theirs in zip(record, held, sent)
    )
    kept, slot_grads = (final_wide[:, :width], final_wide[:, width:])
    hidden, grad_gate, grad_up = (final_narrow[:, inner * k : inner * (k + 1)] for k in range(3))
    return (
        dot_tn(kept, grad_gate)[None, None],
        dot_tn(kept, grad_up)[None, None],
        dot_tn(hidden, slot_grads)[None, None],
        share_in[None],
        share_out[None],
    )


def solution(mesh):
    return jax.shard_map(
        local,
        mesh=mesh,
        in_specs=(
            P(None, "expert", None),
            P(None, "expert"),
            P("section", None, "expert", None),
            P("section", None, "expert"),
            P("section", "expert", None, None),
            P("section", "expert", None, None),
            P("section", "expert", None, None),
            P("section", None, None),
            P("section", None, None),
            P(),
        ),
        out_specs=(
            P("section", "expert", None, None),
            P("section", "expert", None, None),
            P("section", "expert", None, None),
            P("section", "expert", None),
            P("section", None, "expert"),
        ),
        check_vma=False,
    )
```

time: 1410 us -> 1140 us (0.81)
  starting transfers between devices: 251 us -> 118 us
  blocking collectives: 136 us -> 238 us
  waiting for transfers between devices: 483 us -> 392 us
  matrix products: 242 us -> 173 us
  local copies, waits for them, and re-layouts: 181 us -> 139 us
  other arithmetic: 85.2 us -> 45.4 us
    all_to_all x8 -> x14, blocking collectives: 136 us -> 238 us  [exchange(): lax.all_to_all(shaped, 'expert', split_axis=0, concat_axis=0, tiled=True)]
    ppermute x34 -> x14, waiting for transfers between devices: 159 us -> 81.2 us  [the longest x6 53.2 us: ring(): lax.ppermute(value, 'section', [(s, (s + steps) % section_count) for s in...]
    ppermute x34 -> x14, starting transfers between devices: 106 us -> 29.6 us  [the longest x6 17.7 us: ring(): lax.ppermute(value, 'section', [(s, (s + steps) % section_count) for s in...]
    dot_general x180 -> x128, matrix products: 242 us -> 173 us  [the longest x56 77.1 us: dot(): return jnp.dot(left, right, preferred_element_type=jnp.float32)]
    unnamed x2 -> x7, waiting for transfers between devices: 0.03 us -> 60.4 us
    dynamic_slice x43 -> x0, local copies, waits for them, and re-layouts: 59.6 us -> none  [pick_micro(): return lax.dynamic_index_in_dim(stored, micro_id, 0, keepdims=False)]
    all_to_all x28 -> x17, starting transfers between devices: 145 us -> 87.8 us  [exchange(): lax.all_to_all(shaped, 'expert', split_axis=0, concat_axis=0, tiled=True)]
    all_to_all x28 -> x17, waiting for transfers between devices: 207 us -> 164 us  [exchange(): lax.all_to_all(shaped, 'expert', split_axis=0, concat_axis=0, tiled=True)]
  transfers between devices with their start and end apart: 64 -> 37, of which waited for: 59 -> 27; matrix products, arithmetic and copies ran while one was open for 15% -> 22% of each run, Pallas kernels for 0% -> 0%
where the time goes in v1:
time: 1140 us; the launch traced here: 1120 us
  waiting for transfers between devices  392 us (34%)
  blocking collectives  238 us (21%)
  matrix products  173 us (15%)
  local copies, waits for them, and re-layouts  139 us (12%)
  starting transfers between devices  118 us (10%)
  other arithmetic  45.4 us (4%)
  between operations  17 us (1%)
    all_to_all x14, blocking collectives, exchange(): lax.all_to_all(shaped, 'expert', split_axis=0, concat_axis=0, tiled=True)  238 us
    all_to_all x17, waiting for transfers between devices, exchange(): lax.all_to_all(shaped, 'expert', split_axis=0, concat_axis=0, tiled=True)  164 us
    all_to_all x17, starting transfers between devices, exchange(): lax.all_to_all(shaped, 'expert', split_axis=0, concat_axis=0, tiled=True)  87.8 us
    reduce_scatter x1, waiting for transfers between devices, spread_sum(): lax.psum_scatter(mine, 'expert', scatter_dimension=dimension, tiled=True)  86.1 us
    dot_general x56, matrix products, dot(): return jnp.dot(left, right, preferred_element_type=jnp.float32)  77.1 us
    dot_general x34, matrix products, dot_tn(): lax.dot_general(left, right, (((0,), (0,)), ((), ())), preferred_element_...  61.8 us
    unnamed x7, waiting for transfers between devices  60.4 us
    reshape x31, local copies, waits for them, and re-layouts, exchange(): shaped = buffer.reshape(expert_count, -1, buffer.shape[1])  58.7 us
  transfers between devices with their start and end apart: 37, of which 27 were waited for; matrix products, arithmetic and copies ran while one was open for 22% of the time, Pallas kernels for 0%

profile of v1, /device:TPU:1, one launch (start us, length us, event | category | flops | bytes accessed | tf_op | source)
XLA Modules:
  0.0 1122.2 jit_solution(9454358501053625495)
XLA Ops:
  27.0 15.1 %all-to-all-done = bf16[32,6,2048]{2,1,0:T(8,128)(2,1)S(1)} async-done(((bf16[32,6,2048]{2,1,0:T(8,128)(2,1)}), bf16[32,6,2048]{2,1,0:T(8,128)(2,1)S(1)}, u32[]{:S(2)}, u32[]{:S(2)}) %all-to-all-start) | async-done | bytes 786464 | tf_op jit(solution)/shard_map/all_to_all | solution.py:84
  55.5 14.7 %all-to-all-done.1 = bf16[32,6,2048]{2,1,0:T(8,128)(2,1)} async-done(((bf16[32,6,2048]{2,1,0:T(8,128)(2,1)}), bf16[32,6,2048]{2,1,0:T(8,128)(2,1)}, u32[]{:S(2)}, u32[]{:S(2)}) %all-to-all-start.1) | async-done | bytes 786464 | tf_op jit(solution)/shard_map/all_to_all | solution.py:84
  76.5 23.7 %collective-permute-done = bf16[64,2048]{1,0:T(8,128)(2,1)S(1)} collective-permute-done((bf16[64,2048]{1,0:T(8,128)(2,1)S(1)}, bf16[64,2048]{1,0:T(8,128)(2,1)S(1)}, u32[]{:S(2)}, u32[]{:S(2)}) %collective-permute-start) | collective-permute-done | bytes 262176 | tf_op jit(solution)/shard_map/ppermute | solution.py:153
  138.3 11.6 %all-to-all-done.3 = bf16[32,3,2048]{2,1,0:T(4,128)(2,1)} async-done(((bf16[32,3,2048]{2,1,0:T(4,128)(2,1)}), bf16[32,3,2048]{2,1,0:T(4,128)(2,1)}, u32[]{:S(2)}, u32[]{:S(2)}) %all-to-all-start.3) | async-done | bytes 393248 | tf_op jit(solution)/shard_map/all_to_all | solution.py:84
  169.4 17.3 %all_to_all.155 = bf16[32,3,2048]{2,1,0:T(4,128)(2,1)} all-to-all(bf16[32,3,2048]{2,1,0:T(4,128)(2,1)} %reshape.565), channel_id=1, replica_groups=mesh['section'=8,'expert'=32] {'expert'}, dimensions={0} | all-to-all | bytes 786432 | tf_op jit(solution)/shard_map/all_to_all | solution.py:84
  197.6 16.3 %all_to_all.156 = bf16[32,3,2048]{2,1,0:T(4,128)(2,1)} all-to-all(bf16[32,3,2048]{2,1,0:T(4,128)(2,1)} %reshape.567), channel_id=1, replica_groups=mesh['section'=8,'expert'=32] {'expert'}, dimensions={0} | all-to-all | bytes 786432 | tf_op jit(solution)/shard_map/all_to_all | solution.py:84
  221.2 16.3 %all_to_all.157 = bf16[32,3,2048]{2,1,0:T(4,128)(2,1)} all-to-all(bf16[32,3,2048]{2,1,0:T(4,128)(2,1)} %reshape.569), channel_id=1, replica_groups=mesh['section'=8,'expert'=32] {'expert'}, dimensions={0} | all-to-all | bytes 786432 | tf_op jit(solution)/shard_map/all_to_all | solution.py:84
  246.6 16.3 %all_to_all.158 = bf16[32,3,2048]{2,1,0:T(4,128)(2,1)} all-to-all(bf16[32,3,2048]{2,1,0:T(4,128)(2,1)} %reshape.571), channel_id=1, replica_groups=mesh['section'=8,'expert'=32] {'expert'}, dimensions={0} | all-to-all | bytes 786432 | tf_op jit(solution)/shard_map/all_to_all | solution.py:84
  281.8 21.5 %all_to_all.159 = bf16[32,3,2048]{2,1,0:T(4,128)(2,1)} all-to-all(bf16[32,3,2048]{2,1,0:T(4,128)(2,1)} %reshape.573), channel_id=1, replica_groups=mesh['section'=8,'expert'=32] {'expert'}, dimensions={0} | all-to-all | bytes 786432 | tf_op jit(solution)/shard_map/all_to_all | solution.py:84
  338.6 16.3 %all_to_all.160 = bf16[32,3,2048]{2,1,0:T(4,128)(2,1)} all-to-all(bf16[32,3,2048]{2,1,0:T(4,128)(2,1)} %reshape.577), channel_id=1, replica_groups=mesh['section'=8,'expert'=32] {'expert'}, dimensions={0} | all-to-all | bytes 786432 | tf_op jit(solution)/shard_map/all_to_all | solution.py:84
  364.6 16.3 %all_to_all.161 = bf16[32,3,2048]{2,1,0:T(4,128)(2,1)} all-to-all(bf16[32,3,2048]{2,1,0:T(4,128)(2,1)} %reshape.579), channel_id=1, replica_groups=mesh['section'=8,'expert'=32] {'expert'}, dimensions={0} | all-to-all | bytes 786432 | tf_op jit(solution)/shard_map/all_to_all | solution.py:84
  398.0 18.0 %all_to_all.162 = bf16[32,3,2048]{2,1,0:T(4,128)(2,1)} all-to-all(bf16[32,3,2048]{2,1,0:T(4,128)(2,1)} %reshape.581), channel_id=1, replica_groups=mesh['section'=8,'expert'=32] {'expert'}, dimensions={0} | all-to-all | bytes 786432 | tf_op jit(solution)/shard_map/all_to_all | solution.py:84
  427.5 16.3 %all_to_all.163 = bf16[32,3,2048]{2,1,0:T(4,128)(2,1)} all-to-all(bf16[32,3,2048]{2,1,0:T(4,128)(2,1)} %reshape.583), channel_id=1, replica_groups=mesh['section'=8,'expert'=32] {'expert'}, dimensions={0} | all-to-all | bytes 786432 | tf_op jit(solution)/shard_map/all_to_all | solution.py:84
  451.4 16.4 %all_to_all.164 = bf16[32,3,2048]{2,1,0:T(4,128)(2,1)} all-to-all(bf16[32,3,2048]{2,1,0:T(4,128)(2,1)} %reshape.585), channel_id=1, replica_groups=mesh['section'=8,'expert'=32] {'expert'}, dimensions={0} | all-to-all | bytes 786432 | tf_op jit(solution)/shard_map/all_to_all | solution.py:84
  482.5 11.5 %all-to-all-done.15 = bf16[32,3,2048]{2,1,0:T(4,128)(2,1)} async-done(((bf16[32,3,2048]{2,1,0:T(4,128)(2,1)}), bf16[32,3,2048]{2,1,0:T(4,128)(2,1)}, u32[]{:S(2)}, u32[]{:S(2)}) %all-to-all-start.15) | async-done | bytes 393248 | tf_op jit(solution)/shard_map/all_to_all | solution.py:84
  637.4 13.9 %collective-permute-done.8 = bf16[64,2048]{1,0:T(8,128)(2,1)} collective-permute-done((bf16[64,2048]{1,0:T(8,128)(2,1)}, bf16[64,2048]{1,0:T(8,128)(2,1)}, u32[]{:S(2)}, u32[]{:S(2)}) %collective-permute-start.8) | collective-permute-done | bytes 262176 | tf_op jit(solution)/shard_map/ppermute | solution.py:156
  655.4 16.9 %all_to_all.165 = bf16[32,3,2048]{2,1,0:T(4,128)(2,1)} all-to-all(bf16[32,3,2048]{2,1,0:T(4,128)(2,1)} %reshape.597), channel_id=1, replica_groups=mesh['section'=8,'expert'=32] {'expert'}, dimensions={0} | all-to-all | bytes 786432 | tf_op jit(solution)/shard_map/all_to_all | solution.py:84
  680.2 16.5 %all_to_all.166 = bf16[32,3,2048]{2,1,0:T(4,128)(2,1)} all-to-all(bf16[32,3,2048]{2,1,0:T(4,128)(2,1)} %reshape.599), channel_id=1, replica_groups=mesh['section'=8,'expert'=32] {'expert'}, dimensions={0} | all-to-all | bytes 786432 | tf_op jit(solution)/shard_map/all_to_all | solution.py:84
  818.1 16.6 %all_to_all.167 = bf16[32,3,2048]{2,1,0:T(4,128)(2,1)} all-to-all(bf16[32,3,2048]{2,1,0:T(4,128)(2,1)} %reshape.609), channel_id=1, replica_groups=mesh['section'=8,'expert'=32] {'expert'}, dimensions={0} | all-to-all | bytes 786432 | tf_op jit(solution)/shard_map/all_to_all | solution.py:84
  844.2 16.4 %all_to_all.168 = bf16[32,3,2048]{2,1,0:T(4,128)(2,1)} all-to-all(bf16[32,3,2048]{2,1,0:T(4,128)(2,1)} %reshape.611), channel_id=1, replica_groups=mesh['section'=8,'expert'=32] {'expert'}, dimensions={0} | all-to-all | bytes 786432 | tf_op jit(solution)/shard_map/all_to_all | solution.py:84
  882.5 11.7 %all-to-all-done.28 = bf16[32,3,2048]{2,1,0:T(4,128)(2,1)} async-done(((bf16[32,3,2048]{2,1,0:T(4,128)(2,1)}), bf16[32,3,2048]{2,1,0:T(4,128)(2,1)}, u32[]{:S(2)}, u32[]{:S(2)}) %all-to-all-start.28) | async-done | bytes 393248 | tf_op jit(solution)/shard_map/all_to_all | solution.py:84
  944.5 11.1 all-to-all-done.30
  966.2 59.8 %reduce-scatter.13.cloned.1.call-done = bf16[64,128]{1,0:T(8,128)(2,1)} async-done(((bf16[2048,128]{1,0:T(8,128)(2,1)}), bf16[64,128]{1,0:T(8,128)(2,1)}) %reduce-scatter.13.cloned.1.call-update) | async-done | bytes 16400
  1027.5 86.1 %reduce-scatter.9.cloned.1.call-done = bf16[64,128]{1,0:T(8,128)(2,1)} async-done(((bf16[2048,128]{1,0:T(8,128)(2,1)}), bf16[64,128]{1,0:T(8,128)(2,1)}) %reduce-scatter.9.cloned.1.call-update) | async-done | bytes 16400 | tf_op jit(solution)/shard_map/reduce_scatter | solution.py:228
  (648 shorter events, 608.6 us)
Async XLA Ops:
  8.6 18.0 %collective-permute-start.1 = (f32[4,64]{1,0:T(4,128)S(1)}, f32[4,64]{1,0:T(4,128)S(1)}, u32[]{:S(2)}, u32[]{:S(2)}) collective-permute-start(f32[4,64]{1,0:T(4,128)S(1)} %pad_maximum_fusion), channel_id=1, source_target_pairs={{0,32},{32,0},{64,96},{96,64},{128,160},{160,128},{192,224},{224,1... | collective-permute-start | bytes 3080 | tf_op jit(solution)/shard_map/ppermute | solution.py:153
  16.9 25.2 %all-to-all-start = ((bf16[32,6,2048]{2,1,0:T(8,128)(2,1)}), bf16[32,6,2048]{2,1,0:T(8,128)(2,1)S(1)}, u32[]{:S(2)}, u32[]{:S(2)}) async-start(bf16[32,6,2048]{2,1,0:T(8,128)(2,1)} %reshape.557), calls=%async_computation | async-start | bytes 2097152 | tf_op jit(solution)/shard_map/all_to_all | solution.py:84
  24.9 27.9 %collective-permute-start.4 = (bf16[256,2048]{1,0:T(8,128)(2,1)}, bf16[256,2048]{1,0:T(8,128)(2,1)}, u32[]{:S(2)}, u32[]{:S(2)}) collective-permute-start(bf16[256,2048]{1,0:T(8,128)(2,1)} %bitcast.7), channel_id=1, source_target_pairs={{0,32},{32,0},{64,96},{96,64},{128,160},{160,128},{192,224},{224,1... | collective-permute-start | bytes 3145736 | tf_op jit(solution)/shard_map/ppermute | solution.py:153
  25.0 48.9 %collective-permute-start.3 = (bf16[2048,256]{1,0:T(8,128)(2,1)}, bf16[2048,256]{1,0:T(8,128)(2,1)}, u32[]{:S(2)}, u32[]{:S(2)}) collective-permute-start(bf16[2048,256]{1,0:T(8,128)(2,1)} %bitcast.279), channel_id=1, source_target_pairs={{0,32},{32,0},{64,96},{96,64},{128,160},{160,128},{192,224},{224,1... | collective-permute-start | bytes 3145736 | tf_op jit(solution)/shard_map/ppermute | solution.py:153
  26.5 85.9 %collective-permute-start.2 = (bf16[2048,256]{1,0:T(8,128)(2,1)S(1)}, bf16[2048,256]{1,0:T(8,128)(2,1)}, u32[]{:S(2)}, u32[]{:S(2)}) collective-permute-start(bf16[2048,256]{1,0:T(8,128)(2,1)S(1)} %bitcast.277), channel_id=1, source_target_pairs={{0,32},{32,0},{64,96},{96,64},{128,160},{160,128},{192,224},{224,1... | collective-permute-start | bytes 3145736 | tf_op jit(solution)/shard_map/ppermute | solution.py:153
  48.0 22.1 %all-to-all-start.1 = ((bf16[32,6,2048]{2,1,0:T(8,128)(2,1)}), bf16[32,6,2048]{2,1,0:T(8,128)(2,1)}, u32[]{:S(2)}, u32[]{:S(2)}) async-start(bf16[32,6,2048]{2,1,0:T(8,128)(2,1)} %reshape.559), calls=%async_computation.1 | async-start | bytes 2097152 | tf_op jit(solution)/shard_map/all_to_all | solution.py:84
  73.8 26.5 %collective-permute-start = (bf16[64,2048]{1,0:T(8,128)(2,1)S(1)}, bf16[64,2048]{1,0:T(8,128)(2,1)S(1)}, u32[]{:S(2)}, u32[]{:S(2)}) collective-permute-start(bf16[64,2048]{1,0:T(8,128)(2,1)S(1)} %slice.175), channel_id=1, source_target_pairs={{0,32},{32,0},{64,96},{96,64},{128,160},{160,128},{192,224},{224,1... | collective-permute-start | bytes 786440 | tf_op jit(solution)/shard_map/ppermute | solution.py:153
  104.2 19.7 %all-to-all-start.2 = ((bf16[32,3,2048]{2,1,0:T(4,128)(2,1)}), bf16[32,3,2048]{2,1,0:T(4,128)(2,1)}, u32[]{:S(2)}, u32[]{:S(2)}) async-start(bf16[32,3,2048]{2,1,0:T(4,128)(2,1)} %reshape.561), calls=%async_computation.2 | async-start | bytes 1048576 | tf_op jit(solution)/shard_map/all_to_all | solution.py:84
  138.2 360.7 %all-gather.5.cloned.1.call-start = ((), (), s32[]{:S(2)}) async-start(), calls=%async_computation.38 | async-start | bytes 4718592 | tf_op jit(solution)/shard_map/all_gather | solution.py:204
  319.5 180.9 %all-gather.7.cloned.1.call-start = ((), (), s32[]{:S(2)}) async-start(), calls=%async_computation.39 | async-start | bytes 4718592 | tf_op jit(solution)/shard_map/all_gather | solution.py:205
  477.4 16.6 %all-to-all-start.15 = ((bf16[32,3,2048]{2,1,0:T(4,128)(2,1)}), bf16[32,3,2048]{2,1,0:T(4,128)(2,1)}, u32[]{:S(2)}, u32[]{:S(2)}) async-start(bf16[32,3,2048]{2,1,0:T(4,128)(2,1)} %reshape.587), calls=%async_computation.15 | async-start | bytes 1048576 | tf_op jit(solution)/shard_map/all_to_all | solution.py:84
  559.1 16.8 %all-to-all-start.17 = ((bf16[32,3,2048]{2,1,0:T(4,128)(2,1)}), bf16[32,3,2048]{2,1,0:T(4,128)(2,1)}, u32[]{:S(2)}, u32[]{:S(2)}) async-start(bf16[32,3,2048]{2,1,0:T(4,128)(2,1)} %reshape.591), calls=%async_computation.17 | async-start | bytes 1048576 | tf_op jit(solution)/shard_map/all_to_all | solution.py:84
  615.1 324.6 %reduce-scatter.11.cloned.1.call-start = ((), (), s32[]{:S(2)}) async-start(), calls=%async_computation.37 | async-start | bytes 4718592 | tf_op jit(solution)/shard_map/reduce_scatter | solution.py:227
  632.3 18.9 %collective-permute-start.8 = (bf16[64,2048]{1,0:T(8,128)(2,1)}, bf16[64,2048]{1,0:T(8,128)(2,1)}, u32[]{:S(2)}, u32[]{:S(2)}) collective-permute-start(bf16[64,2048]{1,0:T(8,128)(2,1)} %fusion.89), channel_id=1, source_target_pairs={{0,192},{32,224},{64,0},{96,32},{128,64},{160,96},{192,128},{224,1... | collective-permute-start | bytes 786440 | tf_op jit(solution)/shard_map/ppermute | solution.py:156
  705.4 16.5 %all-to-all-start.22 = ((bf16[32,3,2048]{2,1,0:T(4,128)(2,1)}), bf16[32,3,2048]{2,1,0:T(4,128)(2,1)}, u32[]{:S(2)}, u32[]{:S(2)}) async-start(bf16[32,3,2048]{2,1,0:T(4,128)(2,1)} %reshape.601), calls=%async_computation.22 | async-start | bytes 1048576 | tf_op jit(solution)/shard_map/all_to_all | solution.py:84
  770.7 16.4 %all-to-all-start.24 = ((bf16[32,3,2048]{2,1,0:T(4,128)(2,1)}), bf16[32,3,2048]{2,1,0:T(4,128)(2,1)}, u32[]{:S(2)}, u32[]{:S(2)}) async-start(bf16[32,3,2048]{2,1,0:T(4,128)(2,1)} %reshape.605), calls=%async_computation.24 | async-start | bytes 1048576 | tf_op jit(solution)/shard_map/all_to_all | solution.py:84
  795.0 16.4 %all-to-all-start.25 = ((bf16[32,3,2048]{2,1,0:T(4,128)(2,1)}), bf16[32,3,2048]{2,1,0:T(4,128)(2,1)}, u32[]{:S(2)}, u32[]{:S(2)}) async-start(bf16[32,3,2048]{2,1,0:T(4,128)(2,1)} %reshape.607), calls=%async_computation.25 | async-start | bytes 1048576 | tf_op jit(solution)/shard_map/all_to_all | solution.py:84
  799.7 161.0 %reduce-scatter.7.cloned.1.call-start = ((), (), s32[]{:S(2)}) async-start(), calls=%async_computation.35 | async-start | bytes 4718592 | tf_op jit(solution)/shard_map/reduce_scatter | solution.py:227
  877.0 17.3 %all-to-all-start.28 = ((bf16[32,3,2048]{2,1,0:T(4,128)(2,1)}), bf16[32,3,2048]{2,1,0:T(4,128)(2,1)}, u32[]{:S(2)}, u32[]{:S(2)}) async-start(bf16[32,3,2048]{2,1,0:T(4,128)(2,1)} %reshape.613), calls=%async_computation.28 | async-start | bytes 1048576 | tf_op jit(solution)/shard_map/all_to_all | solution.py:84
  927.3 29.4 %collective-permute-start.12 = (bf16[96,4096]{1,0:T(8,128)(2,1)}, bf16[96,4096]{1,0:T(8,128)(2,1)}, u32[]{:S(2)}, u32[]{:S(2)}) collective-permute-start(bf16[96,4096]{1,0:T(8,128)(2,1)} %broadcast_select_fusion.8), channel_id=1, source_target_pairs={{0,32},{32,0},{64,96},{96,64},{128,160},{160,128},{192,224},{224,1... | collective-permute-start | bytes 2359304 | tf_op jit(solution)/shard_map/ppermute | solution.py:153
  933.2 22.4 %all-to-all-start.30 = ((bf16[32,6,2048]{2,1,0:T(8,128)(2,1)}), bf16[32,6,2048]{2,1,0:T(8,128)(2,1)S(1)}, u32[]{:S(2)}, u32[]{:S(2)}) async-start(bf16[32,6,2048]{2,1,0:T(8,128)(2,1)} %reshape.617), calls=%async_computation.30 | async-start | bytes 2097152 | tf_op jit(solution)/shard_map/all_to_all | solution.py:84
  938.3 87.7 %reduce-scatter.13.cloned.1.call-start = ((), (), s32[]{:S(2)}) async-start(), calls=%async_computation.40 | async-start | bytes 540672
  941.8 171.8 %reduce-scatter.9.cloned.1.call-start = ((), (), s32[]{:S(2)}) async-start(), calls=%async_computation.36 | async-start | bytes 540672 | tf_op jit(solution)/shard_map/reduce_scatter | solution.py:228
  942.5 18.2 %collective-permute-start.13 = (bf16[96,768]{1,0:T(8,128)(2,1)}, bf16[96,768]{1,0:T(8,128)(2,1)S(1)}, u32[]{:S(2)}, u32[]{:S(2)}) collective-permute-start(bf16[96,768]{1,0:T(8,128)(2,1)} %broadcast_select_fusion.10), channel_id=1, source_target_pairs={{0,32},{32,0},{64,96},{96,64},{128,160},{160,128},{192,224},{224,1... | collective-permute-start | bytes 442376 | tf_op jit(solution)/shard_map/ppermute | solution.py:153
  (160 other events, 2538.9 us)
Sparse Core Ops, SparseCore 0:
  217.4 54.7 all-gather.4
  322.1 56.6 all-gather.6
  637.5 58.1 reduce-scatter.10
  802.8 57.2 reduce-scatter.6
  942.6 83.3 reduce-scatter.12
  1029.6 83.9 reduce-scatter.8

commit v2 on v1

v2 whole, which is shorter than its diff:
```python
import jax
import jax.numpy as jnp
from jax import lax
from jax.experimental import pallas as pl
from jax.experimental.pallas import tpu as pltpu
from jax.sharding import PartitionSpec as P

epsilon = 1e-06
capacity = 3


def dot(left, right):
    return jnp.dot(left, right, preferred_element_type=jnp.float32)


def dot_t(left, right):
    return lax.dot_general(left, right, (((1,), (1,)), ((), ())), preferred_element_type=jnp.float32)


def dot_tn(left, right):
    return lax.dot_general(left, right, (((0,), (0,)), ((), ())), preferred_element_type=jnp.float32)


def rms_scale(values):
    widened = values.astype(jnp.float32)
    return lax.rsqrt(jnp.mean(widened * widened, axis=-1, keepdims=True) + epsilon)


def norm_back(values, row_scale, grad_norm):
    widened = values.astype(jnp.float32)
    inner_mean = jnp.mean(grad_norm * widened, axis=-1, keepdims=True)
    return row_scale * grad_norm - widened * (row_scale * row_scale * row_scale) * inner_mean


def slot_of_rows(expert_ids, expert_count, stride, offset):
    chosen = (expert_ids[:, None] == jnp.arange(expert_count, dtype=jnp.int32)[None, :]).astype(
        jnp.int32
    )
    earlier = jnp.arange(expert_ids.shape[0])[:, None] > jnp.arange(expert_ids.shape[0])[None, :]
    same = expert_ids[:, None] == expert_ids[None, :]
    rank = jnp.sum((same & earlier).astype(jnp.int32), axis=1)
    return expert_ids * stride + offset + rank


def table_of(slots, slot_count):
    grid = jnp.arange(slot_count, dtype=jnp.int32)
    return (grid[:, None] == slots[None, :]).astype(jnp.bfloat16)


def run_kernel(body, out_shape, scratch, *operands):
    return pl.pallas_call(
        body,
        out_shape=out_shape,
        in_specs=[pl.BlockSpec(memory_space=pltpu.VMEM) for _ in operands],
        out_specs=jax.tree.map(lambda _: pl.BlockSpec(memory_space=pltpu.VMEM), out_shape),
        scratch_shapes=scratch,
        compiler_params=pltpu.CompilerParams(vmem_limit_bytes=40 * 1024 * 1024),
    )(*operands)


def array(shape, dtype=jnp.bfloat16):
    return jax.ShapeDtypeStruct(shape, dtype)


def unpack_slots(source, rows):
    count, depth, _ = source.shape
    for index in range(count):
        rows[depth * index : depth * (index + 1), :] = source[index].astype(jnp.float32)


def pack_slots(rows, target):
    count, depth, _ = target.shape
    for index in range(count):
        target[index] = rows[depth * index : depth * (index + 1), :].astype(jnp.bfloat16)


def normed_rows(values):
    widened = values.astype(jnp.float32)
    return (widened * rms_scale(values)).astype(jnp.bfloat16)


def send_body(values, table, target, rows):
    rows[...] = dot(table[...], normed_rows(values[...]))
    pack_slots(rows, target)


def take_body(returned, pick_table, values, gate, result, rows):
    unpack_slots(returned, rows)
    gathered = dot(pick_table[...], rows[...].astype(jnp.bfloat16))
    result[...] = (values[...].astype(jnp.float32) + gate[...] * gathered).astype(jnp.bfloat16)


def turn_body(returned, pick_table, values, gate, table, result, target, rows):
    take_body(returned, pick_table, values, gate, result, rows)
    send_body(result, table, target, rows)


def send_back_body(grads, gate, table, target, rows):
    grad_out = (gate[...] * grads[...].astype(jnp.float32)).astype(jnp.bfloat16)
    rows[...] = dot(table[...], grad_out)
    pack_slots(rows, target)


def take_back_body(returned, pick_table, values, grads, result, rows):
    unpack_slots(returned, rows)
    grad_norm = dot(pick_table[...], rows[...].astype(jnp.bfloat16))
    value = values[...]
    result[...] = (
        grads[...].astype(jnp.float32) + norm_back(value, rms_scale(value), grad_norm)
    ).astype(jnp.bfloat16)


def turn_back_body(returned, pick_table, values, grads, gate, table, result, target, rows):
    take_back_body(returned, pick_table, values, grads, result, rows)
    send_back_body(result, gate, table, target, rows)


def serve_body(received, gate_mat, up_mat, down_mat, served, kept, gate_pre, up_pre, rows):
    unpack_slots(received, rows)
    kept[...] = rows[...].astype(jnp.bfloat16)
    gate_pre[...] = dot(kept[...], gate_mat[...])
    up_pre[...] = dot(kept[...], up_mat[...])
    gate = gate_pre[...]
    hidden = (gate * jax.nn.sigmoid(gate) * up_pre[...]).astype(jnp.bfloat16)
    rows[...] = dot(hidden, down_mat[...])
    pack_slots(rows, served)


def serve_back_rows(received, gate_pre, up_pre, down_mat, slot_grads, narrow, rows):
    unpack_slots(received, rows)
    slot_grads[...] = rows[...].astype(jnp.bfloat16)
    gate = gate_pre[...]
    up = up_pre[...]
    gate_sig = jax.nn.sigmoid(gate)
    gate_act = gate * gate_sig
    grad_hidden = dot_t(slot_grads[...], down_mat[...])
    grad_gate = (grad_hidden * up * (gate_sig * (1.0 + gate * (1.0 - gate_sig)))).astype(
        jnp.bfloat16
    )
    grad_up = (grad_hidden * gate_act).astype(jnp.bfloat16)
    inner = gate.shape[1]
    narrow[:, :inner] = (gate_act * up).astype(jnp.bfloat16)
    narrow[:, inner : 2 * inner] = grad_gate
    narrow[:, 2 * inner :] = grad_up
    return (grad_gate, grad_up)


def serve_back_body(
    received, gate_pre, up_pre, gate_mat, up_mat, down_mat, target, slot_grads, narrow, rows
):
    grad_gate, grad_up = serve_back_rows(
        received, gate_pre, up_pre, down_mat, slot_grads, narrow, rows
    )
    rows[...] = dot_t(grad_gate, gate_mat[...]) + dot_t(grad_up, up_mat[...])
    pack_slots(rows, target)


def lowrank_body(
    rows, mats, targets, head, grads, all_normed, all_act, all_pre, all_grads, values, inner, scale
):
    count = mats.shape[0]
    values[0] = rows[...]

    def forward(step, carry):
        index = count - 1 - step
        value = values[step]
        row_scale = rms_scale(value)
        normed = (value.astype(jnp.float32) * row_scale).astype(jnp.bfloat16)
        inner_pre = dot(normed, mats[index, 0])
        act = (inner_pre * jax.nn.sigmoid(inner_pre)).astype(jnp.bfloat16)
        all_normed[index] = normed
        all_act[index] = act
        inner[index] = inner_pre
        scale[index] = row_scale
        values[step + 1] = (
            value.astype(jnp.float32) + dot_t(act, mats[index, 1])
        ).astype(jnp.bfloat16)
        return carry

    lax.fori_loop(0, count, forward, 0)
    final = values[count]
    row_scale = rms_scale(final)
    logits = row_scale * jnp.sum(final.astype(jnp.float32) * head[...], axis=1, keepdims=True)
    grad_logit = jax.nn.sigmoid(logits) - targets[...]
    grads[...] = norm_back(final, row_scale, grad_logit * head[...]).astype(jnp.bfloat16)

    def backward(index, carry):
        value = values[count - 1 - index]
        grad = grads[...]
        inner_pre = inner[index]
        inner_sig = jax.nn.sigmoid(inner_pre)
        grad_act = dot(grad, mats[index, 1])
        grad_pre = (grad_act * (inner_sig * (1.0 + inner_pre * (1.0 - inner_sig)))).astype(
            jnp.bfloat16
        )
        grad_norm = dot_t(grad_pre, mats[index, 0])
        all_pre[index] = grad_pre
        all_grads[index] = grad
        grads[...] = (
            grad.astype(jnp.float32) + norm_back(value, scale[index], grad_norm)
        ).astype(jnp.bfloat16)
        return carry

    lax.fori_loop(0, count, backward, 0)


def lowrank_layers(rows, mats, targets, head):
    count, rank = (mats.shape[0], mats.shape[3])
    row_count, width = rows.shape
    wide = array((count, row_count, width))
    narrow = array((count, row_count, rank))
    return run_kernel(
        lowrank_body,
        (array(rows.shape), wide, narrow, narrow, wide),
        [
            pltpu.VMEM((count + 1, row_count, width), jnp.bfloat16),
            pltpu.VMEM((count, row_count, rank), jnp.float32),
            pltpu.VMEM((count, row_count, 1), jnp.float32),
        ],
        rows,
        mats,
        targets,
        head,
    )


def exchange(buffer):
    return lax.all_to_all(buffer, "expert", split_axis=0, concat_axis=0, tiled=True)


def work_rows(slots, width):
    return [pltpu.VMEM((slots, width), jnp.float32)]


def packed_shape(table, width):
    count = lax.axis_size("expert")
    return array((count, table.shape[0] // count, width))


def send(values, table):
    width = values.shape[1]
    return run_kernel(
        send_body, packed_shape(table, width), work_rows(table.shape[0], width), values, table
    )


def take(returned, route, values):
    table, pick_table, gate = route
    width = values.shape[1]
    return run_kernel(
        take_body,
        array(values.shape),
        work_rows(table.shape[0], width),
        returned,
        pick_table,
        values,
        gate,
    )


def turn(returned, route, values, next_table):
    table, pick_table, gate = route
    width = values.shape[1]
    return run_kernel(
        turn_body,
        (array(values.shape), packed_shape(next_table, width)),
        work_rows(table.shape[0], width),
        returned,
        pick_table,
        values,
        gate,
        next_table,
    )


def send_back(grads, route):
    table, _, gate = route
    width = grads.shape[1]
    return run_kernel(
        send_back_body,
        packed_shape(table, width),
        work_rows(table.shape[0], width),
        grads,
        gate,
        table,
    )


def take_back(returned, route, values, grads):
    table, pick_table, _ = route
    width = values.shape[1]
    return run_kernel(
        take_back_body,
        array(values.shape),
        work_rows(table.shape[0], width),
        returned,
        pick_table,
        values,
        grads,
    )


def turn_back(returned, route, values, grads, next_route):
    table, pick_table, _ = route
    width = values.shape[1]
    return run_kernel(
        turn_back_body,
        (array(values.shape), packed_shape(next_route[0], width)),
        work_rows(table.shape[0], width),
        returned,
        pick_table,
        values,
        grads,
        next_route[2],
        next_route[0],
    )


def serve(received, mats):
    count, depth, width = received.shape
    slots, inner = (count * depth, mats[0].shape[1])
    return run_kernel(
        serve_body,
        (
            array(received.shape),
            array((slots, width)),
            array((slots, inner), jnp.float32),
            array((slots, inner), jnp.float32),
        ),
        work_rows(slots, width),
        received,
        *mats,
    )


def serve_back(received, gate_pre, up_pre, mats):
    count, depth, width = received.shape
    slots, inner = gate_pre.shape
    return run_kernel(
        serve_back_body,
        (array(received.shape), array((slots, width)), array((slots, 3 * inner))),
        work_rows(slots, width),
        received,
        gate_pre,
        up_pre,
        *mats,
    )


def serve_last(received, gate_pre, up_pre, down_mat):
    count, depth, width = received.shape
    slots, inner = gate_pre.shape
    return run_kernel(
        lambda *refs: serve_back_rows(*refs) and None,
        (array((slots, width)), array((slots, 3 * inner))),
        work_rows(slots, width),
        received,
        gate_pre,
        up_pre,
        down_mat,
    )


def local(
    features,
    labels,
    routes,
    route_gates,
    gate_weight,
    up_weight,
    down_weight,
    lowrank_in,
    lowrank_out,
    head_weight,
):
    section_count = lax.axis_size("section")
    section = lax.axis_index("section")
    expert_count = lax.axis_size("expert")
    micro_count, row_count, width = features.shape
    inner = gate_weight.shape[3]
    is_even = section % 2 == 0
    pair = section // 2
    to_odd = [(s, s + 1) for s in range(0, section_count, 2)]
    to_even = [(s + 1, s) for s in range(0, section_count, 2)]

    def swap(value):
        return lax.ppermute(value, "section", to_odd + to_even)

    def hop(value, layer):
        first = 0 if layer % 4 < 2 else 2
        links = []
        for start in range(first, first + section_count, 4):
            for lower in (start, start + 1):
                low_end, high_end = (lower % section_count, (lower + 2) % section_count)
                links += [(low_end, high_end), (high_end, low_end)]
        half = value.shape[0] // 2
        parts = [lax.ppermute(part, "section", links) for part in (value[:half], value[half:])]
        return jnp.concatenate(parts, axis=0)

    own = (gate_weight[0, 0], up_weight[0, 0], down_weight[0, 0])
    other = (swap(own[0]), swap(own[1]))
    down_back = lax.ppermute(own[2], "section", to_even)
    mats_odd = tuple(jnp.where(is_even, b, a) for a, b in zip(own, other + (down_back,)))

    ids = routes[0, :, :, 0]
    plan = jnp.concatenate([ids.astype(jnp.float32), route_gates[0]], axis=0)
    plan_other = swap(plan)

    def route_of(slots, slot_count, gates):
        table = table_of(slots, slot_count)
        grid = jnp.arange(slot_count, dtype=jnp.int32)
        pick_table = (slots[:, None] == grid[None, :]).astype(jnp.bfloat16)
        return (table, pick_table, gates[:, None])

    def pick(first, second):
        chosen = jnp.where(is_even, first, second)
        mine = jnp.where(is_even, chosen[0::2], chosen[1::2])
        slots = slot_of_rows(mine[0].astype(jnp.int32), expert_count, capacity, 0)
        return route_of(slots, expert_count * capacity, mine[1])

    route_even = pick(plan, plan_other)
    route_odd = pick(plan_other, plan)
    joint_slots = jnp.concatenate(
        [
            slot_of_rows(ids[m], expert_count, capacity * micro_count, capacity * m)
            for m in range(micro_count)
        ]
    )
    route_all = route_of(
        joint_slots, expert_count * capacity * micro_count, route_gates[0].reshape(-1)
    )
    routing = [route_odd if layer % 2 else route_even for layer in range(section_count)]

    first_rows = features.reshape(-1, width)
    served, kept_all, gate_all, up_all = serve(exchange(send(first_rows, route_all[0])), own)
    second_rows = take(exchange(served), route_all, first_rows)
    crossing = lax.ppermute(second_rows[row_count:], "section", to_odd)
    rows = jnp.where(is_even, second_rows[:row_count], crossing)
    rows, late = lax.optimization_barrier((rows, own[2]))
    down_on = lax.ppermute(late, "section", to_odd)
    mats_even = tuple(jnp.where(is_even, a, b) for a, b in zip(own, other + (down_on,)))
    mats = [mats_odd if layer % 2 else mats_even for layer in range(section_count)]

    layer_rows = {}
    layer_kept = {}
    sending = send(rows, routing[1][0])
    for layer in range(1, section_count):
        layer_rows[layer] = rows
        served, *layer_kept[layer] = serve(exchange(sending), mats[layer])
        returned = exchange(served)
        if layer % 2 == 0:
            rows, sending = turn(returned, routing[layer], rows, routing[layer + 1][0])
            if layer == 2:
                low_own = jnp.stack([lowrank_in[0], lowrank_out[0].T])
                low_own, rows = lax.optimization_barrier((low_own, rows))
                low_mats = lax.all_gather(low_own, "section")
        else:
            rows = take(returned, routing[layer], rows)
            if layer < section_count - 1:
                rows = hop(rows, layer)
                sending = send(rows, routing[layer + 1][0])

    targets = jnp.where(is_even, labels[0], labels[1]).astype(jnp.float32)[:, None]
    grads, low_normed, low_act, low_pre, low_grads = lowrank_layers(
        rows, low_mats, targets, head_weight[None, :]
    )

    def low_part(wide, narrow):
        part = dot_tn(wide, narrow).astype(jnp.bfloat16)
        return part.reshape(expert_count, 1, -1, part.shape[1])

    parts = jnp.stack(
        [
            jnp.concatenate(
                [
                    low_part(low_normed[index], low_pre[index]),
                    low_part(low_grads[index], low_act[index]),
                ],
                axis=1,
            )
            for index in range(section_count)
        ],
        axis=1,
    )
    last_pair = section_count // 2 - 1
    parts = jnp.where(pair == last_pair, parts, jnp.zeros_like(parts))

    saved = {0: None, 1: None}
    sending = send_back(grads, routing[section_count - 1])
    for layer in reversed(range(1, section_count)):
        kept, gate_pre, up_pre = layer_kept[layer]
        target, slot_grads, narrow = serve_back(exchange(sending), gate_pre, up_pre, mats[layer])
        returned = exchange(target)
        values = layer_rows[layer]
        if layer % 2 == 1 and layer > 1:
            grads, sending = turn_back(returned, routing[layer], values, grads, routing[layer - 1])
        else:
            grads = take_back(returned, routing[layer], values, grads)
        record = (kept, slot_grads, narrow)
        past = saved[layer % 2]
        saved[layer % 2] = (
            record
            if past is None
            else tuple(
                jnp.where(pair == layer // 2, new, old) for new, old in zip(record, past)
            )
        )
        if layer == 6:
            parts, grads = lax.optimization_barrier((parts, grads))
            share = lax.psum_scatter(
                parts.reshape(-1, parts.shape[-1]), "expert", scatter_dimension=0, tiled=True
            ).reshape(parts.shape[1:])
        if layer == 2:
            share, grads = lax.optimization_barrier((share, grads))
            share = lax.all_to_all(share, "section", split_axis=0, concat_axis=0, tiled=True)
        if layer % 2 == 0:
            grads = hop(grads, layer - 2)
            sending = send_back(grads, routing[layer - 1])

    all_grads = jnp.concatenate([grads, lax.ppermute(grads, "section", to_even)], axis=0)
    theirs = tuple(swap(jnp.where(is_even, b, a)) for a, b in zip(saved[0], saved[1]))
    held = tuple(jnp.where(is_even, a, b) for a, b in zip(saved[0], saved[1]))
    joint = (kept_all,) + tuple(
        serve_last(exchange(send_back(all_grads, route_all)), gate_all, up_all, own[2])
    )
    kept, slot_grads, narrow = (
        jnp.where(section == 0, both, jnp.concatenate([mine, other], axis=0))
        for both, mine, other in zip(joint, held, theirs)
    )
    hidden, grad_gate, grad_up = (narrow[:, inner * k : inner * (k + 1)] for k in range(3))
    share = jnp.sum(share[2 * last_pair :].astype(jnp.float32), axis=0)
    return (
        dot_tn(kept, grad_gate)[None, None],
        dot_tn(kept, grad_up)[None, None],
        dot_tn(hidden, slot_grads)[None, None],
        share[0][None],
        share[1].T[None],
    )


def solution(mesh):
    return jax.shard_map(
        local,
        mesh=mesh,
        in_specs=(
            P(None, "expert", None),
            P(None, "expert"),
            P("section", None, "expert", None),
            P("section", None, "expert"),
            P("section", "expert", None, None),
            P("section", "expert", None, None),
            P("section", "expert", None, None),
            P("section", None, None),
            P("section", None, None),
            P(),
        ),
        out_specs=(
            P("section", "expert", None, None),
            P("section", "expert", None, None),
            P("section", "expert", None, None),
            P("section", "expert", None),
            P("section", None, "expert"),
        ),
        check_vma=False,
    )
```

time: 1140 us -> 832 us (0.73)
  waiting for transfers between devices: 392 us -> 219 us
  matrix products: 173 us -> 29.6 us
  local copies, waits for them, and re-layouts: 139 us -> 64.9 us
  Pallas kernels: 0 us -> 62.2 us
  blocking collectives: 238 us -> 267 us
    reshape x62 -> x0, local copies, waits for them, and re-layouts: 116 us -> none  [the longest x31 58.7 us: exchange(): shaped = buffer.reshape(expert_count, -1, buffer.shape[1])]
    dot_general x94 -> x0, matrix products: 112 us -> none  [the longest x56 77.1 us: dot(): return jnp.dot(left, right, preferred_element_type=jnp.float32)]
    reduce_scatter x3 -> x1, waiting for transfers between devices: 86.1 us -> 0.01 us  [local(): lax.psum_scatter(parts.reshape(-1, parts.shape[-1]), 'expert', scatter_di...]
    pallas_call x0 -> x42, Pallas kernels: none -> 62.2 us  [run_kernel(): pl.pallas_call(body, out_shape=out_shape, in_specs=[pl.BlockSpec(memory_s...]
    unnamed x7 -> x2, waiting for transfers between devices: 60.4 us -> 0.03 us
    unnamed x297 -> x293, local copies, waits for them, and re-layouts: 21.9 us -> 59.6 us
    dot_general x34 -> x19, matrix products: 61.8 us -> 29.6 us  [dot_tn(): lax.dot_general(left, right, (((0,), (0,)), ((), ())), preferred_element_...]
    all_to_all x17 -> x15, waiting for transfers between devices: 164 us -> 132 us  [the longest x14 129 us: exchange(): lax.all_to_all(buffer, 'expert', split_axis=0, concat_axis=0, tiled=True)]
  transfers between devices with their start and end apart: 37 -> 39, of which waited for: 27 -> 30; matrix products, arithmetic and copies ran while one was open for 22% -> 7% of each run, Pallas kernels for 0% -> 4%
where the time goes in v2:
time: 832 us; the launch traced here: 820 us
  blocking collectives  267 us (32%)
  waiting for transfers between devices  219 us (26%)
  starting transfers between devices  120 us (14%)
  local copies, waits for them, and re-layouts  64.9 us (8%)
  Pallas kernels  62.2 us (7%)
  other arithmetic  40.8 us (5%)
  matrix products  29.6 us (4%)
  between operations  16.1 us (2%)
    all_to_all x17, blocking collectives, exchange(): lax.all_to_all(buffer, 'expert', split_axis=0, concat_axis=0, tiled=True)  267 us
    all_to_all x14, waiting for transfers between devices, exchange(): lax.all_to_all(buffer, 'expert', split_axis=0, concat_axis=0, tiled=True)  129 us
    all_to_all x14, starting transfers between devices, exchange(): lax.all_to_all(buffer, 'expert', split_axis=0, concat_axis=0, tiled=True)  78.1 us
    ppermute x12, waiting for transfers between devices, hop(): lax.ppermute(part, 'section', links)  71.1 us
    pallas_call x42, Pallas kernels, run_kernel(): pl.pallas_call(body, out_shape=out_shape, in_specs=[pl.BlockSpec(memory_s...  62.2 us
    unnamed x293, local copies, waits for them, and re-layouts  59.6 us
    dot_general x19, matrix products, dot_tn(): lax.dot_general(left, right, (((0,), (0,)), ((), ())), preferred_element_...  29.6 us
    ppermute x12, starting transfers between devices, hop(): lax.ppermute(part, 'section', links)  20.7 us
  transfers between devices with their start and end apart: 39, of which 30 were waited for; matrix products, arithmetic and copies ran while one was open for 7% of the time, Pallas kernels for 4%

profile of v2, /device:TPU:1, one launch (start us, length us, event | category | flops | bytes accessed | tf_op | source)
XLA Modules:
  0.0 819.9 jit_solution(5379997315076063841)
XLA Ops:
  25.1 12.2 %all-to-all-done.received = bf16[32,6,2048]{2,1,0:T(8,128)(2,1)S(1)} async-done(((bf16[32,6,2048]{2,1,0:T(8,128)(2,1)}), bf16[32,6,2048]{2,1,0:T(8,128)(2,1)S(1)}, u32[]{:S(2)}, u32[]{:S(2)}) %all-to-all-start) | async-done | bytes 786464 | tf_op jit(solution)/shard_map/all_to_all | solution.py:228
  47.2 17.1 %all-to-all-done.1.returned = bf16[32,6,2048]{2,1,0:T(8,128)(2,1)S(1)} async-done(((bf16[32,6,2048]{2,1,0:T(8,128)(2,1)}), bf16[32,6,2048]{2,1,0:T(8,128)(2,1)S(1)}, u32[]{:S(2)}, u32[]{:S(2)}) %all-to-all-start.1) | async-done | bytes 786464 | tf_op jit(solution)/shard_map/all_to_all | solution.py:228
  115.1 11.5 %all-to-all-done.3.returned = bf16[32,3,2048]{2,1,0:T(4,128)(2,1)} async-done(((bf16[32,3,2048]{2,1,0:T(4,128)(2,1)}), bf16[32,3,2048]{2,1,0:T(4,128)(2,1)}, u32[]{:S(2)}, u32[]{:S(2)}) %all-to-all-start.3) | async-done | bytes 393248 | tf_op jit(solution)/shard_map/all_to_all | solution.py:228
  175.4 11.6 %all-to-all-done.5.returned = bf16[32,3,2048]{2,1,0:T(4,128)(2,1)} async-done(((bf16[32,3,2048]{2,1,0:T(4,128)(2,1)}), bf16[32,3,2048]{2,1,0:T(4,128)(2,1)}, u32[]{:S(2)}, u32[]{:S(2)}) %all-to-all-start.5) | async-done | bytes 393248 | tf_op jit(solution)/shard_map/all_to_all | solution.py:228
  191.3 15.7 %all_to_all.160.received = bf16[32,3,2048]{2,1,0:T(4,128)(2,1)S(1)} all-to-all(bf16[32,3,2048]{2,1,0:T(4,128)(2,1)} %copy-done.55), channel_id=1, replica_groups=mesh['section'=8,'expert'=32] {'expert'}, dimensions={0} | all-to-all | bytes 786432 | tf_op jit(solution)/shard_map/all_to_all | solution.py:228
  210.0 15.2 %all_to_all.161.returned = bf16[32,3,2048]{2,1,0:T(4,128)(2,1)S(1)} all-to-all(bf16[32,3,2048]{2,1,0:T(4,128)(2,1)S(1)} %get-tuple-element.93), channel_id=1, replica_groups=mesh['section'=8,'expert'=32] {'expert'}, dimensions={0} | all-to-all | bytes 786432 | tf_op jit(solution)/shard_map/all_to_all | solution.py:228
  246.1 15.9 %all_to_all.162.received = bf16[32,3,2048]{2,1,0:T(4,128)(2,1)S(1)} all-to-all(bf16[32,3,2048]{2,1,0:T(4,128)(2,1)S(1)} %shard_map.148), channel_id=1, replica_groups=mesh['section'=8,'expert'=32] {'expert'}, dimensions={0} | all-to-all | bytes 786432 | tf_op jit(solution)/shard_map/all_to_all | solution.py:228
  265.1 15.2 %all_to_all.163.returned = bf16[32,3,2048]{2,1,0:T(4,128)(2,1)S(1)} all-to-all(bf16[32,3,2048]{2,1,0:T(4,128)(2,1)S(1)} %get-tuple-element.97), channel_id=1, replica_groups=mesh['section'=8,'expert'=32] {'expert'}, dimensions={0} | all-to-all | bytes 786432 | tf_op jit(solution)/shard_map/all_to_all | solution.py:228
  281.2 15.2 %all_to_all.164.received = bf16[32,3,2048]{2,1,0:T(4,128)(2,1)S(1)} all-to-all(bf16[32,3,2048]{2,1,0:T(4,128)(2,1)S(1)} %get-tuple-element.98), channel_id=1, replica_groups=mesh['section'=8,'expert'=32] {'expert'}, dimensions={0} | all-to-all | bytes 786432 | tf_op jit(solution)/shard_map/all_to_all | solution.py:228
  297.3 15.2 %all_to_all.165.returned = bf16[32,3,2048]{2,1,0:T(4,128)(2,1)S(1)} all-to-all(bf16[32,3,2048]{2,1,0:T(4,128)(2,1)S(1)} %get-tuple-element.99), channel_id=1, replica_groups=mesh['section'=8,'expert'=32] {'expert'}, dimensions={0} | all-to-all | bytes 786432 | tf_op jit(solution)/shard_map/all_to_all | solution.py:228
  329.2 15.5 %all_to_all.166.received = bf16[32,3,2048]{2,1,0:T(4,128)(2,1)S(1)} all-to-all(bf16[32,3,2048]{2,1,0:T(4,128)(2,1)S(1)} %shard_map.153), channel_id=1, replica_groups=mesh['section'=8,'expert'=32] {'expert'}, dimensions={0} | all-to-all | bytes 786432 | tf_op jit(solution)/shard_map/all_to_all | solution.py:228
  345.6 15.6 %all_to_all.167.returned = bf16[32,3,2048]{2,1,0:T(4,128)(2,1)S(1)} all-to-all(bf16[32,3,2048]{2,1,0:T(4,128)(2,1)S(1)} %get-tuple-element.105), channel_id=1, replica_groups=mesh['section'=8,'expert'=32] {'expert'}, dimensions={0} | all-to-all | bytes 786432 | tf_op jit(solution)/shard_map/all_to_all | solution.py:228
  362.8 15.2 %all_to_all.168.received = bf16[32,3,2048]{2,1,0:T(4,128)(2,1)S(1)} all-to-all(bf16[32,3,2048]{2,1,0:T(4,128)(2,1)S(1)} %get-tuple-element.106), channel_id=1, replica_groups=mesh['section'=8,'expert'=32] {'expert'}, dimensions={0} | all-to-all | bytes 786432 | tf_op jit(solution)/shard_map/all_to_all | solution.py:228
  407.0 10.4 %shard_map.158 = (bf16[64,2048]{1,0:T(8,128)(2,1)S(1)}, bf16[8,64,2048]{2,1,0:T(8,128)(2,1)S(1)}, bf16[8,64,128]{2,1,0:T(8,128)(2,1)S(1)}, bf16[8,64,128]{2,1,0:T(8,128)(2,1)S(1)}, bf16[8,64,2048]{2,1,0:T(8,128)(2,1)S(1)}) custom-call(bf16[64,2048]{1,0:T(8,128)(2,1)S(1)} %copy-done.43, bf16[8,2,2048,128]{3,2,1,0:T(8,128)(2,1)S(1)} %bitcast.243, ...), custom_call_target="tpu_custom_call" | custom-call | tf_op jit(solution)/shard_map/pallas_call | solution.py:51
  543.9 15.0 %all_to_all.169.received = bf16[32,3,2048]{2,1,0:T(4,128)(2,1)S(1)} all-to-all(bf16[32,3,2048]{2,1,0:T(4,128)(2,1)S(1)} %shard_map.164), channel_id=1, replica_groups=mesh['section'=8,'expert'=32] {'expert'}, dimensions={0} | all-to-all | bytes 786432 | tf_op jit(solution)/shard_map/all_to_all | solution.py:228
  561.4 15.5 %all_to_all.170.returned = bf16[32,3,2048]{2,1,0:T(4,128)(2,1)S(1)} all-to-all(bf16[32,3,2048]{2,1,0:T(4,128)(2,1)S(1)} %get-tuple-element.128), channel_id=1, replica_groups=mesh['section'=8,'expert'=32] {'expert'}, dimensions={0} | all-to-all | bytes 786432 | tf_op jit(solution)/shard_map/all_to_all | solution.py:228
  577.9 19.7 %all_to_all.171.received = bf16[32,3,2048]{2,1,0:T(4,128)(2,1)S(1)} all-to-all(bf16[32,3,2048]{2,1,0:T(4,128)(2,1)S(1)} %get-tuple-element.129), channel_id=1, replica_groups=mesh['section'=8,'expert'=32] {'expert'}, dimensions={0} | all-to-all | bytes 786432 | tf_op jit(solution)/shard_map/all_to_all | solution.py:228
  599.5 16.6 %all_to_all.172.returned = bf16[32,3,2048]{2,1,0:T(4,128)(2,1)S(1)} all-to-all(bf16[32,3,2048]{2,1,0:T(4,128)(2,1)S(1)} %get-tuple-element.132), channel_id=1, replica_groups=mesh['section'=8,'expert'=32] {'expert'}, dimensions={0} | all-to-all | bytes 786432 | tf_op jit(solution)/shard_map/all_to_all | solution.py:228
  628.9 15.7 %all_to_all.173.received = bf16[32,3,2048]{2,1,0:T(4,128)(2,1)S(1)} all-to-all(bf16[32,3,2048]{2,1,0:T(4,128)(2,1)S(1)} %shard_map.169), channel_id=1, replica_groups=mesh['section'=8,'expert'=32] {'expert'}, dimensions={0} | all-to-all | bytes 786432 | tf_op jit(solution)/shard_map/all_to_all | solution.py:228
  647.2 15.3 %all_to_all.174.returned = bf16[32,3,2048]{2,1,0:T(4,128)(2,1)S(1)} all-to-all(bf16[32,3,2048]{2,1,0:T(4,128)(2,1)S(1)} %get-tuple-element.136), channel_id=1, replica_groups=mesh['section'=8,'expert'=32] {'expert'}, dimensions={0} | all-to-all | bytes 786432 | tf_op jit(solution)/shard_map/all_to_all | solution.py:228
  663.5 15.2 %all_to_all.175.received = bf16[32,3,2048]{2,1,0:T(4,128)(2,1)S(1)} all-to-all(bf16[32,3,2048]{2,1,0:T(4,128)(2,1)S(1)} %get-tuple-element.137), channel_id=1, replica_groups=mesh['section'=8,'expert'=32] {'expert'}, dimensions={0} | all-to-all | bytes 786432 | tf_op jit(solution)/shard_map/all_to_all | solution.py:228
  680.6 15.2 %all_to_all.176.returned = bf16[32,3,2048]{2,1,0:T(4,128)(2,1)S(1)} all-to-all(bf16[32,3,2048]{2,1,0:T(4,128)(2,1)S(1)} %get-tuple-element.140), channel_id=1, replica_groups=mesh['section'=8,'expert'=32] {'expert'}, dimensions={0} | all-to-all | bytes 786432 | tf_op jit(solution)/shard_map/all_to_all | solution.py:228
  721.0 11.7 %all-to-all-done.28.received = bf16[32,3,2048]{2,1,0:T(4,128)(2,1)} async-done(((bf16[32,3,2048]{2,1,0:T(4,128)(2,1)}), bf16[32,3,2048]{2,1,0:T(4,128)(2,1)}, u32[]{:S(2)}, u32[]{:S(2)}) %all-to-all-start.28) | async-done | bytes 393248 | tf_op jit(solution)/shard_map/all_to_all | solution.py:228
  785.2 14.5 %all-to-all-done.30.refs_0_ = bf16[32,6,2048]{2,1,0:T(8,128)(2,1)S(1)} async-done(((bf16[32,6,2048]{2,1,0:T(8,128)(2,1)}), bf16[32,6,2048]{2,1,0:T(8,128)(2,1)S(1)}, u32[]{:S(2)}, u32[]{:S(2)}) %all-to-all-start.30) | async-done | bytes 786464 | tf_op jit(solution)/shard_map/all_to_all | solution.py:228
  (495 shorter events, 447.9 us)
Async XLA Ops:
  11.5 25.8 %all-to-all-start = ((bf16[32,6,2048]{2,1,0:T(8,128)(2,1)}), bf16[32,6,2048]{2,1,0:T(8,128)(2,1)S(1)}, u32[]{:S(2)}, u32[]{:S(2)}) async-start(bf16[32,6,2048]{2,1,0:T(8,128)(2,1)} %shard_map.137), calls=%async_computation | async-start | bytes 2097152 | tf_op jit(solution)/shard_map/all_to_all | solution.py:228
  21.9 56.8 %collective-permute-start.2 = (bf16[2048,256]{1,0:T(8,128)(2,1)}, bf16[2048,256]{1,0:T(8,128)(2,1)}, u32[]{:S(2)}, u32[]{:S(2)}) collective-permute-start(bf16[2048,256]{1,0:T(8,128)(2,1)} %bitcast.3.gate_mat), channel_id=1, source_target_pairs={{0,32},{64,96},{128,160},{192,224},{32,0},{96,64},{160,128},{224,1... | collective-permute-start | bytes 3145736 | tf_op jit(solution)/shard_map/ppermute | solution.py:387
  22.0 59.3 %collective-permute-start.3 = (bf16[2048,256]{1,0:T(8,128)(2,1)}, bf16[2048,256]{1,0:T(8,128)(2,1)}, u32[]{:S(2)}, u32[]{:S(2)}) collective-permute-start(bf16[2048,256]{1,0:T(8,128)(2,1)} %bitcast.4.up_mat), channel_id=1, source_target_pairs={{0,32},{64,96},{128,160},{192,224},{32,0},{96,64},{160,128},{224,1... | collective-permute-start | bytes 3145736 | tf_op jit(solution)/shard_map/ppermute | solution.py:387
  23.4 69.4 %collective-permute-start.4 = (bf16[256,2048]{1,0:T(8,128)(2,1)}, bf16[256,2048]{1,0:T(8,128)(2,1)}, u32[]{:S(2)}, u32[]{:S(2)}) collective-permute-start(bf16[256,2048]{1,0:T(8,128)(2,1)} %bitcast.5.down_mat.refs_3_), channel_id=1, source_target_pairs={{32,0},{96,64},{160,128},{224,192},{33,1},{97,65},{161,129},{225,1... | collective-permute-start | bytes 3145736 | tf_op jit(solution)/shard_map/ppermute | solution.py:402
  42.8 21.4 %all-to-all-start.1 = ((bf16[32,6,2048]{2,1,0:T(8,128)(2,1)}), bf16[32,6,2048]{2,1,0:T(8,128)(2,1)S(1)}, u32[]{:S(2)}, u32[]{:S(2)}) async-start(bf16[32,6,2048]{2,1,0:T(8,128)(2,1)} %copy-done.33), calls=%async_computation.1 | async-start | bytes 2097152 | tf_op jit(solution)/shard_map/all_to_all | solution.py:228
  73.6 25.6 %collective-permute-start.7 = (bf16[256,2048]{1,0:T(8,128)(2,1)}, bf16[256,2048]{1,0:T(8,128)(2,1)}, u32[]{:S(2)}, u32[]{:S(2)}) collective-permute-start(bf16[256,2048]{1,0:T(8,128)(2,1)} %bitcast.5.down_mat.refs_3_), channel_id=1, source_target_pairs={{0,32},{64,96},{128,160},{192,224},{1,33},{65,97},{129,161},{193,2... | collective-permute-start | bytes 3145736 | tf_op jit(solution)/shard_map/ppermute | solution.py:440
  85.3 19.1 %all-to-all-start.2 = ((bf16[32,3,2048]{2,1,0:T(4,128)(2,1)}), bf16[32,3,2048]{2,1,0:T(4,128)(2,1)}, u32[]{:S(2)}, u32[]{:S(2)}) async-start(bf16[32,3,2048]{2,1,0:T(4,128)(2,1)} %shard_map.140), calls=%async_computation.2 | async-start | bytes 1048576 | tf_op jit(solution)/shard_map/all_to_all | solution.py:228
  109.2 17.4 %all-to-all-start.3 = ((bf16[32,3,2048]{2,1,0:T(4,128)(2,1)}), bf16[32,3,2048]{2,1,0:T(4,128)(2,1)}, u32[]{:S(2)}, u32[]{:S(2)}) async-start(bf16[32,3,2048]{2,1,0:T(4,128)(2,1)} %copy-done.54), calls=%async_computation.3 | async-start | bytes 1048576 | tf_op jit(solution)/shard_map/all_to_all | solution.py:228
  145.1 16.9 %all-to-all-start.4 = ((bf16[32,3,2048]{2,1,0:T(4,128)(2,1)}), bf16[32,3,2048]{2,1,0:T(4,128)(2,1)}, u32[]{:S(2)}, u32[]{:S(2)}) async-start(bf16[32,3,2048]{2,1,0:T(4,128)(2,1)} %copy-done.28), calls=%async_computation.4 | async-start | bytes 1048576 | tf_op jit(solution)/shard_map/all_to_all | solution.py:228
  170.4 16.6 %all-to-all-start.5 = ((bf16[32,3,2048]{2,1,0:T(4,128)(2,1)}), bf16[32,3,2048]{2,1,0:T(4,128)(2,1)}, u32[]{:S(2)}, u32[]{:S(2)}) async-start(bf16[32,3,2048]{2,1,0:T(4,128)(2,1)} %copy-done.51), calls=%async_computation.5 | async-start | bytes 1048576 | tf_op jit(solution)/shard_map/all_to_all | solution.py:228
  175.3 226.0 %all-gather.3.cloned.1.call-start = ((), (), s32[]{:S(2)}) async-start(), calls=%async_computation.34 | async-start | bytes 9437184 | tf_op jit(solution)/shard_map/all_gather | solution.py:456
  228.5 17.0 %collective-permute-start.9 = (bf16[32,2048]{1,0:T(8,128)(2,1)S(1)}, bf16[32,2048]{1,0:T(8,128)(2,1)S(1)}, u32[]{:S(2)}, u32[]{:S(2)}) collective-permute-start(bf16[32,2048]{1,0:T(8,128)(2,1)S(1)} %get-tuple-element.188), channel_id=1, source_target_pairs={{64,128},{128,64},{96,160},{160,96},{192,0},{0,192},{224,32},{32,2... | collective-permute-start | bytes 393224 | tf_op jit(solution)/shard_map/ppermute | solution.py:397
  381.8 16.4 %all-to-all-start.15 = ((bf16[32,3,2048]{2,1,0:T(4,128)(2,1)}), bf16[32,3,2048]{2,1,0:T(4,128)(2,1)}, u32[]{:S(2)}, u32[]{:S(2)}) async-start(bf16[32,3,2048]{2,1,0:T(4,128)(2,1)} %copy-done.48), calls=%async_computation.15 | async-start | bytes 1048576 | tf_op jit(solution)/shard_map/all_to_all | solution.py:228
  434.0 16.4 %all-to-all-start.16 = ((bf16[32,3,2048]{2,1,0:T(4,128)(2,1)}), bf16[32,3,2048]{2,1,0:T(4,128)(2,1)}, u32[]{:S(2)}, u32[]{:S(2)}) async-start(bf16[32,3,2048]{2,1,0:T(4,128)(2,1)} %copy-done.26), calls=%async_computation.16 | async-start | bytes 1048576 | tf_op jit(solution)/shard_map/all_to_all | solution.py:228
  457.2 18.3 %all-to-all-start.17 = ((bf16[32,3,2048]{2,1,0:T(4,128)(2,1)}), bf16[32,3,2048]{2,1,0:T(4,128)(2,1)}, u32[]{:S(2)}, u32[]{:S(2)}) async-start(bf16[32,3,2048]{2,1,0:T(4,128)(2,1)} %copy-done.50), calls=%async_computation.17 | async-start | bytes 1048576 | tf_op jit(solution)/shard_map/all_to_all | solution.py:228
  481.0 16.4 %all-to-all-start.18 = ((bf16[32,3,2048]{2,1,0:T(4,128)(2,1)}), bf16[32,3,2048]{2,1,0:T(4,128)(2,1)}, u32[]{:S(2)}, u32[]{:S(2)}) async-start(bf16[32,3,2048]{2,1,0:T(4,128)(2,1)} %copy-done.52), calls=%async_computation.18 | async-start | bytes 1048576 | tf_op jit(solution)/shard_map/all_to_all | solution.py:228
  507.8 16.4 %all-to-all-start.19 = ((bf16[32,3,2048]{2,1,0:T(4,128)(2,1)}), bf16[32,3,2048]{2,1,0:T(4,128)(2,1)}, u32[]{:S(2)}, u32[]{:S(2)}) async-start(bf16[32,3,2048]{2,1,0:T(4,128)(2,1)} %copy-done.53), calls=%async_computation.19 | async-start | bytes 1048576 | tf_op jit(solution)/shard_map/all_to_all | solution.py:228
  512.5 184.6 %reduce-scatter.2.cloned.1.call-start = ((), (), s32[]{:S(2)}) async-start(), calls=%async_computation.33 | async-start | bytes 8650752 | tf_op jit(solution)/shard_map/reduce_scatter | solution.py:510
  715.8 16.9 %all-to-all-start.28 = ((bf16[32,3,2048]{2,1,0:T(4,128)(2,1)}), bf16[32,3,2048]{2,1,0:T(4,128)(2,1)}, u32[]{:S(2)}, u32[]{:S(2)}) async-start(bf16[32,3,2048]{2,1,0:T(4,128)(2,1)} %copy-done.27), calls=%async_computation.29 | async-start | bytes 1048576 | tf_op jit(solution)/shard_map/all_to_all | solution.py:228
  747.6 17.4 %all-to-all-start.29 = ((bf16[32,3,2048]{2,1,0:T(4,128)(2,1)}), bf16[32,3,2048]{2,1,0:T(4,128)(2,1)S(1)}, u32[]{:S(2)}, u32[]{:S(2)}) async-start(bf16[32,3,2048]{2,1,0:T(4,128)(2,1)} %copy-done.49), calls=%async_computation.30 | async-start | bytes 1048576 | tf_op jit(solution)/shard_map/all_to_all | solution.py:228
  755.1 48.5 %collective-permute-start.12 = (bf16[96,2048]{1,0:T(8,128)(2,1)}, bf16[96,2048]{1,0:T(8,128)(2,1)}, u32[]{:S(2)}, u32[]{:S(2)}) collective-permute-start(bf16[96,2048]{1,0:T(8,128)(2,1)} %broadcast_select_fusion.9), channel_id=1, source_target_pairs={{0,32},{64,96},{128,160},{192,224},{32,0},{96,64},{160,128},{224,1... | collective-permute-start | bytes 1179656 | tf_op jit(solution)/shard_map/ppermute | solution.py:387
  768.3 34.2 %collective-permute-start.20 = (bf16[96,768]{1,0:T(8,128)(2,1)}, bf16[96,768]{1,0:T(8,128)(2,1)}, u32[]{:S(2)}, u32[]{:S(2)}) collective-permute-start(bf16[96,768]{1,0:T(8,128)(2,1)} %broadcast_select_fusion.11), channel_id=1, source_target_pairs={{0,32},{64,96},{128,160},{192,224},{32,0},{96,64},{160,128},{224,1... | collective-permute-start | bytes 442376 | tf_op jit(solution)/shard_map/ppermute | solution.py:387
  776.5 23.2 %all-to-all-start.30 = ((bf16[32,6,2048]{2,1,0:T(8,128)(2,1)}), bf16[32,6,2048]{2,1,0:T(8,128)(2,1)S(1)}, u32[]{:S(2)}, u32[]{:S(2)}) async-start(bf16[32,6,2048]{2,1,0:T(8,128)(2,1)} %shard_map.177), calls=%async_computation.31 | async-start | bytes 2097152 | tf_op jit(solution)/shard_map/all_to_all | solution.py:228
  785.2 24.6 %collective-permute-start.21 = (bf16[96,2048]{1,0:T(8,128)(2,1)}, bf16[96,2048]{1,0:T(8,128)(2,1)}, u32[]{:S(2)}, u32[]{:S(2)}) collective-permute-start(bf16[96,2048]{1,0:T(8,128)(2,1)} %broadcast_select_fusion.7), channel_id=1, source_target_pairs={{0,32},{64,96},{128,160},{192,224},{32,0},{96,64},{160,128},{224,1... | collective-permute-start | bytes 1179656 | tf_op jit(solution)/shard_map/ppermute | solution.py:387
  (158 other events, 1739.0 us)
Sparse Core Ops, SparseCore 0:
  191.5 103.2 all-gather.2
  528.6 99.4 reduce-scatter.1

commit v3 on v2

--- a/solution.py
+++ b/solution.py
@@ -47,13 +47,26 @@
     return (grid[:, None] == slots[None, :]).astype(jnp.bfloat16)
 
 
-def run_kernel(body, out_shape, scratch, *operands):
+def run_kernel(body, out_shape, scratch, *operands, far=(), far_out=(), scalars=(), aliases={}):
+    everywhere = pl.BlockSpec(memory_space=pltpu.HBM)
+    near = pl.BlockSpec(memory_space=pltpu.VMEM)
+    small = pl.BlockSpec(memory_space=pltpu.SMEM)
+    in_specs = [
+        small if k in scalars else everywhere if k in far else near for k in range(len(operands))
+    ]
+    leaves, treedef = jax.tree.flatten(out_shape)
+    leaves = [
+        pltpu.HBM(leaf.shape, leaf.dtype) if k in far_out else leaf
+        for k, leaf in enumerate(leaves)
+    ]
+    out_specs = [everywhere if k in far_out else near for k in range(len(leaves))]
     return pl.pallas_call(
         body,
-        out_shape=out_shape,
-        in_specs=[pl.BlockSpec(memory_space=pltpu.VMEM) for _ in operands],
-        out_specs=jax.tree.map(lambda _: pl.BlockSpec(memory_space=pltpu.VMEM), out_shape),
+        out_shape=jax.tree.unflatten(treedef, leaves),
+        in_specs=in_specs,
+        out_specs=jax.tree.unflatten(treedef, out_specs),
         scratch_shapes=scratch,
+        input_output_aliases=aliases,
         compiler_params=pltpu.CompilerParams(vmem_limit_bytes=40 * 1024 * 1024),
     )(*operands)
 
@@ -84,15 +97,34 @@
     pack_slots(rows, target)
 
 
-def take_body(returned, pick_table, values, gate, result, rows):
+def take_rows(returned, pick_table, values, gate, result, rows):
     unpack_slots(returned, rows)
     gathered = dot(pick_table[...], rows[...].astype(jnp.bfloat16))
     result[...] = (values[...].astype(jnp.float32) + gate[...] * gathered).astype(jnp.bfloat16)
 
 
-def turn_body(returned, pick_table, values, gate, table, result, target, rows):
-    take_body(returned, pick_table, values, gate, result, rows)
+def keep(flag, copies, begin):
+    @pl.when(flag[0] == 1)
+    def _():
+        for copy in copies:
+            copy.start() if begin else copy.wait()
+
+
+def take_body(flag, returned, pick_table, values, gate, old, result, record, rows, done):
+    copies = [pltpu.make_async_copy(values, record, done.at[0])]
+    keep(flag, copies, True)
+    take_rows(returned, pick_table, values, gate, result, rows)
+    keep(flag, copies, False)
+
+
+def turn_body(
+    flag, returned, pick_table, values, gate, old, table, result, record, target, rows, done
+):
+    copies = [pltpu.make_async_copy(values, record, done.at[0])]
+    keep(flag, copies, True)
+    take_rows(returned, pick_table, values, gate, result, rows)
     send_body(result, table, target, rows)
+    keep(flag, copies, False)
 
 
 def send_back_body(grads, gate, table, target, rows):
@@ -101,39 +133,67 @@
     pack_slots(rows, target)
 
 
-def take_back_body(returned, pick_table, values, grads, result, rows):
+def take_back_body(returned, pick_table, record, grads, result, rows, values, done):
+    load = pltpu.make_async_copy(record, values, done.at[0])
+    load.start()
     unpack_slots(returned, rows)
     grad_norm = dot(pick_table[...], rows[...].astype(jnp.bfloat16))
+    load.wait()
     value = values[...]
     result[...] = (
         grads[...].astype(jnp.float32) + norm_back(value, rms_scale(value), grad_norm)
     ).astype(jnp.bfloat16)
 
 
-def turn_back_body(returned, pick_table, values, grads, gate, table, result, target, rows):
-    take_back_body(returned, pick_table, values, grads, result, rows)
+def turn_back_body(
+    returned, pick_table, record, grads, gate, table, result, target, rows, values, done
+):
+    take_back_body(returned, pick_table, record, grads, result, rows, values, done)
     send_back_body(result, gate, table, target, rows)
 
 
-def serve_body(received, gate_mat, up_mat, down_mat, served, kept, gate_pre, up_pre, rows):
+def serve_body(
+    flag,
+    received,
+    gate_mat,
+    up_mat,
+    down_mat,
+    old_kept,
+    old_pre,
+    served,
+    kept_record,
+    pre_record,
+    rows,
+    kept,
+    pre,
+    done,
+):
     unpack_slots(received, rows)
     kept[...] = rows[...].astype(jnp.bfloat16)
-    gate_pre[...] = dot(kept[...], gate_mat[...])
-    up_pre[...] = dot(kept[...], up_mat[...])
-    gate = gate_pre[...]
-    hidden = (gate * jax.nn.sigmoid(gate) * up_pre[...]).astype(jnp.bfloat16)
+    first = [pltpu.make_async_copy(kept, kept_record, done.at[0])]
+    keep(flag, first, True)
+    pre[0] = dot(kept[...], gate_mat[...])
+    pre[1] = dot(kept[...], up_mat[...])
+    second = [pltpu.make_async_copy(pre, pre_record, done.at[1])]
+    keep(flag, second, True)
+    gate = pre[0]
+    hidden = (gate * jax.nn.sigmoid(gate) * pre[1]).astype(jnp.bfloat16)
     rows[...] = dot(hidden, down_mat[...])
     pack_slots(rows, served)
-
-
-def serve_back_rows(received, gate_pre, up_pre, down_mat, slot_grads, narrow, rows):
+    keep(flag, first + second, False)
+
+
+def serve_back_rows(received, load, pre, down_mat, slot_grads, narrow, rows, begin):
+    load.start()
     unpack_slots(received, rows)
     slot_grads[...] = rows[...].astype(jnp.bfloat16)
-    gate = gate_pre[...]
-    up = up_pre[...]
+    begin()
+    grad_hidden = dot_t(slot_grads[...], down_mat[...])
+    load.wait()
+    gate = pre[0]
+    up = pre[1]
     gate_sig = jax.nn.sigmoid(gate)
     gate_act = gate * gate_sig
-    grad_hidden = dot_t(slot_grads[...], down_mat[...])
     grad_gate = (grad_hidden * up * (gate_sig * (1.0 + gate * (1.0 - gate_sig)))).astype(
         jnp.bfloat16
     )
@@ -146,13 +206,38 @@
 
 
 def serve_back_body(
-    received, gate_pre, up_pre, gate_mat, up_mat, down_mat, target, slot_grads, narrow, rows
+    flag,
+    received,
+    pre_record,
+    gate_mat,
+    up_mat,
+    down_mat,
+    old_grads,
+    old_narrow,
+    target,
+    grads_record,
+    narrow_record,
+    rows,
+    pre,
+    slot_grads,
+    narrow,
+    done,
 ):
+    load = pltpu.make_async_copy(pre_record, pre, done.at[0])
+    first = [pltpu.make_async_copy(slot_grads, grads_record, done.at[1])]
     grad_gate, grad_up = serve_back_rows(
-        received, gate_pre, up_pre, down_mat, slot_grads, narrow, rows
-    )
+        received, load, pre, down_mat, slot_grads, narrow, rows, lambda: keep(flag, first, True)
+    )
+    second = [pltpu.make_async_copy(narrow, narrow_record, done.at[2])]
+    keep(flag, second, True)
     rows[...] = dot_t(grad_gate, gate_mat[...]) + dot_t(grad_up, up_mat[...])
     pack_slots(rows, target)
+    keep(flag, first + second, False)
+
+
+def serve_last_body(received, pre_record, down_mat, slot_grads, narrow, rows, pre, done):
+    load = pltpu.make_async_copy(pre_record, pre, done.at[0])
+    serve_back_rows(received, load, pre, down_mat, slot_grads, narrow, rows, lambda: None)
 
 
 def lowrank_body(
@@ -244,32 +329,43 @@
     )
 
 
-def take(returned, route, values):
+def take(flag, returned, route, values, record):
     table, pick_table, gate = route
-    width = values.shape[1]
     return run_kernel(
         take_body,
-        array(values.shape),
-        work_rows(table.shape[0], width),
+        (array(values.shape), array(record.shape)),
+        work_rows(table.shape[0], values.shape[1]) + [pltpu.SemaphoreType.DMA((1,))],
+        flag,
         returned,
         pick_table,
         values,
         gate,
-    )
-
-
-def turn(returned, route, values, next_table):
+        record,
+        far=(5,),
+        far_out=(1,),
+        scalars=(0,),
+        aliases={5: 1},
+    )
+
+
+def turn(flag, returned, route, values, record, next_table):
     table, pick_table, gate = route
     width = values.shape[1]
     return run_kernel(
         turn_body,
-        (array(values.shape), packed_shape(next_table, width)),
-        work_rows(table.shape[0], width),
+        (array(values.shape), array(record.shape), packed_shape(next_table, width)),
+        work_rows(table.shape[0], width) + [pltpu.SemaphoreType.DMA((1,))],
+        flag,
         returned,
         pick_table,
         values,
         gate,
+        record,
         next_table,
+        far=(5,),
+        far_out=(1,),
+        scalars=(0,),
+        aliases={5: 1},
     )
 
 
@@ -286,78 +382,103 @@
     )
 
 
+def load_rows(slots, values):
+    return work_rows(slots, values.shape[1]) + [
+        pltpu.VMEM(values.shape, jnp.bfloat16),
+        pltpu.SemaphoreType.DMA((1,)),
+    ]
+
+
 def take_back(returned, route, values, grads):
     table, pick_table, _ = route
-    width = values.shape[1]
     return run_kernel(
         take_back_body,
         array(values.shape),
-        work_rows(table.shape[0], width),
+        load_rows(table.shape[0], values),
         returned,
         pick_table,
         values,
         grads,
+        far=(2,),
     )
 
 
 def turn_back(returned, route, values, grads, next_route):
     table, pick_table, _ = route
-    width = values.shape[1]
     return run_kernel(
         turn_back_body,
-        (array(values.shape), packed_shape(next_route[0], width)),
-        work_rows(table.shape[0], width),
+        (array(values.shape), packed_shape(next_route[0], values.shape[1])),
+        load_rows(table.shape[0], values),
         returned,
         pick_table,
         values,
         grads,
         next_route[2],
         next_route[0],
-    )
-
-
-def serve(received, mats):
-    count, depth, width = received.shape
-    slots, inner = (count * depth, mats[0].shape[1])
+        far=(2,),
+    )
+
+
+def serve(flag, received, mats, kept, pre):
+    slots, width = kept.shape
     return run_kernel(
         serve_body,
-        (
-            array(received.shape),
-            array((slots, width)),
-            array((slots, inner), jnp.float32),
-            array((slots, inner), jnp.float32),
-        ),
-        work_rows(slots, width),
+        (array(received.shape), array(kept.shape), array(pre.shape, jnp.float32)),
+        work_rows(slots, width)
+        + [
+            pltpu.VMEM(kept.shape, jnp.bfloat16),
+            pltpu.VMEM(pre.shape, jnp.float32),
+            pltpu.SemaphoreType.DMA((2,)),
+        ],
+        flag,
         received,
         *mats,
-    )
-
-
-def serve_back(received, gate_pre, up_pre, mats):
-    count, depth, width = received.shape
-    slots, inner = gate_pre.shape
+        kept,
+        pre,
+        far=(5, 6),
+        far_out=(1, 2),
+        scalars=(0,),
+        aliases={5: 1, 6: 2},
+    )
+
+
+def serve_back(flag, received, pre, mats, grads, narrow):
+    slots, width = grads.shape
     return run_kernel(
         serve_back_body,
-        (array(received.shape), array((slots, width)), array((slots, 3 * inner))),
-        work_rows(slots, width),
+        (array(received.shape), array(grads.shape), array(narrow.shape)),
+        work_rows(slots, width)
+        + [
+            pltpu.VMEM(pre.shape, jnp.float32),
+            pltpu.VMEM(grads.shape, jnp.bfloat16),
+            pltpu.VMEM(narrow.shape, jnp.bfloat16),
+            pltpu.SemaphoreType.DMA((3,)),
+        ],
+        flag,
         received,
-        gate_pre,
-        up_pre,
+        pre,
         *mats,
-    )
-
-
-def serve_last(received, gate_pre, up_pre, down_mat):
-    count, depth, width = received.shape
-    slots, inner = gate_pre.shape
-    return run_kernel(
-        lambda *refs: serve_back_rows(*refs) and None,
+        grads,
+        narrow,
+        far=(2, 6, 7),
+        far_out=(1, 2),
+        scalars=(0,),
+        aliases={6: 1, 7: 2},
+    )
+
+
+def serve_last(received, pre, down_mat):
+    width = received.shape[2]
+    _, slots, inner = pre.shape
+    return run_kernel(
+        serve_last_body,
         (array((slots, width)), array((slots, 3 * inner))),
-        work_rows(slots, width),
+        work_rows(slots, width)
+        + [pltpu.VMEM(pre.shape, jnp.float32), pltpu.SemaphoreType.DMA((1,))],
         received,
-        gate_pre,
-        up_pre,
+        pre,
         down_mat,
+        far=(1,),
     )
 
 
@@ -398,9 +519,9 @@
         return jnp.concatenate(parts, axis=0)
 
     own = (gate_weight[0, 0], up_weight[0, 0], down_weight[0, 0])
-    other = (swap(own[0]), swap(own[1]))
+    gate_other = swap(own[0])
+    up_back = lax.ppermute(own[1], "section", to_even)
     down_back = lax.ppermute(own[2], "section", to_even)
-    mats_odd = tuple(jnp.where(is_even, b, a) for a, b in zip(own, other + (down_back,)))
 
     ids = routes[0, :, :, 0]
     plan = jnp.concatenate([ids.astype(jnp.float32), route_gates[0]], axis=0)
@@ -431,38 +552,81 @@
     )
     routing = [route_odd if layer % 2 else route_even for layer in range(section_count)]
 
+    slot_count = expert_count * capacity
+
+    def blank(*shape, dtype=jnp.bfloat16):
+        return jnp.zeros(shape, dtype)
+
+    flags = [(pair == layer // 2).astype(jnp.int32)[None] for layer in range(section_count)]
+    always = jnp.ones((1,), jnp.int32)
     first_rows = features.reshape(-1, width)
-    served, kept_all, gate_all, up_all = serve(exchange(send(first_rows, route_all[0])), own)
-    second_rows = take(exchange(served), route_all, first_rows)
+    served, kept_all, pre_all = serve(
+        always,
+        exchange(send(first_rows, route_all[0])),
+        own,
+        blank(micro_count * slot_count, width),
+        blank(2, micro_count * slot_count, inner, dtype=jnp.float32),
+    )
+    second_rows, _ = take(
+        always, exchange(served), route_all, first_rows, blank(*first_rows.shape)
+    )
     crossing = lax.ppermute(second_rows[row_count:], "section", to_odd)
     rows = jnp.where(is_even, second_rows[:row_count], crossing)
-    rows, late = lax.optimization_barrier((rows, own[2]))
-    down_on = lax.ppermute(late, "section", to_odd)
-    mats_even = tuple(jnp.where(is_even, a, b) for a, b in zip(own, other + (down_on,)))
-    mats = [mats_odd if layer % 2 else mats_even for layer in range(section_count)]
-
-    layer_rows = {}
-    layer_kept = {}
     sending = send(rows, routing[1][0])
+    sending, gate_other, up_back, down_back, *late = lax.optimization_barrier(
+        (sending, gate_other, up_back, down_back, *own)
+    )
+    back = (gate_other, up_back, down_back)
+    mats_odd = tuple(jnp.where(is_even, b, a) for a, b in zip(own, back))
+    up_on = lax.ppermute(late[1], "section", to_odd)
+    down_on = lax.ppermute(late[2], "section", to_odd)
+
+    row_record = [blank(row_count, width) for _ in range(2)]
+    kept_record = [blank(slot_count, width) for _ in range(2)]
+    pre_record = [blank(2, slot_count, inner, dtype=jnp.float32) for _ in range(2)]
     for layer in range(1, section_count):
-        layer_rows[layer] = rows
-        served, *layer_kept[layer] = serve(exchange(sending), mats[layer])
+        side = layer % 2
+        if layer == 2:
+            up_on, down_on, sending = lax.optimization_barrier((up_on, down_on, sending))
+            on = (gate_other, up_on, down_on)
+            mats_even = tuple(jnp.where(is_even, a, b) for a, b in zip(own, on))
+        served, kept_record[side], pre_record[side] = serve(
+            flags[layer],
+            exchange(sending),
+            mats_odd if side else mats_even,
+            kept_record[side],
+            pre_record[side],
+        )
         returned = exchange(served)
-        if layer % 2 == 0:
-            rows, sending = turn(returned, routing[layer], rows, routing[layer + 1][0])
+        if side == 0:
+            rows, row_record[side], sending = turn(
+                flags[layer],
+                returned,
+                routing[layer],
+                rows,
+                row_record[side],
+                routing[layer + 1][0],
+            )
             if layer == 2:
                 low_own = jnp.stack([lowrank_in[0], lowrank_out[0].T])
                 low_own, rows = lax.optimization_barrier((low_own, rows))
                 low_mats = lax.all_gather(low_own, "section")
         else:
-            rows = take(returned, routing[layer], rows)
+            rows, row_record[side] = take(
+                flags[layer], returned, routing[layer], rows, row_record[side]
+            )
             if layer < section_count - 1:
                 rows = hop(rows, layer)
                 sending = send(rows, routing[layer + 1][0])
+    mats = [mats_odd if layer % 2 else mats_even for layer in range(section_count)]
 
     targets = jnp.where(is_even, labels[0], labels[1]).astype(jnp.float32)[:, None]
     grads, low_normed, low_act, low_pre, low_grads = lowrank_layers(
         rows, low_mats, targets, head_weight[None, :]
+    )
+    sending = send_back(grads, routing[section_count - 1])
+    sending, low_normed, low_act, low_pre, low_grads = lax.optimization_barrier(
+        (sending, low_normed, low_act, low_pre, low_grads)
     )
 
     def low_part(wide, narrow):
@@ -485,26 +649,24 @@
     last_pair = section_count // 2 - 1
     parts = jnp.where(pair == last_pair, parts, jnp.zeros_like(parts))
 
-    saved = {0: None, 1: None}
-    sending = send_back(grads, routing[section_count - 1])
+    grads_record = [blank(slot_count, width) for _ in range(2)]
+    narrow_record = [blank(slot_count, 3 * inner) for _ in range(2)]
     for layer in reversed(range(1, section_count)):
-        kept, gate_pre, up_pre = layer_kept[layer]
-        target, slot_grads, narrow = serve_back(exchange(sending), gate_pre, up_pre, mats[layer])
+        side = layer % 2
+        target, grads_record[side], narrow_record[side] = serve_back(
+            flags[layer],
+            exchange(sending),
+            pre_record[side],
+            mats[layer],
+            grads_record[side],
+            narrow_record[side],
+        )
         returned = exchange(target)
-        values = layer_rows[layer]
-        if layer % 2 == 1 and layer > 1:
+        values = row_record[side]
+        if side == 1 and layer > 1:
             grads, sending = turn_back(returned, routing[layer], values, grads, routing[layer - 1])
         else:
             grads = take_back(returned, routing[layer], values, grads)
-        record = (kept, slot_grads, narrow)
-        past = saved[layer % 2]
-        saved[layer % 2] = (
-            record
-            if past is None
-            else tuple(
-                jnp.where(pair == layer // 2, new, old) for new, old in zip(record, past)
-            )
-        )
         if layer == 6:
             parts, grads = lax.optimization_barrier((parts, grads))
             share = lax.psum_scatter(
@@ -518,10 +680,11 @@
             sending = send_back(grads, routing[layer - 1])
 
     all_grads = jnp.concatenate([grads, lax.ppermute(grads, "section", to_even)], axis=0)
-    theirs = tuple(swap(jnp.where(is_even, b, a)) for a, b in zip(saved[0], saved[1]))
-    held = tuple(jnp.where(is_even, a, b) for a, b in zip(saved[0], saved[1]))
+    saved = tuple(zip(kept_record, grads_record, narrow_record))
+    theirs = tuple(swap(jnp.where(is_even, b, a)) for a, b in zip(*saved))
+    held = tuple(jnp.where(is_even, a, b) for a, b in zip(*saved))
     joint = (kept_all,) + tuple(
-        serve_last(exchange(send_back(all_grads, route_all)), gate_all, up_all, own[2])
+        serve_last(exchange(send_back(all_grads, route_all)), pre_all, own[2])
     )
     kept, slot_grads, narrow = (
         jnp.where(section == 0, both, jnp.concatenate([mine, other], axis=0))

time: 832 us -> 857 us (1.030)
  waiting for transfers between devices: 219 us -> 263 us
  blocking collectives: 267 us -> 252 us
  local copies, waits for them, and re-layouts: 64.9 us -> 54.6 us
    ppermute x12, waiting for transfers between devices: 71.1 us -> 93.5 us  [hop(): lax.ppermute(part, 'section', links)]
    unnamed x293 -> x177, local copies, waits for them, and re-layouts: 59.6 us -> 40 us
    all_to_all x17 -> x16, blocking collectives: 267 us -> 252 us  [exchange(): lax.all_to_all(buffer, 'expert', split_axis=0, concat_axis=0, tiled=True)]
    ppermute x1, waiting for transfers between devices: 0.01 us -> 14.3 us  [local(): down_back = lax.ppermute(own[2], 'section', to_even)]
    all_to_all x14 -> x15, waiting for transfers between devices: 129 us -> 143 us  [exchange(): lax.all_to_all(buffer, 'expert', split_axis=0, concat_axis=0, tiled=True)]
    all_to_all x14 -> x15, starting transfers between devices: 78.1 us -> 84 us  [exchange(): lax.all_to_all(buffer, 'expert', split_axis=0, concat_axis=0, tiled=True)]
  transfers between devices with their start and end apart: 39 -> 41, of which waited for: 30 -> 31; matrix products, arithmetic and copies ran while one was open for 7% -> 6% of each run, Pallas kernels for 4% -> 4%
where the time goes in v3:
time: 857 us; the launch traced here: 844 us
  waiting for transfers between devices  263 us (31%)
  blocking collectives  252 us (29%)
  starting transfers between devices  128 us (15%)
  Pallas kernels  68.6 us (8%)
  local copies, waits for them, and re-layouts  54.6 us (6%)
  other arithmetic  33.3 us (4%)
  matrix products  29.7 us (3%)
  between operations  15.8 us (2%)
    all_to_all x16, blocking collectives, exchange(): lax.all_to_all(buffer, 'expert', split_axis=0, concat_axis=0, tiled=True)  252 us
    all_to_all x15, waiting for transfers between devices, exchange(): lax.all_to_all(buffer, 'expert', split_axis=0, concat_axis=0, tiled=True)  143 us
    ppermute x12, waiting for transfers between devices, hop(): lax.ppermute(part, 'section', links)  93.5 us
    all_to_all x15, starting transfers between devices, exchange(): lax.all_to_all(buffer, 'expert', split_axis=0, concat_axis=0, tiled=True)  84 us
    pallas_call x42, Pallas kernels, run_kernel(): pl.pallas_call(body, out_shape=jax.tree.unflatten(treedef, leaves), in_sp...  68.6 us
    unnamed x177, local copies, waits for them, and re-layouts  40 us
    dot_general x19, matrix products, dot_tn(): lax.dot_general(left, right, (((0,), (0,)), ((), ())), preferred_element_...  29.7 us
    ppermute x12, starting transfers between devices, hop(): lax.ppermute(part, 'section', links)  22.1 us
  transfers between devices with their start and end apart: 41, of which 31 were waited for; matrix products, arithmetic and copies ran while one was open for 6% of the time, Pallas kernels for 4%

profile of v3, /device:TPU:1, one launch (start us, length us, event | category | flops | bytes accessed | tf_op | source)
XLA Modules:
  0.0 844.2 jit_solution(9339342736602905403)
XLA Ops:
  47.9 17.1 %all-to-all-done.1.returned = bf16[32,6,2048]{2,1,0:T(8,128)(2,1)S(1)} async-done(((bf16[32,6,2048]{2,1,0:T(8,128)(2,1)}), bf16[32,6,2048]{2,1,0:T(8,128)(2,1)S(1)}, u32[]{:S(2)}, u32[]{:S(2)}) %all-to-all-start.1) | async-done | bytes 786464 | tf_op jit(solution)/shard_map/all_to_all | solution.py:313
  77.1 14.3 %collective-permute-done.4 = bf16[256,2048]{1,0:T(8,128)(2,1)} collective-permute-done((bf16[256,2048]{1,0:T(8,128)(2,1)}, bf16[256,2048]{1,0:T(8,128)(2,1)}, u32[]{:S(2)}, u32[]{:S(2)}) %collective-permute-start.4) | collective-permute-done | bytes 1048608 | tf_op jit(solution)/shard_map/ppermute | solution.py:524
  137.7 32.1 %collective-permute-done.7 = bf16[32,2048]{1,0:T(8,128)(2,1)S(1)} collective-permute-done((bf16[32,2048]{1,0:T(8,128)(2,1)S(1)}, bf16[32,2048]{1,0:T(8,128)(2,1)S(1)}, u32[]{:S(2)}, u32[]{:S(2)}) %collective-permute-start.7) | collective-permute-done | bytes 131104 | tf_op jit(solution)/shard_map/ppermute | solution.py:518
  206.8 11.6 %all-to-all-done.5.returned = bf16[32,3,2048]{2,1,0:T(4,128)(2,1)} async-done(((bf16[32,3,2048]{2,1,0:T(4,128)(2,1)}), bf16[32,3,2048]{2,1,0:T(4,128)(2,1)}, u32[]{:S(2)}, u32[]{:S(2)}) %all-to-all-start.5) | async-done | bytes 393248 | tf_op jit(solution)/shard_map/all_to_all | solution.py:313
  222.5 15.7 %all_to_all.160.received = bf16[32,3,2048]{2,1,0:T(4,128)(2,1)S(1)} all-to-all(bf16[32,3,2048]{2,1,0:T(4,128)(2,1)} %copy-done.49), channel_id=1, replica_groups=mesh['section'=8,'expert'=32] {'expert'}, dimensions={0} | all-to-all | bytes 786432 | tf_op jit(solution)/shard_map/all_to_all | solution.py:313
  239.1 15.2 %all_to_all.161.returned = bf16[32,3,2048]{2,1,0:T(4,128)(2,1)S(1)} all-to-all(bf16[32,3,2048]{2,1,0:T(4,128)(2,1)S(1)} %get-tuple-element.119), channel_id=1, replica_groups=mesh['section'=8,'expert'=32] {'expert'}, dimensions={0} | all-to-all | bytes 786432 | tf_op jit(solution)/shard_map/all_to_all | solution.py:313
  284.7 11.7 %all-to-all-done.8.received = bf16[32,3,2048]{2,1,0:T(4,128)(2,1)} async-done(((bf16[32,3,2048]{2,1,0:T(4,128)(2,1)}), bf16[32,3,2048]{2,1,0:T(4,128)(2,1)}, u32[]{:S(2)}, u32[]{:S(2)}) %all-to-all-start.8) | async-done | bytes 393248 | tf_op jit(solution)/shard_map/all_to_all | solution.py:313
  302.1 15.2 %all_to_all.162.returned = bf16[32,3,2048]{2,1,0:T(4,128)(2,1)S(1)} all-to-all(bf16[32,3,2048]{2,1,0:T(4,128)(2,1)S(1)} %get-tuple-element.126), channel_id=1, replica_groups=mesh['section'=8,'expert'=32] {'expert'}, dimensions={0} | all-to-all | bytes 786432 | tf_op jit(solution)/shard_map/all_to_all | solution.py:313
  318.2 15.2 %all_to_all.163.received = bf16[32,3,2048]{2,1,0:T(4,128)(2,1)S(1)} all-to-all(bf16[32,3,2048]{2,1,0:T(4,128)(2,1)S(1)} %get-tuple-element.128), channel_id=1, replica_groups=mesh['section'=8,'expert'=32] {'expert'}, dimensions={0} | all-to-all | bytes 786432 | tf_op jit(solution)/shard_map/all_to_all | solution.py:313
  334.3 15.2 %all_to_all.164.returned = bf16[32,3,2048]{2,1,0:T(4,128)(2,1)S(1)} all-to-all(bf16[32,3,2048]{2,1,0:T(4,128)(2,1)S(1)} %get-tuple-element.131), channel_id=1, replica_groups=mesh['section'=8,'expert'=32] {'expert'}, dimensions={0} | all-to-all | bytes 786432 | tf_op jit(solution)/shard_map/all_to_all | solution.py:313
  370.9 11.7 %all-to-all-done.12.received = bf16[32,3,2048]{2,1,0:T(4,128)(2,1)} async-done(((bf16[32,3,2048]{2,1,0:T(4,128)(2,1)}), bf16[32,3,2048]{2,1,0:T(4,128)(2,1)}, u32[]{:S(2)}, u32[]{:S(2)}) %all-to-all-start.12) | async-done | bytes 393248 | tf_op jit(solution)/shard_map/all_to_all | solution.py:313
  388.2 15.6 %all_to_all.165.returned = bf16[32,3,2048]{2,1,0:T(4,128)(2,1)S(1)} all-to-all(bf16[32,3,2048]{2,1,0:T(4,128)(2,1)S(1)} %get-tuple-element.138), channel_id=1, replica_groups=mesh['section'=8,'expert'=32] {'expert'}, dimensions={0} | all-to-all | bytes 786432 | tf_op jit(solution)/shard_map/all_to_all | solution.py:313
  404.7 15.2 %all_to_all.166.received = bf16[32,3,2048]{2,1,0:T(4,128)(2,1)S(1)} all-to-all(bf16[32,3,2048]{2,1,0:T(4,128)(2,1)S(1)} %get-tuple-element.140), channel_id=1, replica_groups=mesh['section'=8,'expert'=32] {'expert'}, dimensions={0} | all-to-all | bytes 786432 | tf_op jit(solution)/shard_map/all_to_all | solution.py:313
  577.7 15.0 %all_to_all.167.received = bf16[32,3,2048]{2,1,0:T(4,128)(2,1)S(1)} all-to-all(bf16[32,3,2048]{2,1,0:T(4,128)(2,1)S(1)} %shard_map.164), channel_id=1, replica_groups=mesh['section'=8,'expert'=32] {'expert'}, dimensions={0} | all-to-all | bytes 786432 | tf_op jit(solution)/shard_map/all_to_all | solution.py:313
  594.9 15.5 %all_to_all.168.returned = bf16[32,3,2048]{2,1,0:T(4,128)(2,1)S(1)} all-to-all(bf16[32,3,2048]{2,1,0:T(4,128)(2,1)S(1)} %get-tuple-element.171), channel_id=1, replica_groups=mesh['section'=8,'expert'=32] {'expert'}, dimensions={0} | all-to-all | bytes 786432 | tf_op jit(solution)/shard_map/all_to_all | solution.py:313
  611.4 19.6 %all_to_all.169.received = bf16[32,3,2048]{2,1,0:T(4,128)(2,1)S(1)} all-to-all(bf16[32,3,2048]{2,1,0:T(4,128)(2,1)S(1)} %get-tuple-element.172), channel_id=1, replica_groups=mesh['section'=8,'expert'=32] {'expert'}, dimensions={0} | all-to-all | bytes 786432 | tf_op jit(solution)/shard_map/all_to_all | solution.py:313
  633.2 16.6 %all_to_all.170.returned = bf16[32,3,2048]{2,1,0:T(4,128)(2,1)S(1)} all-to-all(bf16[32,3,2048]{2,1,0:T(4,128)(2,1)S(1)} %get-tuple-element.175), channel_id=1, replica_groups=mesh['section'=8,'expert'=32] {'expert'}, dimensions={0} | all-to-all | bytes 786432 | tf_op jit(solution)/shard_map/all_to_all | solution.py:313
  662.4 16.6 %all_to_all.171.received = bf16[32,3,2048]{2,1,0:T(4,128)(2,1)S(1)} all-to-all(bf16[32,3,2048]{2,1,0:T(4,128)(2,1)S(1)} %shard_map.169), channel_id=1, replica_groups=mesh['section'=8,'expert'=32] {'expert'}, dimensions={0} | all-to-all | bytes 786432 | tf_op jit(solution)/shard_map/all_to_all | solution.py:313
  681.2 15.2 %all_to_all.172.returned = bf16[32,3,2048]{2,1,0:T(4,128)(2,1)S(1)} all-to-all(bf16[32,3,2048]{2,1,0:T(4,128)(2,1)S(1)} %get-tuple-element.179), channel_id=1, replica_groups=mesh['section'=8,'expert'=32] {'expert'}, dimensions={0} | all-to-all | bytes 786432 | tf_op jit(solution)/shard_map/all_to_all | solution.py:313
  697.4 15.2 %all_to_all.173.received = bf16[32,3,2048]{2,1,0:T(4,128)(2,1)S(1)} all-to-all(bf16[32,3,2048]{2,1,0:T(4,128)(2,1)S(1)} %get-tuple-element.180), channel_id=1, replica_groups=mesh['section'=8,'expert'=32] {'expert'}, dimensions={0} | all-to-all | bytes 786432 | tf_op jit(solution)/shard_map/all_to_all | solution.py:313
  714.8 15.2 %all_to_all.174.returned = bf16[32,3,2048]{2,1,0:T(4,128)(2,1)S(1)} all-to-all(bf16[32,3,2048]{2,1,0:T(4,128)(2,1)S(1)} %get-tuple-element.183), channel_id=1, replica_groups=mesh['section'=8,'expert'=32] {'expert'}, dimensions={0} | all-to-all | bytes 786432 | tf_op jit(solution)/shard_map/all_to_all | solution.py:313
  749.6 15.3 %all_to_all.175.received = bf16[32,3,2048]{2,1,0:T(4,128)(2,1)S(1)} all-to-all(bf16[32,3,2048]{2,1,0:T(4,128)(2,1)S(1)} %shard_map.174), channel_id=1, replica_groups=mesh['section'=8,'expert'=32] {'expert'}, dimensions={0} | all-to-all | bytes 786432 | tf_op jit(solution)/shard_map/all_to_all | solution.py:313
  772.0 11.7 %all-to-all-done.29.returned = bf16[32,3,2048]{2,1,0:T(4,128)(2,1)S(1)} async-done(((bf16[32,3,2048]{2,1,0:T(4,128)(2,1)}), bf16[32,3,2048]{2,1,0:T(4,128)(2,1)S(1)}, u32[]{:S(2)}, u32[]{:S(2)}) %all-to-all-start.29) | async-done | bytes 393248 | tf_op jit(solution)/shard_map/all_to_all | solution.py:313
  812.2 13.6 %all-to-all-done.30.received = bf16[32,6,2048]{2,1,0:T(8,128)(2,1)S(1)} async-done(((bf16[32,6,2048]{2,1,0:T(8,128)(2,1)}), bf16[32,6,2048]{2,1,0:T(8,128)(2,1)S(1)}, u32[]{:S(2)}, u32[]{:S(2)}) %all-to-all-start.30) | async-done | bytes 786464 | tf_op jit(solution)/shard_map/all_to_all | solution.py:313
  (394 shorter events, 453.1 us)
Async XLA Ops:
  11.5 25.8 %all-to-all-start = ((bf16[32,6,2048]{2,1,0:T(8,128)(2,1)}), bf16[32,6,2048]{2,1,0:T(8,128)(2,1)S(1)}, u32[]{:S(2)}, u32[]{:S(2)}) async-start(bf16[32,6,2048]{2,1,0:T(8,128)(2,1)} %shard_map.137), calls=%async_computation | async-start | bytes 2097152 | tf_op jit(solution)/shard_map/all_to_all | solution.py:313
  21.9 55.1 %collective-permute-start.2 = (bf16[2048,256]{1,0:T(8,128)(2,1)}, bf16[2048,256]{1,0:T(8,128)(2,1)}, u32[]{:S(2)}, u32[]{:S(2)}) collective-permute-start(bf16[2048,256]{1,0:T(8,128)(2,1)} %bitcast.3.gate_mat), channel_id=1, source_target_pairs={{0,32},{64,96},{128,160},{192,224},{32,0},{96,64},{160,128},{224,1... | collective-permute-start | bytes 3145736 | tf_op jit(solution)/shard_map/ppermute | solution.py:508
  22.0 55.0 %collective-permute-start.3 = (bf16[2048,256]{1,0:T(8,128)(2,1)}, bf16[2048,256]{1,0:T(8,128)(2,1)}, u32[]{:S(2)}, u32[]{:S(2)}) collective-permute-start(bf16[2048,256]{1,0:T(8,128)(2,1)} %bitcast.4.up_mat), channel_id=1, source_target_pairs={{32,0},{96,64},{160,128},{224,192},{33,1},{97,65},{161,129},{225,1... | collective-permute-start | bytes 3145736 | tf_op jit(solution)/shard_map/ppermute | solution.py:523
  23.3 68.1 %collective-permute-start.4 = (bf16[256,2048]{1,0:T(8,128)(2,1)}, bf16[256,2048]{1,0:T(8,128)(2,1)}, u32[]{:S(2)}, u32[]{:S(2)}) collective-permute-start(bf16[256,2048]{1,0:T(8,128)(2,1)} %bitcast.5.down_mat), channel_id=1, source_target_pairs={{32,0},{96,64},{160,128},{224,192},{33,1},{97,65},{161,129},{225,1... | collective-permute-start | bytes 3145736 | tf_op jit(solution)/shard_map/ppermute | solution.py:524
  43.5 21.4 %all-to-all-start.1 = ((bf16[32,6,2048]{2,1,0:T(8,128)(2,1)}), bf16[32,6,2048]{2,1,0:T(8,128)(2,1)S(1)}, u32[]{:S(2)}, u32[]{:S(2)}) async-start(bf16[32,6,2048]{2,1,0:T(8,128)(2,1)} %copy-done.37), calls=%async_computation.1 | async-start | bytes 2097152 | tf_op jit(solution)/shard_map/all_to_all | solution.py:313
  91.4 20.1 %all-to-all-start.2 = ((bf16[32,3,2048]{2,1,0:T(4,128)(2,1)}), bf16[32,3,2048]{2,1,0:T(4,128)(2,1)}, u32[]{:S(2)}, u32[]{:S(2)}) async-start(bf16[32,3,2048]{2,1,0:T(4,128)(2,1)} %shard_map.140), calls=%async_computation.2 | async-start | bytes 1048576 | tf_op jit(solution)/shard_map/all_to_all | solution.py:313
  120.8 53.2 %collective-permute-start.5 = (bf16[2048,256]{1,0:T(8,128)(2,1)}, bf16[2048,256]{1,0:T(8,128)(2,1)}, u32[]{:S(2)}, u32[]{:S(2)}) collective-permute-start(bf16[2048,256]{1,0:T(8,128)(2,1)} %bitcast.4.up_mat), channel_id=1, source_target_pairs={{0,32},{64,96},{128,160},{192,224},{1,33},{65,97},{129,161},{193,2... | collective-permute-start | bytes 3145736 | tf_op jit(solution)/shard_map/ppermute | solution.py:581
  123.1 50.9 %collective-permute-start.6 = (bf16[256,2048]{1,0:T(8,128)(2,1)}, bf16[256,2048]{1,0:T(8,128)(2,1)}, u32[]{:S(2)}, u32[]{:S(2)}) collective-permute-start(bf16[256,2048]{1,0:T(8,128)(2,1)} %bitcast.5.down_mat), channel_id=1, source_target_pairs={{0,32},{64,96},{128,160},{192,224},{1,33},{65,97},{129,161},{193,2... | collective-permute-start | bytes 3145736 | tf_op jit(solution)/shard_map/ppermute | solution.py:582
  135.2 34.6 %collective-permute-start.7 = (bf16[32,2048]{1,0:T(8,128)(2,1)S(1)}, bf16[32,2048]{1,0:T(8,128)(2,1)S(1)}, u32[]{:S(2)}, u32[]{:S(2)}) collective-permute-start(bf16[32,2048]{1,0:T(8,128)(2,1)S(1)} %get-tuple-element.216), channel_id=1, source_target_pairs={{0,64},{64,0},{32,96},{96,32},{128,192},{192,128},{160,224},{224,1... | collective-permute-start | bytes 393224 | tf_op jit(solution)/shard_map/ppermute | solution.py:518
  137.4 35.2 %collective-permute-start.8 = (bf16[32,2048]{1,0:T(8,128)(2,1)S(1)}, bf16[32,2048]{1,0:T(8,128)(2,1)S(1)}, u32[]{:S(2)}, u32[]{:S(2)}) collective-permute-start(bf16[32,2048]{1,0:T(8,128)(2,1)S(1)} %get-tuple-element.215), channel_id=1, source_target_pairs={{0,64},{64,0},{32,96},{96,32},{128,192},{192,128},{160,224},{224,1... | collective-permute-start | bytes 393224 | tf_op jit(solution)/shard_map/ppermute | solution.py:518
  173.9 19.9 %all-to-all-start.4 = ((bf16[32,3,2048]{2,1,0:T(4,128)(2,1)}), bf16[32,3,2048]{2,1,0:T(4,128)(2,1)}, u32[]{:S(2)}, u32[]{:S(2)}) async-start(bf16[32,3,2048]{2,1,0:T(4,128)(2,1)} %copy-done.30), calls=%async_computation.4 | async-start | bytes 1048576 | tf_op jit(solution)/shard_map/all_to_all | solution.py:313
  201.8 16.6 %all-to-all-start.5 = ((bf16[32,3,2048]{2,1,0:T(4,128)(2,1)}), bf16[32,3,2048]{2,1,0:T(4,128)(2,1)}, u32[]{:S(2)}, u32[]{:S(2)}) async-start(bf16[32,3,2048]{2,1,0:T(4,128)(2,1)} %copy-done.44), calls=%async_computation.5 | async-start | bytes 1048576 | tf_op jit(solution)/shard_map/all_to_all | solution.py:313
  206.6 233.8 %all-gather.3.cloned.1.call-start = ((), (), s32[]{:S(2)}) async-start(), calls=%async_computation.34 | async-start | bytes 9437184 | tf_op jit(solution)/shard_map/all_gather | solution.py:613
  254.8 17.0 %collective-permute-start.9 = (bf16[32,2048]{1,0:T(8,128)(2,1)S(1)}, bf16[32,2048]{1,0:T(8,128)(2,1)S(1)}, u32[]{:S(2)}, u32[]{:S(2)}) collective-permute-start(bf16[32,2048]{1,0:T(8,128)(2,1)S(1)} %get-tuple-element.214), channel_id=1, source_target_pairs={{64,128},{128,64},{96,160},{160,96},{192,0},{0,192},{224,32},{32,2... | collective-permute-start | bytes 393224 | tf_op jit(solution)/shard_map/ppermute | solution.py:518
  261.6 16.7 %collective-permute-start.10 = (bf16[32,2048]{1,0:T(8,128)(2,1)S(1)}, bf16[32,2048]{1,0:T(8,128)(2,1)S(1)}, u32[]{:S(2)}, u32[]{:S(2)}) collective-permute-start(bf16[32,2048]{1,0:T(8,128)(2,1)S(1)} %get-tuple-element.213), channel_id=1, source_target_pairs={{64,128},{128,64},{96,160},{160,96},{192,0},{0,192},{224,32},{32,2... | collective-permute-start | bytes 393224 | tf_op jit(solution)/shard_map/ppermute | solution.py:518
  279.6 16.8 %all-to-all-start.8 = ((bf16[32,3,2048]{2,1,0:T(4,128)(2,1)}), bf16[32,3,2048]{2,1,0:T(4,128)(2,1)}, u32[]{:S(2)}, u32[]{:S(2)}) async-start(bf16[32,3,2048]{2,1,0:T(4,128)(2,1)} %copy-done.31), calls=%async_computation.8 | async-start | bytes 1048576 | tf_op jit(solution)/shard_map/all_to_all | solution.py:313
  366.1 16.5 %all-to-all-start.12 = ((bf16[32,3,2048]{2,1,0:T(4,128)(2,1)}), bf16[32,3,2048]{2,1,0:T(4,128)(2,1)}, u32[]{:S(2)}, u32[]{:S(2)}) async-start(bf16[32,3,2048]{2,1,0:T(4,128)(2,1)} %copy-done.32), calls=%async_computation.12 | async-start | bytes 1048576 | tf_op jit(solution)/shard_map/all_to_all | solution.py:313
  493.5 18.5 %all-to-all-start.17 = ((bf16[32,3,2048]{2,1,0:T(4,128)(2,1)}), bf16[32,3,2048]{2,1,0:T(4,128)(2,1)}, u32[]{:S(2)}, u32[]{:S(2)}) async-start(bf16[32,3,2048]{2,1,0:T(4,128)(2,1)} %copy-done.45), calls=%async_computation.17 | async-start | bytes 1048576 | tf_op jit(solution)/shard_map/all_to_all | solution.py:313
  516.5 16.4 %all-to-all-start.18 = ((bf16[32,3,2048]{2,1,0:T(4,128)(2,1)}), bf16[32,3,2048]{2,1,0:T(4,128)(2,1)}, u32[]{:S(2)}, u32[]{:S(2)}) async-start(bf16[32,3,2048]{2,1,0:T(4,128)(2,1)} %copy-done.47), calls=%async_computation.18 | async-start | bytes 1048576 | tf_op jit(solution)/shard_map/all_to_all | solution.py:313
  547.6 183.8 %reduce-scatter.2.cloned.1.call-start = ((), (), s32[]{:S(2)}) async-start(), calls=%async_computation.33 | async-start | bytes 8650752 | tf_op jit(solution)/shard_map/reduce_scatter | solution.py:672
  791.7 36.4 %collective-permute-start.13 = (bf16[96,2048]{1,0:T(8,128)(2,1)}, bf16[96,2048]{1,0:T(8,128)(2,1)}, u32[]{:S(2)}, u32[]{:S(2)}) collective-permute-start(bf16[96,2048]{1,0:T(8,128)(2,1)} %get-tuple-element.202), channel_id=1, source_target_pairs={{0,32},{64,96},{128,160},{192,224},{32,0},{96,64},{160,128},{224,1... | collective-permute-start | bytes 1179656 | tf_op jit(solution)/shard_map/ppermute | solution.py:508
  802.9 22.9 %all-to-all-start.30 = ((bf16[32,6,2048]{2,1,0:T(8,128)(2,1)}), bf16[32,6,2048]{2,1,0:T(8,128)(2,1)S(1)}, u32[]{:S(2)}, u32[]{:S(2)}) async-start(bf16[32,6,2048]{2,1,0:T(8,128)(2,1)} %shard_map.177), calls=%async_computation.31 | async-start | bytes 2097152 | tf_op jit(solution)/shard_map/all_to_all | solution.py:313
  809.8 18.2 %collective-permute-start.21 = (bf16[96,768]{1,0:T(8,128)(2,1)}, bf16[96,768]{1,0:T(8,128)(2,1)S(1)}, u32[]{:S(2)}, u32[]{:S(2)}) collective-permute-start(bf16[96,768]{1,0:T(8,128)(2,1)} %get-tuple-element.204), channel_id=1, source_target_pairs={{0,32},{64,96},{128,160},{192,224},{32,0},{96,64},{160,128},{224,1... | collective-permute-start | bytes 442376 | tf_op jit(solution)/shard_map/ppermute | solution.py:508
  810.7 23.4 %collective-permute-start.22 = (bf16[96,2048]{1,0:T(8,128)(2,1)}, bf16[96,2048]{1,0:T(8,128)(2,1)}, u32[]{:S(2)}, u32[]{:S(2)}) collective-permute-start(bf16[96,2048]{1,0:T(8,128)(2,1)} %get-tuple-element.200), channel_id=1, source_target_pairs={{0,32},{64,96},{128,160},{192,224},{32,0},{96,64},{160,128},{224,1... | collective-permute-start | bytes 1179656 | tf_op jit(solution)/shard_map/ppermute | solution.py:508
  (102 other events, 900.4 us)
Sparse Core Ops, SparseCore 0:
  222.7 104.2 all-gather.2
  563.8 99.9 reduce-scatter.1

commit v4 on v3

--- a/solution.py
+++ b/solution.py
@@ -47,7 +47,24 @@
     return (grid[:, None] == slots[None, :]).astype(jnp.bfloat16)
 
 
-def run_kernel(body, out_shape, scratch, *operands, far=(), far_out=(), scalars=(), aliases={}):
+def run_kernel(
+    body, out_shape, scratch, *operands, far=(), far_out=(), scalars=(), aliases={}, limit=16
+):
+    absent = [k for k, operand in enumerate(operands) if operand is None]
+    if absent:
+        count, inner_body = (len(operands), body)
+        operands = [operand for operand in operands if operand is not None]
+        shift = {
+            k: k - sum(gone < k for gone in absent) for k in range(count) if k not in absent
+        }
+        far, scalars = (tuple(shift[k] for k in group if k in shift) for group in (far, scalars))
+        aliases = {shift[k]: out for k, out in aliases.items() if k in shift}
+
+        def body(*refs):
+            refs = iter(refs)
+            given = [None if k in absent else next(refs) for k in range(count)]
+            inner_body(*given, *refs)
+
     everywhere = pl.BlockSpec(memory_space=pltpu.HBM)
     near = pl.BlockSpec(memory_space=pltpu.VMEM)
     small = pl.BlockSpec(memory_space=pltpu.SMEM)
@@ -67,7 +84,7 @@
         out_specs=jax.tree.unflatten(treedef, out_specs),
         scratch_shapes=scratch,
         input_output_aliases=aliases,
-        compiler_params=pltpu.CompilerParams(vmem_limit_bytes=40 * 1024 * 1024),
+        compiler_params=pltpu.CompilerParams(vmem_limit_bytes=limit * 1024 * 1024),
     )(*operands)
 
 
@@ -241,9 +258,10 @@
 
 
 def lowrank_body(
-    rows, mats, targets, head, grads, all_normed, all_act, all_pre, all_grads, values, inner, scale
+    flag, rows, mats, targets, head, grads, all_normed, all_act, all_pre, all_grads, values, inner, scale
 ):
     count = mats.shape[0]
+    live = flag[0].astype(jnp.float32)
     values[0] = rows[...]
 
     def forward(step, carry):
@@ -254,7 +272,7 @@
         inner_pre = dot(normed, mats[index, 0])
         act = (inner_pre * jax.nn.sigmoid(inner_pre)).astype(jnp.bfloat16)
         all_normed[index] = normed
-        all_act[index] = act
+        all_act[index] = (act.astype(jnp.float32) * live).astype(jnp.bfloat16)
         inner[index] = inner_pre
         scale[index] = row_scale
         values[step + 1] = (
@@ -279,7 +297,7 @@
             jnp.bfloat16
         )
         grad_norm = dot_t(grad_pre, mats[index, 0])
-        all_pre[index] = grad_pre
+        all_pre[index] = (grad_pre.astype(jnp.float32) * live).astype(jnp.bfloat16)
         all_grads[index] = grad
         grads[...] = (
             grad.astype(jnp.float32) + norm_back(value, scale[index], grad_norm)
@@ -289,7 +307,7 @@
     lax.fori_loop(0, count, backward, 0)
 
 
-def lowrank_layers(rows, mats, targets, head):
+def lowrank_layers(flag, rows, mats, targets, head):
     count, rank = (mats.shape[0], mats.shape[3])
     row_count, width = rows.shape
     wide = array((count, row_count, width))
@@ -302,11 +320,42 @@
             pltpu.VMEM((count, row_count, rank), jnp.float32),
             pltpu.VMEM((count, row_count, 1), jnp.float32),
         ],
+        flag,
         rows,
         mats,
         targets,
         head,
-    )
+        scalars=(0,),
+        limit=40,
+    )
+
+
+def parts_body(normed, pre, grads, act, parts):
+    blocks, _, _, depth, rank = parts.shape
+    for kind, (wide, narrow) in enumerate(((normed, pre), (grads, act))):
+        part = dot_tn(wide[0], narrow[0]).astype(jnp.bfloat16)
+        parts[:, 0, kind] = part.reshape(blocks, depth, rank)
+
+
+def lowrank_sums(normed, pre, grads, act, blocks):
+    count, row_count, width = normed.shape
+    rank = pre.shape[2]
+    wide = pl.BlockSpec((1, row_count, width), lambda k: (k, 0, 0))
+    narrow = pl.BlockSpec((1, row_count, rank), lambda k: (k, 0, 0))
+    depth = width // blocks
+    return pl.pallas_call(
+        parts_body,
+        grid=(count,),
+        out_shape=array((blocks, count, 2, depth, rank)),
+        in_specs=[wide, narrow, wide, narrow],
+        out_specs=pl.BlockSpec((blocks, 1, 2, depth, rank), lambda k: (0, k, 0, 0, 0)),
+        compiler_params=pltpu.CompilerParams(vmem_limit_bytes=16 * 1024 * 1024),
+        cost_estimate=pl.CostEstimate(
+            flops=4 * count * row_count * width * rank,
+            bytes_accessed=4 * count * width * (row_count + rank),
+            transcendentals=0,
+        ),
+    )(normed, pre, grads, act)
 
 
 def exchange(buffer):
@@ -333,7 +382,7 @@
     table, pick_table, gate = route
     return run_kernel(
         take_body,
-        (array(values.shape), array(record.shape)),
+        (array(values.shape), array(values.shape)),
         work_rows(table.shape[0], values.shape[1]) + [pltpu.SemaphoreType.DMA((1,))],
         flag,
         returned,
@@ -353,7 +402,7 @@
     width = values.shape[1]
     return run_kernel(
         turn_body,
-        (array(values.shape), array(record.shape), packed_shape(next_table, width)),
+        (array(values.shape), array(values.shape), packed_shape(next_table, width)),
         work_rows(table.shape[0], width) + [pltpu.SemaphoreType.DMA((1,))],
         flag,
         returned,
@@ -420,14 +469,15 @@
 
 
 def serve(flag, received, mats, kept, pre):
-    slots, width = kept.shape
+    count, depth, width = received.shape
+    slots, inner = (count * depth, mats[0].shape[1])
     return run_kernel(
         serve_body,
-        (array(received.shape), array(kept.shape), array(pre.shape, jnp.float32)),
+        (array(received.shape), array((slots, width)), array((2, slots, inner), jnp.float32)),
         work_rows(slots, width)
         + [
-            pltpu.VMEM(kept.shape, jnp.bfloat16),
-            pltpu.VMEM(pre.shape, jnp.float32),
+            pltpu.VMEM((slots, width), jnp.bfloat16),
+            pltpu.VMEM((2, slots, inner), jnp.float32),
             pltpu.SemaphoreType.DMA((2,)),
         ],
         flag,
@@ -443,15 +493,16 @@
 
 
 def serve_back(flag, received, pre, mats, grads, narrow):
-    slots, width = grads.shape
+    width = received.shape[2]
+    _, slots, inner = pre.shape
     return run_kernel(
         serve_back_body,
-        (array(received.shape), array(grads.shape), array(narrow.shape)),
+        (array(received.shape), array((slots, width)), array((slots, 3 * inner))),
         work_rows(slots, width)
         + [
             pltpu.VMEM(pre.shape, jnp.float32),
-            pltpu.VMEM(grads.shape, jnp.bfloat16),
-            pltpu.VMEM(narrow.shape, jnp.bfloat16),
+            pltpu.VMEM((slots, width), jnp.bfloat16),
+            pltpu.VMEM((slots, 3 * inner), jnp.bfloat16),
             pltpu.SemaphoreType.DMA((3,)),
         ],
         flag,
@@ -519,9 +570,7 @@
         return jnp.concatenate(parts, axis=0)
 
     own = (gate_weight[0, 0], up_weight[0, 0], down_weight[0, 0])
-    gate_other = swap(own[0])
-    up_back = lax.ppermute(own[1], "section", to_even)
-    down_back = lax.ppermute(own[2], "section", to_even)
+    gate_other, up_other = (swap(own[0]), swap(own[1]))
 
     ids = routes[0, :, :, 0]
     plan = jnp.concatenate([ids.astype(jnp.float32), route_gates[0]], axis=0)
@@ -552,44 +601,29 @@
     )
     routing = [route_odd if layer % 2 else route_even for layer in range(section_count)]
 
-    slot_count = expert_count * capacity
-
-    def blank(*shape, dtype=jnp.bfloat16):
-        return jnp.zeros(shape, dtype)
-
     flags = [(pair == layer // 2).astype(jnp.int32)[None] for layer in range(section_count)]
     always = jnp.ones((1,), jnp.int32)
     first_rows = features.reshape(-1, width)
     served, kept_all, pre_all = serve(
-        always,
-        exchange(send(first_rows, route_all[0])),
-        own,
-        blank(micro_count * slot_count, width),
-        blank(2, micro_count * slot_count, inner, dtype=jnp.float32),
-    )
-    second_rows, _ = take(
-        always, exchange(served), route_all, first_rows, blank(*first_rows.shape)
-    )
+        always, exchange(send(first_rows, route_all[0])), own, None, None
+    )
+    second_rows, _ = take(always, exchange(served), route_all, first_rows, None)
+    second_rows, late = lax.optimization_barrier((second_rows, own[2]))
     crossing = lax.ppermute(second_rows[row_count:], "section", to_odd)
+    down_back = lax.ppermute(late, "section", to_even)
     rows = jnp.where(is_even, second_rows[:row_count], crossing)
+    rows, late = lax.optimization_barrier((rows, own[2]))
+    down_on = lax.ppermute(late, "section", to_odd)
     sending = send(rows, routing[1][0])
-    sending, gate_other, up_back, down_back, *late = lax.optimization_barrier(
-        (sending, gate_other, up_back, down_back, *own)
-    )
-    back = (gate_other, up_back, down_back)
-    mats_odd = tuple(jnp.where(is_even, b, a) for a, b in zip(own, back))
-    up_on = lax.ppermute(late[1], "section", to_odd)
-    down_on = lax.ppermute(late[2], "section", to_odd)
-
-    row_record = [blank(row_count, width) for _ in range(2)]
-    kept_record = [blank(slot_count, width) for _ in range(2)]
-    pre_record = [blank(2, slot_count, inner, dtype=jnp.float32) for _ in range(2)]
+    sending, gate_other, up_other = lax.optimization_barrier((sending, gate_other, up_other))
+    others = (gate_other, up_other)
+    mats_odd = tuple(jnp.where(is_even, b, a) for a, b in zip(own, others + (down_back,)))
+
+    row_record = [None, None]
+    kept_record = [None, None]
+    pre_record = [None, None]
     for layer in range(1, section_count):
         side = layer % 2
-        if layer == 2:
-            up_on, down_on, sending = lax.optimization_barrier((up_on, down_on, sending))
-            on = (gate_other, up_on, down_on)
-            mats_even = tuple(jnp.where(is_even, a, b) for a, b in zip(own, on))
         served, kept_record[side], pre_record[side] = serve(
             flags[layer],
             exchange(sending),
@@ -597,6 +631,9 @@
             kept_record[side],
             pre_record[side],
         )
+        if layer == 1:
+            served, down_on = lax.optimization_barrier((served, down_on))
+            mats_even = tuple(jnp.where(is_even, a, b) for a, b in zip(own, others + (down_on,)))
         returned = exchange(served)
         if side == 0:
             rows, row_record[side], sending = turn(
@@ -622,35 +659,18 @@
 
     targets = jnp.where(is_even, labels[0], labels[1]).astype(jnp.float32)[:, None]
     grads, low_normed, low_act, low_pre, low_grads = lowrank_layers(
-        rows, low_mats, targets, head_weight[None, :]
+        flags[-1], rows, low_mats, targets, head_weight[None, :]
     )
     sending = send_back(grads, routing[section_count - 1])
     sending, low_normed, low_act, low_pre, low_grads = lax.optimization_barrier(
         (sending, low_normed, low_act, low_pre, low_grads)
     )
 
-    def low_part(wide, narrow):
-        part = dot_tn(wide, narrow).astype(jnp.bfloat16)
-        return part.reshape(expert_count, 1, -1, part.shape[1])
-
-    parts = jnp.stack(
-        [
-            jnp.concatenate(
-                [
-                    low_part(low_normed[index], low_pre[index]),
-                    low_part(low_grads[index], low_act[index]),
-                ],
-                axis=1,
-            )
-            for index in range(section_count)
-        ],
-        axis=1,
-    )
+    parts = lowrank_sums(low_normed, low_pre, low_grads, low_act, expert_count)
     last_pair = section_count // 2 - 1
-    parts = jnp.where(pair == last_pair, parts, jnp.zeros_like(parts))
-
-    grads_record = [blank(slot_count, width) for _ in range(2)]
-    narrow_record = [blank(slot_count, 3 * inner) for _ in range(2)]
+
+    grads_record = [None, None]
+    narrow_record = [None, None]
     for layer in reversed(range(1, section_count)):
         side = layer % 2
         target, grads_record[side], narrow_record[side] = serve_back(
@@ -667,8 +687,8 @@
             grads, sending = turn_back(returned, routing[layer], values, grads, routing[layer - 1])
         else:
             grads = take_back(returned, routing[layer], values, grads)
-        if layer == 6:
-            parts, grads = lax.optimization_barrier((parts, grads))
+        if layer == section_count - 1:
+            parts, sending = lax.optimization_barrier((parts, sending))
             share = lax.psum_scatter(
                 parts.reshape(-1, parts.shape[-1]), "expert", scatter_dimension=0, tiled=True
             ).reshape(parts.shape[1:])

time: 857 us -> 798 us (0.931)
  blocking collectives: 252 us -> 301 us
  waiting for transfers between devices: 263 us -> 216 us
  matrix products: 29.7 us -> 8.97 us
  other arithmetic: 33.3 us -> 14.5 us
  starting transfers between devices: 128 us -> 110 us
    all_to_all x16 -> x19, blocking collectives: 252 us -> 301 us  [exchange(): lax.all_to_all(buffer, 'expert', split_axis=0, concat_axis=0, tiled=True)]
    all_to_all x15 -> x12, waiting for transfers between devices: 143 us -> 121 us  [exchange(): lax.all_to_all(buffer, 'expert', split_axis=0, concat_axis=0, tiled=True)]
    ppermute x12, waiting for transfers between devices: 93.5 us -> 72.5 us  [hop(): lax.ppermute(part, 'section', links)]
    dot_general x19 -> x3, matrix products: 29.7 us -> 8.97 us  [dot_tn(): lax.dot_general(left, right, (((0,), (0,)), ((), ())), preferred_element_...]
    all_to_all x15 -> x12, starting transfers between devices: 84 us -> 67.8 us  [exchange(): lax.all_to_all(buffer, 'expert', split_axis=0, concat_axis=0, tiled=True)]
    unnamed x7 -> x0, other arithmetic: 11.2 us -> none
    unnamed x177 -> x165, local copies, waits for them, and re-layouts: 40 us -> 47.4 us
  transfers between devices with their start and end apart: 41 -> 37, of which waited for: 31 -> 27; matrix products, arithmetic and copies ran while one was open for 6% -> 3% of each run, Pallas kernels for 4% -> 5%
where the time goes in v4:
time: 798 us; the launch traced here: 786 us
  blocking collectives  301 us (38%)
  waiting for transfers between devices  216 us (27%)
  starting transfers between devices  110 us (14%)
  Pallas kernels  68.1 us (9%)
  local copies, waits for them, and re-layouts  51 us (6%)
  between operations  15.7 us (2%)
  other arithmetic  14.5 us (2%)
  matrix products  8.97 us (1%)
    all_to_all x19, blocking collectives, exchange(): lax.all_to_all(buffer, 'expert', split_axis=0, concat_axis=0, tiled=True)  301 us
    all_to_all x12, waiting for transfers between devices, exchange(): lax.all_to_all(buffer, 'expert', split_axis=0, concat_axis=0, tiled=True)  121 us
    ppermute x12, waiting for transfers between devices, hop(): lax.ppermute(part, 'section', links)  72.5 us
    all_to_all x12, starting transfers between devices, exchange(): lax.all_to_all(buffer, 'expert', split_axis=0, concat_axis=0, tiled=True)  67.8 us
    pallas_call x42, Pallas kernels, run_kernel(): pl.pallas_call(body, out_shape=jax.tree.unflatten(treedef, leaves), in_sp...  63.8 us
    unnamed x165, local copies, waits for them, and re-layouts  47.4 us
    ppermute x12, starting transfers between devices, hop(): lax.ppermute(part, 'section', links)  19.4 us
  transfers between devices with their start and end apart: 37, of which 27 were waited for; matrix products, arithmetic and copies ran while one was open for 3% of the time, Pallas kernels for 5%

profile of v4, /device:TPU:1, one launch (start us, length us, event | category | flops | bytes accessed | tf_op | source)
XLA Modules:
  0.0 786.2 jit_solution(11701938165366086965)
XLA Ops:
  25.2 12.1 %all-to-all-done.refs_1_ = bf16[32,6,2048]{2,1,0:T(8,128)(2,1)S(1)} async-done(((bf16[32,6,2048]{2,1,0:T(8,128)(2,1)}), bf16[32,6,2048]{2,1,0:T(8,128)(2,1)S(1)}, u32[]{:S(2)}, u32[]{:S(2)}) %all-to-all-start) | async-done | bytes 786464 | tf_op jit(solution)/shard_map/all_to_all | solution.py:362
  47.0 17.1 %all-to-all-done.1.refs_1_ = bf16[32,6,2048]{2,1,0:T(8,128)(2,1)S(1)} async-done(((bf16[32,6,2048]{2,1,0:T(8,128)(2,1)}), bf16[32,6,2048]{2,1,0:T(8,128)(2,1)S(1)}, u32[]{:S(2)}, u32[]{:S(2)}) %all-to-all-start.1) | async-done | bytes 786464 | tf_op jit(solution)/shard_map/all_to_all | solution.py:362
  190.0 15.7 %all_to_all.160.received = bf16[32,3,2048]{2,1,0:T(4,128)(2,1)S(1)} all-to-all(bf16[32,3,2048]{2,1,0:T(4,128)(2,1)} %copy-done.49), channel_id=1, replica_groups=mesh['section'=8,'expert'=32] {'expert'}, dimensions={0} | all-to-all | bytes 786432 | tf_op jit(solution)/shard_map/all_to_all | solution.py:362
  206.6 15.2 %all_to_all.161.returned = bf16[32,3,2048]{2,1,0:T(4,128)(2,1)S(1)} all-to-all(bf16[32,3,2048]{2,1,0:T(4,128)(2,1)S(1)} %get-tuple-element.119), channel_id=1, replica_groups=mesh['section'=8,'expert'=32] {'expert'}, dimensions={0} | all-to-all | bytes 786432 | tf_op jit(solution)/shard_map/all_to_all | solution.py:362
  249.4 11.7 %all-to-all-done.8.received = bf16[32,3,2048]{2,1,0:T(4,128)(2,1)} async-done(((bf16[32,3,2048]{2,1,0:T(4,128)(2,1)}), bf16[32,3,2048]{2,1,0:T(4,128)(2,1)}, u32[]{:S(2)}, u32[]{:S(2)}) %all-to-all-start.8) | async-done | bytes 393248 | tf_op jit(solution)/shard_map/all_to_all | solution.py:362
  266.8 15.2 %all_to_all.162.returned = bf16[32,3,2048]{2,1,0:T(4,128)(2,1)S(1)} all-to-all(bf16[32,3,2048]{2,1,0:T(4,128)(2,1)S(1)} %get-tuple-element.126), channel_id=1, replica_groups=mesh['section'=8,'expert'=32] {'expert'}, dimensions={0} | all-to-all | bytes 786432 | tf_op jit(solution)/shard_map/all_to_all | solution.py:362
  282.9 15.2 %all_to_all.163.received = bf16[32,3,2048]{2,1,0:T(4,128)(2,1)S(1)} all-to-all(bf16[32,3,2048]{2,1,0:T(4,128)(2,1)S(1)} %get-tuple-element.128), channel_id=1, replica_groups=mesh['section'=8,'expert'=32] {'expert'}, dimensions={0} | all-to-all | bytes 786432 | tf_op jit(solution)/shard_map/all_to_all | solution.py:362
  299.0 15.2 %all_to_all.164.returned = bf16[32,3,2048]{2,1,0:T(4,128)(2,1)S(1)} all-to-all(bf16[32,3,2048]{2,1,0:T(4,128)(2,1)S(1)} %get-tuple-element.131), channel_id=1, replica_groups=mesh['section'=8,'expert'=32] {'expert'}, dimensions={0} | all-to-all | bytes 786432 | tf_op jit(solution)/shard_map/all_to_all | solution.py:362
  336.8 11.7 %all-to-all-done.12.received = bf16[32,3,2048]{2,1,0:T(4,128)(2,1)} async-done(((bf16[32,3,2048]{2,1,0:T(4,128)(2,1)}), bf16[32,3,2048]{2,1,0:T(4,128)(2,1)}, u32[]{:S(2)}, u32[]{:S(2)}) %all-to-all-start.12) | async-done | bytes 393248 | tf_op jit(solution)/shard_map/all_to_all | solution.py:362
  354.2 15.4 %all_to_all.165.returned = bf16[32,3,2048]{2,1,0:T(4,128)(2,1)S(1)} all-to-all(bf16[32,3,2048]{2,1,0:T(4,128)(2,1)S(1)} %get-tuple-element.138), channel_id=1, replica_groups=mesh['section'=8,'expert'=32] {'expert'}, dimensions={0} | all-to-all | bytes 786432 | tf_op jit(solution)/shard_map/all_to_all | solution.py:362
  370.5 15.2 %all_to_all.166.received = bf16[32,3,2048]{2,1,0:T(4,128)(2,1)S(1)} all-to-all(bf16[32,3,2048]{2,1,0:T(4,128)(2,1)S(1)} %get-tuple-element.140), channel_id=1, replica_groups=mesh['section'=8,'expert'=32] {'expert'}, dimensions={0} | all-to-all | bytes 786432 | tf_op jit(solution)/shard_map/all_to_all | solution.py:362
  421.9 15.2 %all_to_all.167.refs_1_ = bf16[32,3,2048]{2,1,0:T(4,128)(2,1)S(1)} all-to-all(bf16[32,3,2048]{2,1,0:T(4,128)(2,1)S(1)} %shard_map.159), channel_id=1, replica_groups=mesh['section'=8,'expert'=32] {'expert'}, dimensions={0} | all-to-all | bytes 786432 | tf_op jit(solution)/shard_map/all_to_all | solution.py:362
  462.1 19.1 %all_to_all.168.refs_1_ = bf16[32,3,2048]{2,1,0:T(4,128)(2,1)S(1)} all-to-all(bf16[32,3,2048]{2,1,0:T(4,128)(2,1)} %copy-done.48), channel_id=1, replica_groups=mesh['section'=8,'expert'=32] {'expert'}, dimensions={0} | all-to-all | bytes 786432 | tf_op jit(solution)/shard_map/all_to_all | solution.py:362
  488.1 15.2 %all_to_all.169.returned = bf16[32,3,2048]{2,1,0:T(4,128)(2,1)S(1)} all-to-all(bf16[32,3,2048]{2,1,0:T(4,128)(2,1)S(1)} %get-tuple-element.166), channel_id=1, replica_groups=mesh['section'=8,'expert'=32] {'expert'}, dimensions={0} | all-to-all | bytes 786432 | tf_op jit(solution)/shard_map/all_to_all | solution.py:362
  518.3 19.7 %all_to_all.170.received = bf16[32,3,2048]{2,1,0:T(4,128)(2,1)S(1)} all-to-all(bf16[32,3,2048]{2,1,0:T(4,128)(2,1)S(1)} %shard_map.165), channel_id=1, replica_groups=mesh['section'=8,'expert'=32] {'expert'}, dimensions={0} | all-to-all | bytes 786432 | tf_op jit(solution)/shard_map/all_to_all | solution.py:362
  540.1 16.7 %all_to_all.171.returned = bf16[32,3,2048]{2,1,0:T(4,128)(2,1)S(1)} all-to-all(bf16[32,3,2048]{2,1,0:T(4,128)(2,1)S(1)} %get-tuple-element.171), channel_id=1, replica_groups=mesh['section'=8,'expert'=32] {'expert'}, dimensions={0} | all-to-all | bytes 786432 | tf_op jit(solution)/shard_map/all_to_all | solution.py:362
  557.9 15.8 %all_to_all.172.received = bf16[32,3,2048]{2,1,0:T(4,128)(2,1)S(1)} all-to-all(bf16[32,3,2048]{2,1,0:T(4,128)(2,1)S(1)} %get-tuple-element.172), channel_id=1, replica_groups=mesh['section'=8,'expert'=32] {'expert'}, dimensions={0} | all-to-all | bytes 786432 | tf_op jit(solution)/shard_map/all_to_all | solution.py:362
  575.8 15.4 %all_to_all.173.returned = bf16[32,3,2048]{2,1,0:T(4,128)(2,1)S(1)} all-to-all(bf16[32,3,2048]{2,1,0:T(4,128)(2,1)S(1)} %get-tuple-element.175), channel_id=1, replica_groups=mesh['section'=8,'expert'=32] {'expert'}, dimensions={0} | all-to-all | bytes 786432 | tf_op jit(solution)/shard_map/all_to_all | solution.py:362
  605.4 16.0 %all_to_all.174.received = bf16[32,3,2048]{2,1,0:T(4,128)(2,1)S(1)} all-to-all(bf16[32,3,2048]{2,1,0:T(4,128)(2,1)S(1)} %shard_map.170), channel_id=1, replica_groups=mesh['section'=8,'expert'=32] {'expert'}, dimensions={0} | all-to-all | bytes 786432 | tf_op jit(solution)/shard_map/all_to_all | solution.py:362
  623.6 15.4 %all_to_all.175.returned = bf16[32,3,2048]{2,1,0:T(4,128)(2,1)S(1)} all-to-all(bf16[32,3,2048]{2,1,0:T(4,128)(2,1)S(1)} %get-tuple-element.179), channel_id=1, replica_groups=mesh['section'=8,'expert'=32] {'expert'}, dimensions={0} | all-to-all | bytes 786432 | tf_op jit(solution)/shard_map/all_to_all | solution.py:362
  639.9 15.2 %all_to_all.176.received = bf16[32,3,2048]{2,1,0:T(4,128)(2,1)S(1)} all-to-all(bf16[32,3,2048]{2,1,0:T(4,128)(2,1)S(1)} %get-tuple-element.180), channel_id=1, replica_groups=mesh['section'=8,'expert'=32] {'expert'}, dimensions={0} | all-to-all | bytes 786432 | tf_op jit(solution)/shard_map/all_to_all | solution.py:362
  657.3 15.2 %all_to_all.177.returned = bf16[32,3,2048]{2,1,0:T(4,128)(2,1)S(1)} all-to-all(bf16[32,3,2048]{2,1,0:T(4,128)(2,1)S(1)} %get-tuple-element.183), channel_id=1, replica_groups=mesh['section'=8,'expert'=32] {'expert'}, dimensions={0} | all-to-all | bytes 786432 | tf_op jit(solution)/shard_map/all_to_all | solution.py:362
  691.2 15.4 %all_to_all.178.received = bf16[32,3,2048]{2,1,0:T(4,128)(2,1)S(1)} all-to-all(bf16[32,3,2048]{2,1,0:T(4,128)(2,1)S(1)} %shard_map.175), channel_id=1, replica_groups=mesh['section'=8,'expert'=32] {'expert'}, dimensions={0} | all-to-all | bytes 786432 | tf_op jit(solution)/shard_map/all_to_all | solution.py:362
  754.3 13.5 %all-to-all-done.30.received = bf16[32,6,2048]{2,1,0:T(8,128)(2,1)S(1)} async-done(((bf16[32,6,2048]{2,1,0:T(8,128)(2,1)}), bf16[32,6,2048]{2,1,0:T(8,128)(2,1)S(1)}, u32[]{:S(2)}, u32[]{:S(2)}) %all-to-all-start.30) | async-done | bytes 786464 | tf_op jit(solution)/shard_map/all_to_all | solution.py:362
  (339 shorter events, 402.9 us)
Async XLA Ops:
  11.5 25.8 %all-to-all-start = ((bf16[32,6,2048]{2,1,0:T(8,128)(2,1)}), bf16[32,6,2048]{2,1,0:T(8,128)(2,1)S(1)}, u32[]{:S(2)}, u32[]{:S(2)}) async-start(bf16[32,6,2048]{2,1,0:T(8,128)(2,1)} %shard_map.137), calls=%async_computation | async-start | bytes 2097152 | tf_op jit(solution)/shard_map/all_to_all | solution.py:362
  21.9 53.4 %collective-permute-start.2 = (bf16[2048,256]{1,0:T(8,128)(2,1)}, bf16[2048,256]{1,0:T(8,128)(2,1)}, u32[]{:S(2)}, u32[]{:S(2)}) collective-permute-start(bf16[2048,256]{1,0:T(8,128)(2,1)} %bitcast.3.refs_2_), channel_id=1, source_target_pairs={{0,32},{64,96},{128,160},{192,224},{32,0},{96,64},{160,128},{224,1... | collective-permute-start | bytes 3145736 | tf_op jit(solution)/shard_map/ppermute | solution.py:559
  22.0 53.3 %collective-permute-start.3 = (bf16[2048,256]{1,0:T(8,128)(2,1)}, bf16[2048,256]{1,0:T(8,128)(2,1)}, u32[]{:S(2)}, u32[]{:S(2)}) collective-permute-start(bf16[2048,256]{1,0:T(8,128)(2,1)} %bitcast.4.refs_3_), channel_id=1, source_target_pairs={{0,32},{64,96},{128,160},{192,224},{32,0},{96,64},{160,128},{224,1... | collective-permute-start | bytes 3145736 | tf_op jit(solution)/shard_map/ppermute | solution.py:559
  42.6 21.4 %all-to-all-start.1 = ((bf16[32,6,2048]{2,1,0:T(8,128)(2,1)}), bf16[32,6,2048]{2,1,0:T(8,128)(2,1)S(1)}, u32[]{:S(2)}, u32[]{:S(2)}) async-start(bf16[32,6,2048]{2,1,0:T(8,128)(2,1)} %copy-done.39), calls=%async_computation.1 | async-start | bytes 2097152 | tf_op jit(solution)/shard_map/all_to_all | solution.py:362
  69.1 26.2 %collective-permute-start.4 = (bf16[256,2048]{1,0:T(8,128)(2,1)}, bf16[256,2048]{1,0:T(8,128)(2,1)}, u32[]{:S(2)}, u32[]{:S(2)}) collective-permute-start(bf16[256,2048]{1,0:T(8,128)(2,1)} %bitcast.72), channel_id=1, source_target_pairs={{32,0},{96,64},{160,128},{224,192},{33,1},{97,65},{161,129},{225,1... | collective-permute-start | bytes 3145736 | tf_op jit(solution)/shard_map/ppermute | solution.py:613
  75.3 21.4 %all-to-all-start.2 = ((bf16[32,3,2048]{2,1,0:T(4,128)(2,1)}), bf16[32,3,2048]{2,1,0:T(4,128)(2,1)}, u32[]{:S(2)}, u32[]{:S(2)}) async-start(bf16[32,3,2048]{2,1,0:T(4,128)(2,1)} %shard_map.140), calls=%async_computation.2 | async-start | bytes 1048576 | tf_op jit(solution)/shard_map/all_to_all | solution.py:362
  82.1 26.6 %collective-permute-start.5 = (bf16[256,2048]{1,0:T(8,128)(2,1)}, bf16[256,2048]{1,0:T(8,128)(2,1)}, u32[]{:S(2)}, u32[]{:S(2)}) collective-permute-start(bf16[256,2048]{1,0:T(8,128)(2,1)} %bitcast.73), channel_id=1, source_target_pairs={{0,32},{64,96},{128,160},{192,224},{1,33},{65,97},{129,161},{193,2... | collective-permute-start | bytes 3145736 | tf_op jit(solution)/shard_map/ppermute | solution.py:616
  108.8 19.8 %all-to-all-start.3 = ((bf16[32,3,2048]{2,1,0:T(4,128)(2,1)}), bf16[32,3,2048]{2,1,0:T(4,128)(2,1)}, u32[]{:S(2)}, u32[]{:S(2)}) async-start(bf16[32,3,2048]{2,1,0:T(4,128)(2,1)} %copy-done.46), calls=%async_computation.3 | async-start | bytes 1048576 | tf_op jit(solution)/shard_map/all_to_all | solution.py:362
  146.2 17.0 %all-to-all-start.4 = ((bf16[32,3,2048]{2,1,0:T(4,128)(2,1)}), bf16[32,3,2048]{2,1,0:T(4,128)(2,1)}, u32[]{:S(2)}, u32[]{:S(2)}) async-start(bf16[32,3,2048]{2,1,0:T(4,128)(2,1)} %copy-done.34), calls=%async_computation.4 | async-start | bytes 1048576 | tf_op jit(solution)/shard_map/all_to_all | solution.py:362
  169.7 16.8 %all-to-all-start.5 = ((bf16[32,3,2048]{2,1,0:T(4,128)(2,1)}), bf16[32,3,2048]{2,1,0:T(4,128)(2,1)}, u32[]{:S(2)}, u32[]{:S(2)}) async-start(bf16[32,3,2048]{2,1,0:T(4,128)(2,1)} %copy-done.44), calls=%async_computation.5 | async-start | bytes 1048576 | tf_op jit(solution)/shard_map/all_to_all | solution.py:362
  174.8 231.4 %all-gather.3.cloned.1.call-start = ((), (), s32[]{:S(2)}) async-start(), calls=%async_computation.34 | async-start | bytes 9437184 | tf_op jit(solution)/shard_map/all_gather | solution.py:650
  225.5 17.0 %collective-permute-start.9 = (bf16[32,2048]{1,0:T(8,128)(2,1)S(1)}, bf16[32,2048]{1,0:T(8,128)(2,1)S(1)}, u32[]{:S(2)}, u32[]{:S(2)}) collective-permute-start(bf16[32,2048]{1,0:T(8,128)(2,1)S(1)} %get-tuple-element.215), channel_id=1, source_target_pairs={{64,128},{128,64},{96,160},{160,96},{192,0},{0,192},{224,32},{32,2... | collective-permute-start | bytes 393224 | tf_op jit(solution)/shard_map/ppermute | solution.py:569
  243.9 17.2 %all-to-all-start.8 = ((bf16[32,3,2048]{2,1,0:T(4,128)(2,1)}), bf16[32,3,2048]{2,1,0:T(4,128)(2,1)}, u32[]{:S(2)}, u32[]{:S(2)}) async-start(bf16[32,3,2048]{2,1,0:T(4,128)(2,1)} %copy-done.33), calls=%async_computation.8 | async-start | bytes 1048576 | tf_op jit(solution)/shard_map/all_to_all | solution.py:362
  331.7 16.9 %all-to-all-start.12 = ((bf16[32,3,2048]{2,1,0:T(4,128)(2,1)}), bf16[32,3,2048]{2,1,0:T(4,128)(2,1)}, u32[]{:S(2)}, u32[]{:S(2)}) async-start(bf16[32,3,2048]{2,1,0:T(4,128)(2,1)} %copy-done.32), calls=%async_computation.12 | async-start | bytes 1048576 | tf_op jit(solution)/shard_map/all_to_all | solution.py:362
  387.4 16.4 %all-to-all-start.15 = ((bf16[32,3,2048]{2,1,0:T(4,128)(2,1)}), bf16[32,3,2048]{2,1,0:T(4,128)(2,1)}, u32[]{:S(2)}, u32[]{:S(2)}) async-start(bf16[32,3,2048]{2,1,0:T(4,128)(2,1)} %copy-done.47), calls=%async_computation.15 | async-start | bytes 1048576 | tf_op jit(solution)/shard_map/all_to_all | solution.py:362
  440.1 17.4 %all-to-all-start.17 = ((bf16[32,3,2048]{2,1,0:T(4,128)(2,1)}), bf16[32,3,2048]{2,1,0:T(4,128)(2,1)}, u32[]{:S(2)}, u32[]{:S(2)}) async-start(bf16[32,3,2048]{2,1,0:T(4,128)(2,1)} %copy-done.45), calls=%async_computation.17 | async-start | bytes 1048576 | tf_op jit(solution)/shard_map/all_to_all | solution.py:362
  444.8 229.1 %reduce-scatter.2.cloned.1.call-start = ((), (), s32[]{:S(2)}) async-start(), calls=%async_computation.33 | async-start | bytes 8650752 | tf_op jit(solution)/shard_map/reduce_scatter | solution.py:692
  504.1 13.7 %collective-permute-start.14 = (bf16[32,2048]{1,0:T(8,128)(2,1)S(1)}, bf16[32,2048]{1,0:T(8,128)(2,1)S(1)}, u32[]{:S(2)}, u32[]{:S(2)}) collective-permute-start(bf16[32,2048]{1,0:T(8,128)(2,1)S(1)} %get-tuple-element.211), channel_id=1, source_target_pairs={{0,64},{64,0},{32,96},{96,32},{128,192},{192,128},{160,224},{224,1... | collective-permute-start | bytes 393224 | tf_op jit(solution)/shard_map/ppermute | solution.py:569
  709.6 15.8 %all-to-all-start.29 = ((bf16[32,3,2048]{2,1,0:T(4,128)(2,1)}), bf16[32,3,2048]{2,1,0:T(4,128)(2,1)S(1)}, u32[]{:S(2)}, u32[]{:S(2)}) async-start(bf16[32,3,2048]{2,1,0:T(4,128)(2,1)} %copy-done.43), calls=%async_computation.30 | async-start | bytes 1048576 | tf_op jit(solution)/shard_map/all_to_all | solution.py:362
  725.3 15.4 %all-to-all-start.31 = ((bf16[8,2,64,128]{3,2,1,0:T(8,128)(2,1)}), bf16[8,2,64,128]{3,2,1,0:T(8,128)(2,1)S(1)}, u32[]{:S(2)}, u32[]{:S(2)}) async-start(bf16[8,2,64,128]{3,2,1,0:T(8,128)(2,1)} %bitcast.81), calls=%async_computation.32 | async-start | bytes 524288 | tf_op jit(solution)/shard_map/all_to_all | solution.py:697
  733.9 36.1 %collective-permute-start.12 = (bf16[96,2048]{1,0:T(8,128)(2,1)}, bf16[96,2048]{1,0:T(8,128)(2,1)}, u32[]{:S(2)}, u32[]{:S(2)}) collective-permute-start(bf16[96,2048]{1,0:T(8,128)(2,1)} %get-tuple-element.204), channel_id=1, source_target_pairs={{0,32},{64,96},{128,160},{192,224},{32,0},{96,64},{160,128},{224,1... | collective-permute-start | bytes 1179656 | tf_op jit(solution)/shard_map/ppermute | solution.py:559
  745.0 22.9 %all-to-all-start.30 = ((bf16[32,6,2048]{2,1,0:T(8,128)(2,1)}), bf16[32,6,2048]{2,1,0:T(8,128)(2,1)S(1)}, u32[]{:S(2)}, u32[]{:S(2)}) async-start(bf16[32,6,2048]{2,1,0:T(8,128)(2,1)} %shard_map.178), calls=%async_computation.31 | async-start | bytes 2097152 | tf_op jit(solution)/shard_map/all_to_all | solution.py:362
  751.9 17.9 %collective-permute-start.20 = (bf16[96,768]{1,0:T(8,128)(2,1)}, bf16[96,768]{1,0:T(8,128)(2,1)S(1)}, u32[]{:S(2)}, u32[]{:S(2)}) collective-permute-start(bf16[96,768]{1,0:T(8,128)(2,1)} %get-tuple-element.206), channel_id=1, source_target_pairs={{0,32},{64,96},{128,160},{192,224},{32,0},{96,64},{160,128},{224,1... | collective-permute-start | bytes 442376 | tf_op jit(solution)/shard_map/ppermute | solution.py:559
  752.9 23.3 %collective-permute-start.21 = (bf16[96,2048]{1,0:T(8,128)(2,1)}, bf16[96,2048]{1,0:T(8,128)(2,1)}, u32[]{:S(2)}, u32[]{:S(2)}) collective-permute-start(bf16[96,2048]{1,0:T(8,128)(2,1)} %get-tuple-element.202), channel_id=1, source_target_pairs={{0,32},{64,96},{128,160},{192,224},{32,0},{96,64},{160,128},{224,1... | collective-permute-start | bytes 1179656 | tf_op jit(solution)/shard_map/ppermute | solution.py:559
  (92 other events, 815.0 us)
Sparse Core Ops, SparseCore 0:
  190.1 103.5 all-gather.2
  462.2 104.0 reduce-scatter.1

commit v5 on v4

--- a/solution.py
+++ b/solution.py
@@ -184,20 +184,48 @@
     kept,
     pre,
     done,
+    ready=lambda index: None,
 ):
     unpack_slots(received, rows)
     kept[...] = rows[...].astype(jnp.bfloat16)
     first = [pltpu.make_async_copy(kept, kept_record, done.at[0])]
     keep(flag, first, True)
+    ready(0)
     pre[0] = dot(kept[...], gate_mat[...])
+    ready(1)
     pre[1] = dot(kept[...], up_mat[...])
     second = [pltpu.make_async_copy(pre, pre_record, done.at[1])]
     keep(flag, second, True)
     gate = pre[0]
     hidden = (gate * jax.nn.sigmoid(gate) * pre[1]).astype(jnp.bfloat16)
+    ready(2)
     rows[...] = dot(hidden, down_mat[...])
     pack_slots(rows, served)
     keep(flag, first + second, False)
+
+
+def fetch(sources, targets, done):
+    copies = [
+        pltpu.make_async_copy(source, target, done.at[index])
+        for index, (source, target) in enumerate(zip(sources, targets))
+    ]
+    for copy in copies:
+        copy.start()
+    return lambda index: copies[index].wait()
+
+
+def serve_far_body(flag, received, *refs):
+    sources, refs, mats, loaded = (refs[:3], refs[3:-4], refs[-4:-1], refs[-1])
+    old, outs, work = (refs[:2], refs[2:5], refs[8:])
+    ready = fetch(sources, mats, loaded)
+    serve_body(flag, received, *mats, *old, *outs, *work, ready=ready)
+
+
+def serve_back_far_body(flag, received, pre_record, *refs):
+    sources, refs, mats, loaded = (refs[:3], refs[3:-4], refs[-4:-1], refs[-1])
+    old, outs, work = (refs[:2], refs[2:5], refs[8:])
+    ready = fetch(sources[::-1], mats[::-1], loaded)
+    serve_back_body(flag, received, pre_record, *mats, *old, *outs, *work, ready=ready)
 
 
 def serve_back_rows(received, load, pre, down_mat, slot_grads, narrow, rows, begin):
@@ -239,12 +267,22 @@
     slot_grads,
     narrow,
     done,
+    ready=lambda index: None,
 ):
     load = pltpu.make_async_copy(pre_record, pre, done.at[0])
     first = [pltpu.make_async_copy(slot_grads, grads_record, done.at[1])]
     grad_gate, grad_up = serve_back_rows(
-        received, load, pre, down_mat, slot_grads, narrow, rows, lambda: keep(flag, first, True)
-    )
+        received,
+        load,
+        pre,
+        down_mat,
+        slot_grads,
+        narrow,
+        rows,
+        lambda: (keep(flag, first, True), ready(0)),
+    )
+    ready(1)
+    ready(2)
     second = [pltpu.make_async_copy(narrow, narrow_record, done.at[2])]
     keep(flag, second, True)
     rows[...] = dot_t(grad_gate, gate_mat[...]) + dot_t(grad_up, up_mat[...])
@@ -258,10 +296,45 @@
 
 
 def lowrank_body(
-    flag, rows, mats, targets, head, grads, all_normed, all_act, all_pre, all_grads, values, inner, scale
+    flag,
+    rows,
+    far_in,
+    targets,
+    head,
+    grads,
+    far_normed,
+    far_act,
+    far_pre,
+    far_grads,
+    far_same,
+    mats,
+    all_normed,
+    all_act,
+    all_pre,
+    all_grads,
+    values,
+    inner,
+    scale,
+    loaded,
+    stored,
 ):
     count = mats.shape[0]
     live = flag[0].astype(jnp.float32)
+
+    def load(index):
+        return pltpu.make_async_copy(far_in.at[index], mats.at[index], loaded.at[index])
+
+    def store(kind, index):
+        near, far = (
+            (all_normed, far_normed),
+            (all_act, far_act),
+            (all_pre, far_pre),
+            (all_grads, far_grads),
+        )[kind]
+        return pltpu.make_async_copy(near.at[index], far.at[index], stored.at[kind, index])
+
+    for index in reversed(range(count)):
+        load(index).start()
     values[0] = rows[...]
 
     def forward(step, carry):
@@ -269,10 +342,13 @@
         value = values[step]
         row_scale = rms_scale(value)
         normed = (value.astype(jnp.float32) * row_scale).astype(jnp.bfloat16)
+        load(index).wait()
         inner_pre = dot(normed, mats[index, 0])
         act = (inner_pre * jax.nn.sigmoid(inner_pre)).astype(jnp.bfloat16)
         all_normed[index] = normed
         all_act[index] = (act.astype(jnp.float32) * live).astype(jnp.bfloat16)
+        store(0, index).start()
+        store(1, index).start()
         inner[index] = inner_pre
         scale[index] = row_scale
         values[step + 1] = (
@@ -299,35 +375,56 @@
         grad_norm = dot_t(grad_pre, mats[index, 0])
         all_pre[index] = (grad_pre.astype(jnp.float32) * live).astype(jnp.bfloat16)
         all_grads[index] = grad
+        store(2, index).start()
+        store(3, index).start()
         grads[...] = (
             grad.astype(jnp.float32) + norm_back(value, scale[index], grad_norm)
         ).astype(jnp.bfloat16)
         return carry
 
     lax.fori_loop(0, count, backward, 0)
+    for index in range(count):
+        for kind in range(4):
+            store(kind, index).wait()
 
 
 def lowrank_layers(flag, rows, mats, targets, head):
     count, rank = (mats.shape[0], mats.shape[3])
     row_count, width = rows.shape
-    wide = array((count, row_count, width))
-    narrow = array((count, row_count, rank))
+    wide, narrow = ((count, row_count, width), (count, row_count, rank))
     return run_kernel(
         lowrank_body,
-        (array(rows.shape), wide, narrow, narrow, wide),
+        (
+            array(rows.shape),
+            array(wide),
+            array(narrow),
+            array(narrow),
+            array(wide),
+            array(mats.shape),
+        ),
         [
+            pltpu.VMEM(mats.shape, jnp.bfloat16),
+            pltpu.VMEM(wide, jnp.bfloat16),
+            pltpu.VMEM(narrow, jnp.bfloat16),
+            pltpu.VMEM(narrow, jnp.bfloat16),
+            pltpu.VMEM(wide, jnp.bfloat16),
             pltpu.VMEM((count + 1, row_count, width), jnp.bfloat16),
             pltpu.VMEM((count, row_count, rank), jnp.float32),
             pltpu.VMEM((count, row_count, 1), jnp.float32),
+            pltpu.SemaphoreType.DMA((count,)),
+            pltpu.SemaphoreType.DMA((4, count)),
         ],
         flag,
         rows,
         mats,
         targets,
         head,
+        far=(2,),
+        far_out=(1, 2, 3, 4, 5),
         scalars=(0,),
+        aliases={2: 5},
         limit=40,
-    )
+    )[:5]
 
 
 def parts_body(normed, pre, grads, act, parts):
@@ -346,7 +443,7 @@
     return pl.pallas_call(
         parts_body,
         grid=(count,),
-        out_shape=array((blocks, count, 2, depth, rank)),
+        out_shape=pltpu.HBM((blocks, count, 2, depth, rank), jnp.bfloat16),
         in_specs=[wide, narrow, wide, narrow],
         out_specs=pl.BlockSpec((blocks, 1, 2, depth, rank), lambda k: (0, k, 0, 0, 0)),
         compiler_params=pltpu.CompilerParams(vmem_limit_bytes=16 * 1024 * 1024),
@@ -356,6 +453,30 @@
             transcendentals=0,
         ),
     )(normed, pre, grads, act)
+
+
+def weights_body(kept, slot_grads, narrow, gate, up, down):
+    inner = gate.shape[1]
+    gate[...] = dot_tn(kept[...], narrow[:, inner : 2 * inner])
+    up[...] = dot_tn(kept[...], narrow[:, 2 * inner :])
+    down[...] = dot_tn(narrow[:, :inner], slot_grads[...])
+
+
+def weight_sums(kept, slot_grads, narrow):
+    slots, width = kept.shape
+    inner = narrow.shape[1] // 3
+    wide = pl.BlockSpec((slots, inner), lambda k: (0, k))
+    tall = pl.BlockSpec((inner, inner), lambda k: (k, 0))
+    return pl.pallas_call(
+        weights_body,
+        grid=(width // inner,),
+        out_shape=tuple(
+            jax.ShapeDtypeStruct(shape, jnp.float32)
+            for shape in ((width, inner), (width, inner), (inner, width))
+        ),
+        in_specs=[wide, wide, pl.BlockSpec(narrow.shape, lambda k: (0, 0))],
+        out_specs=(tall, tall, pl.BlockSpec((inner, inner), lambda k: (0, k))),
+    )(kept, slot_grads, narrow)
 
 
 def exchange(buffer):
@@ -468,53 +589,61 @@
     )
 
 
-def serve(flag, received, mats, kept, pre):
+def far_mats(mats):
+    return [pltpu.VMEM(mat.shape, mat.dtype) for mat in mats] + [pltpu.SemaphoreType.DMA((3,))]
+
+
+def serve(flag, received, mats, kept, pre, far=False):
     count, depth, width = received.shape
     slots, inner = (count * depth, mats[0].shape[1])
     return run_kernel(
-        serve_body,
-        (array(received.shape), array((slots, width)), array((2, slots, inner), jnp.float32)),
+        serve_far_body if far else serve_body,
+        (array(received.shape), array((slots, width)), array((2, slots, inner), jnp.float32))
+        + (tuple(array(mat.shape) for mat in mats) if far else ()),
         work_rows(slots, width)
         + [
             pltpu.VMEM((slots, width), jnp.bfloat16),
             pltpu.VMEM((2, slots, inner), jnp.float32),
             pltpu.SemaphoreType.DMA((2,)),
-        ],
+        ]
+        + (far_mats(mats) if far else []),
         flag,
         received,
         *mats,
         kept,
         pre,
-        far=(5, 6),
-        far_out=(1, 2),
+        far=(2, 3, 4, 5, 6) if far else (5, 6),
+        far_out=(1, 2, 3, 4, 5),
         scalars=(0,),
-        aliases={5: 1, 6: 2},
-    )
-
-
-def serve_back(flag, received, pre, mats, grads, narrow):
+        aliases={2: 3, 3: 4, 4: 5, 5: 1, 6: 2} if far else {5: 1, 6: 2},
+    )
+
+
+def serve_back(flag, received, pre, mats, grads, narrow, far=False):
     width = received.shape[2]
     _, slots, inner = pre.shape
     return run_kernel(
-        serve_back_body,
-        (array(received.shape), array((slots, width)), array((slots, 3 * inner))),
+        serve_back_far_body if far else serve_back_body,
+        (array(received.shape), array((slots, width)), array((slots, 3 * inner)))
+        + (tuple(array(mat.shape) for mat in mats) if far else ()),
         work_rows(slots, width)
         + [
             pltpu.VMEM(pre.shape, jnp.float32),
             pltpu.VMEM((slots, width), jnp.bfloat16),
             pltpu.VMEM((slots, 3 * inner), jnp.bfloat16),
             pltpu.SemaphoreType.DMA((3,)),
-        ],
+        ]
+        + (far_mats(mats) if far else []),
         flag,
         received,
         pre,
         *mats,
         grads,
         narrow,
-        far=(2, 6, 7),
-        far_out=(1, 2),
+        far=(2, 3, 4, 5, 6, 7) if far else (2, 6, 7),
+        far_out=(1, 2, 3, 4, 5),
         scalars=(0,),
-        aliases={6: 1, 7: 2},
+        aliases={3: 3, 4: 4, 5: 5, 6: 1, 7: 2} if far else {6: 1, 7: 2},
     )
 
 
@@ -549,7 +678,6 @@
     section = lax.axis_index("section")
     expert_count = lax.axis_size("expert")
     micro_count, row_count, width = features.shape
-    inner = gate_weight.shape[3]
     is_even = section % 2 == 0
     pair = section // 2
     to_odd = [(s, s + 1) for s in range(0, section_count, 2)]
@@ -624,16 +752,16 @@
     pre_record = [None, None]
     for layer in range(1, section_count):
         side = layer % 2
-        served, kept_record[side], pre_record[side] = serve(
+        served, kept_record[side], pre_record[side], *moved = serve(
             flags[layer],
             exchange(sending),
             mats_odd if side else mats_even,
             kept_record[side],
             pre_record[side],
+            far=side == 0,
         )
-        if layer == 1:
-            served, down_on = lax.optimization_barrier((served, down_on))
-            mats_even = tuple(jnp.where(is_even, a, b) for a, b in zip(own, others + (down_on,)))
+        if side == 0:
+            mats_even = moved
         returned = exchange(served)
         if side == 0:
             rows, row_record[side], sending = turn(
@@ -652,10 +780,13 @@
             rows, row_record[side] = take(
                 flags[layer], returned, routing[layer], rows, row_record[side]
             )
+            if layer == 1:
+                rows, down_on = lax.optimization_barrier((rows, down_on))
+                on = others + (down_on,)
+                mats_even = tuple(jnp.where(is_even, a, b) for a, b in zip(own, on))
             if layer < section_count - 1:
                 rows = hop(rows, layer)
                 sending = send(rows, routing[layer + 1][0])
-    mats = [mats_odd if layer % 2 else mats_even for layer in range(section_count)]
 
     targets = jnp.where(is_even, labels[0], labels[1]).astype(jnp.float32)[:, None]
     grads, low_normed, low_act, low_pre, low_grads = lowrank_layers(
@@ -673,14 +804,16 @@
     narrow_record = [None, None]
     for layer in reversed(range(1, section_count)):
         side = layer % 2
-        target, grads_record[side], narrow_record[side] = serve_back(
+        target, grads_record[side], narrow_record[side], *moved = serve_back(
             flags[layer],
             exchange(sending),
             pre_record[side],
-            mats[layer],
+            mats_odd if side else mats_even,
             grads_record[side],
             narrow_record[side],
+            far=side == 0,
         )
+        mats_even = moved if side == 0 else mats_even
         returned = exchange(target)
         values = row_record[side]
         if side == 1 and layer > 1:
@@ -710,12 +843,12 @@
         jnp.where(section == 0, both, jnp.concatenate([mine, other], axis=0))
         for both, mine, other in zip(joint, held, theirs)
     )
-    hidden, grad_gate, grad_up = (narrow[:, inner * k : inner * (k + 1)] for k in range(3))
+    sums = weight_sums(kept, slot_grads, narrow)
     share = jnp.sum(share[2 * last_pair :].astype(jnp.float32), axis=0)
     return (
-        dot_tn(kept, grad_gate)[None, None],
-        dot_tn(kept, grad_up)[None, None],
-        dot_tn(hidden, slot_grads)[None, None],
+        sums[0][None, None],
+        sums[1][None, None],
+        sums[2][None, None],
         share[0][None],
         share[1].T[None],
     )

time: 798 us -> 785 us (0.984)
  Pallas kernels: 68.1 us -> 88.5 us
  local copies, waits for them, and re-layouts: 51 us -> 34.1 us
  blocking collectives: 301 us -> 286 us
  other arithmetic: 14.5 us -> 24.2 us
  matrix products: 8.97 us -> 0 us
    unnamed x165 -> x119, local copies, waits for them, and re-layouts: 47.4 us -> 30.5 us
    all_to_all x19 -> x18, blocking collectives: 301 us -> 286 us  [exchange(): lax.all_to_all(buffer, 'expert', split_axis=0, concat_axis=0, tiled=True)]
    pallas_call x42, Pallas kernels: 63.8 us -> 74.8 us  [run_kernel(): pl.pallas_call(body, out_shape=jax.tree.unflatten(treedef, leaves), in_sp...]
    pallas_call x1 -> x2, Pallas kernels: 4.3 us -> 13.7 us  [the longest x1 7.24 us: weight_sums(): pl.pallas_call(weights_body, grid=(width // inner,), out_shape=tuple((jax...]
    all_to_all x12 -> x13, waiting for transfers between devices: 121 us -> 130 us  [exchange(): lax.all_to_all(buffer, 'expert', split_axis=0, concat_axis=0, tiled=True)]
    ppermute x1, waiting for transfers between devices: 8.99 us -> 0.01 us  [local(): down_on = lax.ppermute(late, 'section', to_odd)]
    dot_general x3 -> x0, matrix products: 8.97 us -> none  [dot_tn(): lax.dot_general(left, right, (((0,), (0,)), ((), ())), preferred_element_...]
    all_to_all x12 -> x13, starting transfers between devices: 67.8 us -> 69.1 us  [exchange(): lax.all_to_all(buffer, 'expert', split_axis=0, concat_axis=0, tiled=True)]
  transfers between devices with their start and end apart: 37 -> 38, of which waited for: 27 -> 28; matrix products, arithmetic and copies ran while one was open for 3% -> 3% of each run, Pallas kernels for 5% -> 7%
where the time goes in v5:
time: 785 us; the launch traced here: 773 us
  blocking collectives  286 us (36%)
  waiting for transfers between devices  216 us (28%)
  starting transfers between devices  108 us (14%)
  Pallas kernels  88.5 us (11%)
  local copies, waits for them, and re-layouts  34.1 us (4%)
  other arithmetic  24.2 us (3%)
  between operations  15.7 us (2%)
    all_to_all x18, blocking collectives, exchange(): lax.all_to_all(buffer, 'expert', split_axis=0, concat_axis=0, tiled=True)  286 us
    all_to_all x13, waiting for transfers between devices, exchange(): lax.all_to_all(buffer, 'expert', split_axis=0, concat_axis=0, tiled=True)  130 us
    pallas_call x42, Pallas kernels, run_kernel(): pl.pallas_call(body, out_shape=jax.tree.unflatten(treedef, leaves), in_sp...  74.8 us
    ppermute x12, waiting for transfers between devices, hop(): lax.ppermute(part, 'section', links)  71.3 us
    all_to_all x13, starting transfers between devices, exchange(): lax.all_to_all(buffer, 'expert', split_axis=0, concat_axis=0, tiled=True)  69.1 us
    unnamed x119, local copies, waits for them, and re-layouts  30.5 us
    ppermute x12, starting transfers between devices, hop(): lax.ppermute(part, 'section', links)  20 us
  transfers between devices with their start and end apart: 38, of which 28 were waited for; matrix products, arithmetic and copies ran while one was open for 3% of the time, Pallas kernels for 7%

profile of v5, /device:TPU:1, one launch (start us, length us, event | category | flops | bytes accessed | tf_op | source)
XLA Modules:
  0.0 772.8 jit_solution(2743993692073341665)
XLA Ops:
  49.3 17.1 %all-to-all-done.1.refs_1_ = bf16[32,6,2048]{2,1,0:T(8,128)(2,1)S(1)} async-done(((bf16[32,6,2048]{2,1,0:T(8,128)(2,1)}), bf16[32,6,2048]{2,1,0:T(8,128)(2,1)S(1)}, u32[]{:S(2)}, u32[]{:S(2)}) %all-to-all-start.1) | async-done | bytes 786464 | tf_op jit(solution)/shard_map/all_to_all | solution.py:483
  107.5 11.6 %all-to-all-done.3.refs_1_ = bf16[32,3,2048]{2,1,0:T(4,128)(2,1)} async-done(((bf16[32,3,2048]{2,1,0:T(4,128)(2,1)}), bf16[32,3,2048]{2,1,0:T(4,128)(2,1)}, u32[]{:S(2)}, u32[]{:S(2)}) %all-to-all-start.3) | async-done | bytes 393248 | tf_op jit(solution)/shard_map/all_to_all | solution.py:483
  177.3 15.7 %all_to_all.160.received = bf16[32,3,2048]{2,1,0:T(4,128)(2,1)S(1)} all-to-all(bf16[32,3,2048]{2,1,0:T(4,128)(2,1)} %copy-done.32), channel_id=1, replica_groups=mesh['section'=8,'expert'=32] {'expert'}, dimensions={0} | all-to-all | bytes 786432 | tf_op jit(solution)/shard_map/all_to_all | solution.py:483
  193.9 15.2 %all_to_all.161.returned = bf16[32,3,2048]{2,1,0:T(4,128)(2,1)S(1)} all-to-all(bf16[32,3,2048]{2,1,0:T(4,128)(2,1)S(1)} %get-tuple-element.137), channel_id=1, replica_groups=mesh['section'=8,'expert'=32] {'expert'}, dimensions={0} | all-to-all | bytes 786432 | tf_op jit(solution)/shard_map/all_to_all | solution.py:483
  236.5 11.7 %all-to-all-done.8.received = bf16[32,3,2048]{2,1,0:T(4,128)(2,1)} async-done(((bf16[32,3,2048]{2,1,0:T(4,128)(2,1)}), bf16[32,3,2048]{2,1,0:T(4,128)(2,1)}, u32[]{:S(2)}, u32[]{:S(2)}) %all-to-all-start.8) | async-done | bytes 393248 | tf_op jit(solution)/shard_map/all_to_all | solution.py:483
  251.8 15.2 %all_to_all.162.returned = bf16[32,3,2048]{2,1,0:T(4,128)(2,1)S(1)} all-to-all(bf16[32,3,2048]{2,1,0:T(4,128)(2,1)S(1)} %get-tuple-element.147), channel_id=1, replica_groups=mesh['section'=8,'expert'=32] {'expert'}, dimensions={0} | all-to-all | bytes 786432 | tf_op jit(solution)/shard_map/all_to_all | solution.py:483
  267.9 15.2 %all_to_all.163.received = bf16[32,3,2048]{2,1,0:T(4,128)(2,1)S(1)} all-to-all(bf16[32,3,2048]{2,1,0:T(4,128)(2,1)S(1)} %get-tuple-element.149), channel_id=1, replica_groups=mesh['section'=8,'expert'=32] {'expert'}, dimensions={0} | all-to-all | bytes 786432 | tf_op jit(solution)/shard_map/all_to_all | solution.py:483
  284.1 15.2 %all_to_all.164.returned = bf16[32,3,2048]{2,1,0:T(4,128)(2,1)S(1)} all-to-all(bf16[32,3,2048]{2,1,0:T(4,128)(2,1)S(1)} %get-tuple-element.152), channel_id=1, replica_groups=mesh['section'=8,'expert'=32] {'expert'}, dimensions={0} | all-to-all | bytes 786432 | tf_op jit(solution)/shard_map/all_to_all | solution.py:483
  337.3 15.2 %all_to_all.165.returned = bf16[32,3,2048]{2,1,0:T(4,128)(2,1)S(1)} all-to-all(bf16[32,3,2048]{2,1,0:T(4,128)(2,1)S(1)} %get-tuple-element.162), channel_id=1, replica_groups=mesh['section'=8,'expert'=32] {'expert'}, dimensions={0} | all-to-all | bytes 786432 | tf_op jit(solution)/shard_map/all_to_all | solution.py:483
  353.4 15.2 %all_to_all.166.received = bf16[32,3,2048]{2,1,0:T(4,128)(2,1)S(1)} all-to-all(bf16[32,3,2048]{2,1,0:T(4,128)(2,1)S(1)} %get-tuple-element.164), channel_id=1, replica_groups=mesh['section'=8,'expert'=32] {'expert'}, dimensions={0} | all-to-all | bytes 786432 | tf_op jit(solution)/shard_map/all_to_all | solution.py:483
  390.6 12.5 %shard_map.158 = (bf16[64,2048]{1,0:T(8,128)(2,1)S(1)}, bf16[8,64,2048]{2,1,0:T(8,128)(2,1)}, bf16[8,64,128]{2,1,0:T(8,128)(2,1)}, bf16[8,64,128]{2,1,0:T(8,128)...) custom-call(s32[1]{0:T(128)} %bitcast.6.flag.refs_0_, ...), custom_call_target="tpu_custom_call", output_to_operand_aliasing={{5}: (2, {})} | custom-call | tf_op jit(solution)/shard_map/pallas_call | solution.py:80
  403.6 15.2 %all_to_all.167.refs_1_ = bf16[32,3,2048]{2,1,0:T(4,128)(2,1)S(1)} all-to-all(bf16[32,3,2048]{2,1,0:T(4,128)(2,1)S(1)} %shard_map.159), channel_id=1, replica_groups=mesh['section'=8,'expert'=32] {'expert'}, dimensions={0} | all-to-all | bytes 786432 | tf_op jit(solution)/shard_map/all_to_all | solution.py:483
  442.7 18.9 %all_to_all.168.refs_1_ = bf16[32,3,2048]{2,1,0:T(4,128)(2,1)S(1)} all-to-all(bf16[32,3,2048]{2,1,0:T(4,128)(2,1)} %copy-done.30), channel_id=1, replica_groups=mesh['section'=8,'expert'=32] {'expert'}, dimensions={0} | all-to-all | bytes 786432 | tf_op jit(solution)/shard_map/all_to_all | solution.py:483
  465.7 15.4 %all_to_all.169.returned = bf16[32,3,2048]{2,1,0:T(4,128)(2,1)S(1)} all-to-all(bf16[32,3,2048]{2,1,0:T(4,128)(2,1)S(1)} %get-tuple-element.193), channel_id=1, replica_groups=mesh['section'=8,'expert'=32] {'expert'}, dimensions={0} | all-to-all | bytes 786432 | tf_op jit(solution)/shard_map/all_to_all | solution.py:483
  495.7 19.4 %all_to_all.170.received = bf16[32,3,2048]{2,1,0:T(4,128)(2,1)S(1)} all-to-all(bf16[32,3,2048]{2,1,0:T(4,128)(2,1)S(1)} %shard_map.165), channel_id=1, replica_groups=mesh['section'=8,'expert'=32] {'expert'}, dimensions={0} | all-to-all | bytes 786432 | tf_op jit(solution)/shard_map/all_to_all | solution.py:483
  517.3 16.7 %all_to_all.171.returned = bf16[32,3,2048]{2,1,0:T(4,128)(2,1)S(1)} all-to-all(bf16[32,3,2048]{2,1,0:T(4,128)(2,1)S(1)} %get-tuple-element.198), channel_id=1, replica_groups=mesh['section'=8,'expert'=32] {'expert'}, dimensions={0} | all-to-all | bytes 786432 | tf_op jit(solution)/shard_map/all_to_all | solution.py:483
  535.1 16.1 %all_to_all.172.received = bf16[32,3,2048]{2,1,0:T(4,128)(2,1)S(1)} all-to-all(bf16[32,3,2048]{2,1,0:T(4,128)(2,1)S(1)} %get-tuple-element.199), channel_id=1, replica_groups=mesh['section'=8,'expert'=32] {'expert'}, dimensions={0} | all-to-all | bytes 786432 | tf_op jit(solution)/shard_map/all_to_all | solution.py:483
  554.3 15.8 %all_to_all.173.returned = bf16[32,3,2048]{2,1,0:T(4,128)(2,1)S(1)} all-to-all(bf16[32,3,2048]{2,1,0:T(4,128)(2,1)S(1)} %get-tuple-element.205), channel_id=1, replica_groups=mesh['section'=8,'expert'=32] {'expert'}, dimensions={0} | all-to-all | bytes 786432 | tf_op jit(solution)/shard_map/all_to_all | solution.py:483
  584.2 16.0 %all_to_all.174.received = bf16[32,3,2048]{2,1,0:T(4,128)(2,1)S(1)} all-to-all(bf16[32,3,2048]{2,1,0:T(4,128)(2,1)S(1)} %shard_map.170), channel_id=1, replica_groups=mesh['section'=8,'expert'=32] {'expert'}, dimensions={0} | all-to-all | bytes 786432 | tf_op jit(solution)/shard_map/all_to_all | solution.py:483
  602.4 15.2 %all_to_all.175.returned = bf16[32,3,2048]{2,1,0:T(4,128)(2,1)S(1)} all-to-all(bf16[32,3,2048]{2,1,0:T(4,128)(2,1)S(1)} %get-tuple-element.209), channel_id=1, replica_groups=mesh['section'=8,'expert'=32] {'expert'}, dimensions={0} | all-to-all | bytes 786432 | tf_op jit(solution)/shard_map/all_to_all | solution.py:483
  618.6 15.5 %all_to_all.176.received = bf16[32,3,2048]{2,1,0:T(4,128)(2,1)S(1)} all-to-all(bf16[32,3,2048]{2,1,0:T(4,128)(2,1)S(1)} %get-tuple-element.210), channel_id=1, replica_groups=mesh['section'=8,'expert'=32] {'expert'}, dimensions={0} | all-to-all | bytes 786432 | tf_op jit(solution)/shard_map/all_to_all | solution.py:483
  637.2 15.2 %all_to_all.177.returned = bf16[32,3,2048]{2,1,0:T(4,128)(2,1)S(1)} all-to-all(bf16[32,3,2048]{2,1,0:T(4,128)(2,1)S(1)} %get-tuple-element.216), channel_id=1, replica_groups=mesh['section'=8,'expert'=32] {'expert'}, dimensions={0} | all-to-all | bytes 786432 | tf_op jit(solution)/shard_map/all_to_all | solution.py:483
  698.3 11.7 %all-to-all-done.29.returned = bf16[32,3,2048]{2,1,0:T(4,128)(2,1)S(1)} async-done(((bf16[32,3,2048]{2,1,0:T(4,128)(2,1)}), bf16[32,3,2048]{2,1,0:T(4,128)(2,1)S(1)}, u32[]{:S(2)}, u32[]{:S(2)}) %all-to-all-start.29) | async-done | bytes 393248 | tf_op jit(solution)/shard_map/all_to_all | solution.py:483
  737.0 14.1 %all-to-all-done.30.received = bf16[32,6,2048]{2,1,0:T(8,128)(2,1)S(1)} async-done(((bf16[32,6,2048]{2,1,0:T(8,128)(2,1)}), bf16[32,6,2048]{2,1,0:T(8,128)(2,1)S(1)}, u32[]{:S(2)}, u32[]{:S(2)}) %all-to-all-start.30) | async-done | bytes 786464 | tf_op jit(solution)/shard_map/all_to_all | solution.py:483
  (294 shorter events, 392.0 us)
Async XLA Ops:
  8.7 21.6 %collective-permute-start.1 = (f32[4,64]{1,0:T(4,128)S(1)}, f32[4,64]{1,0:T(4,128)S(1)}, u32[]{:S(2)}, u32[]{:S(2)}) collective-permute-start(f32[4,64]{1,0:T(4,128)S(1)} %pad_maximum_fusion.2), channel_id=1, source_target_pairs={{0,32},{64,96},{128,160},{192,224},{32,0},{96,64},{160,128},{224,1... | collective-permute-start | bytes 3080 | tf_op jit(solution)/shard_map/ppermute | solution.py:687
  16.1 25.2 %all-to-all-start = ((bf16[32,6,2048]{2,1,0:T(8,128)(2,1)}), bf16[32,6,2048]{2,1,0:T(8,128)(2,1)S(1)}, u32[]{:S(2)}, u32[]{:S(2)}) async-start(bf16[32,6,2048]{2,1,0:T(8,128)(2,1)} %copy-done.9), calls=%async_computation | async-start | bytes 2097152 | tf_op jit(solution)/shard_map/all_to_all | solution.py:483
  24.1 53.7 %collective-permute-start.2 = (bf16[2048,256]{1,0:T(8,128)(2,1)S(1)}, bf16[2048,256]{1,0:T(8,128)(2,1)}, u32[]{:S(2)}, u32[]{:S(2)}) collective-permute-start(bf16[2048,256]{1,0:T(8,128)(2,1)S(1)} %bitcast.68), channel_id=1, source_target_pairs={{0,32},{64,96},{128,160},{192,224},{32,0},{96,64},{160,128},{224,1... | collective-permute-start | bytes 3145736 | tf_op jit(solution)/shard_map/ppermute | solution.py:687
  24.3 53.6 %collective-permute-start.3 = (bf16[2048,256]{1,0:T(8,128)(2,1)S(1)}, bf16[2048,256]{1,0:T(8,128)(2,1)}, u32[]{:S(2)}, u32[]{:S(2)}) collective-permute-start(bf16[2048,256]{1,0:T(8,128)(2,1)S(1)} %bitcast.70), channel_id=1, source_target_pairs={{0,32},{64,96},{128,160},{192,224},{32,0},{96,64},{160,128},{224,1... | collective-permute-start | bytes 3145736 | tf_op jit(solution)/shard_map/ppermute | solution.py:687
  45.1 21.3 %all-to-all-start.1 = ((bf16[32,6,2048]{2,1,0:T(8,128)(2,1)}), bf16[32,6,2048]{2,1,0:T(8,128)(2,1)S(1)}, u32[]{:S(2)}, u32[]{:S(2)}) async-start(bf16[32,6,2048]{2,1,0:T(8,128)(2,1)} %copy-done.22), calls=%async_computation.1 | async-start | bytes 2097152 | tf_op jit(solution)/shard_map/all_to_all | solution.py:483
  70.7 26.2 %collective-permute-start.4 = (bf16[256,2048]{1,0:T(8,128)(2,1)}, bf16[256,2048]{1,0:T(8,128)(2,1)}, u32[]{:S(2)}, u32[]{:S(2)}) collective-permute-start(bf16[256,2048]{1,0:T(8,128)(2,1)} %bitcast.5.refs_4_.down_mat), channel_id=1, source_target_pairs={{32,0},{96,64},{160,128},{224,192},{33,1},{97,65},{161,129},{225,1... | collective-permute-start | bytes 3145736 | tf_op jit(solution)/shard_map/ppermute | solution.py:741
  77.9 20.7 %all-to-all-start.2 = ((bf16[32,3,2048]{2,1,0:T(4,128)(2,1)}), bf16[32,3,2048]{2,1,0:T(4,128)(2,1)}, u32[]{:S(2)}, u32[]{:S(2)}) async-start(bf16[32,3,2048]{2,1,0:T(4,128)(2,1)} %shard_map.140), calls=%async_computation.2 | async-start | bytes 1048576 | tf_op jit(solution)/shard_map/all_to_all | solution.py:483
  85.1 36.1 %collective-permute-start.5 = (bf16[256,2048]{1,0:T(8,128)(2,1)}, bf16[256,2048]{1,0:T(8,128)(2,1)}, u32[]{:S(2)}, u32[]{:S(2)}) collective-permute-start(bf16[256,2048]{1,0:T(8,128)(2,1)} %bitcast.5.refs_4_.down_mat), channel_id=1, source_target_pairs={{0,32},{64,96},{128,160},{192,224},{1,33},{65,97},{129,161},{193,2... | collective-permute-start | bytes 3145736 | tf_op jit(solution)/shard_map/ppermute | solution.py:744
  101.7 17.5 %all-to-all-start.3 = ((bf16[32,3,2048]{2,1,0:T(4,128)(2,1)}), bf16[32,3,2048]{2,1,0:T(4,128)(2,1)}, u32[]{:S(2)}, u32[]{:S(2)}) async-start(bf16[32,3,2048]{2,1,0:T(4,128)(2,1)} %copy-done.31), calls=%async_computation.3 | async-start | bytes 1048576 | tf_op jit(solution)/shard_map/all_to_all | solution.py:483
  136.2 16.4 %all-to-all-start.4 = ((bf16[32,3,2048]{2,1,0:T(4,128)(2,1)}), bf16[32,3,2048]{2,1,0:T(4,128)(2,1)}, u32[]{:S(2)}, u32[]{:S(2)}) async-start(bf16[32,3,2048]{2,1,0:T(4,128)(2,1)} %copy-done.17), calls=%async_computation.4 | async-start | bytes 1048576 | tf_op jit(solution)/shard_map/all_to_all | solution.py:483
  157.0 16.8 %all-to-all-start.5 = ((bf16[32,3,2048]{2,1,0:T(4,128)(2,1)}), bf16[32,3,2048]{2,1,0:T(4,128)(2,1)}, u32[]{:S(2)}, u32[]{:S(2)}) async-start(bf16[32,3,2048]{2,1,0:T(4,128)(2,1)} %copy-done.26), calls=%async_computation.5 | async-start | bytes 1048576 | tf_op jit(solution)/shard_map/all_to_all | solution.py:483
  162.1 227.1 %all-gather.3.cloned.1.call-start = ((), (), s32[]{:S(2)}) async-start(), calls=%async_computation.34 | async-start | bytes 9437184 | tf_op jit(solution)/shard_map/all_gather | solution.py:778
  212.7 17.0 %collective-permute-start.9 = (bf16[32,2048]{1,0:T(8,128)(2,1)S(1)}, bf16[32,2048]{1,0:T(8,128)(2,1)S(1)}, u32[]{:S(2)}, u32[]{:S(2)}) collective-permute-start(bf16[32,2048]{1,0:T(8,128)(2,1)S(1)} %get-tuple-element.251), channel_id=1, source_target_pairs={{64,128},{128,64},{96,160},{160,96},{192,0},{0,192},{224,32},{32,2... | collective-permute-start | bytes 393224 | tf_op jit(solution)/shard_map/ppermute | solution.py:697
  231.0 17.2 %all-to-all-start.8 = ((bf16[32,3,2048]{2,1,0:T(4,128)(2,1)}), bf16[32,3,2048]{2,1,0:T(4,128)(2,1)}, u32[]{:S(2)}, u32[]{:S(2)}) async-start(bf16[32,3,2048]{2,1,0:T(4,128)(2,1)} %copy-done.16), calls=%async_computation.8 | async-start | bytes 1048576 | tf_op jit(solution)/shard_map/all_to_all | solution.py:483
  316.7 17.1 %all-to-all-start.12 = ((bf16[32,3,2048]{2,1,0:T(4,128)(2,1)}), bf16[32,3,2048]{2,1,0:T(4,128)(2,1)}, u32[]{:S(2)}, u32[]{:S(2)}) async-start(bf16[32,3,2048]{2,1,0:T(4,128)(2,1)} %copy-done.15), calls=%async_computation.12 | async-start | bytes 1048576 | tf_op jit(solution)/shard_map/all_to_all | solution.py:483
  370.4 16.4 %all-to-all-start.15 = ((bf16[32,3,2048]{2,1,0:T(4,128)(2,1)}), bf16[32,3,2048]{2,1,0:T(4,128)(2,1)}, u32[]{:S(2)}, u32[]{:S(2)}) async-start(bf16[32,3,2048]{2,1,0:T(4,128)(2,1)} %copy-done.29), calls=%async_computation.15 | async-start | bytes 1048576 | tf_op jit(solution)/shard_map/all_to_all | solution.py:483
  421.8 16.4 %all-to-all-start.17 = ((bf16[32,3,2048]{2,1,0:T(4,128)(2,1)}), bf16[32,3,2048]{2,1,0:T(4,128)(2,1)}, u32[]{:S(2)}, u32[]{:S(2)}) async-start(bf16[32,3,2048]{2,1,0:T(4,128)(2,1)} %copy-done.28), calls=%async_computation.17 | async-start | bytes 1048576 | tf_op jit(solution)/shard_map/all_to_all | solution.py:483
  426.4 227.4 %reduce-scatter.2.cloned.1.call-start = ((), (), s32[]{:S(2)}) async-start(), calls=%async_computation.33 | async-start | bytes 8650752 | tf_op jit(solution)/shard_map/reduce_scatter | solution.py:825
  672.4 16.9 %all-to-all-start.28 = ((bf16[32,3,2048]{2,1,0:T(4,128)(2,1)}), bf16[32,3,2048]{2,1,0:T(4,128)(2,1)}, u32[]{:S(2)}, u32[]{:S(2)}) async-start(bf16[32,3,2048]{2,1,0:T(4,128)(2,1)} %copy-done.14), calls=%async_computation.29 | async-start | bytes 1048576 | tf_op jit(solution)/shard_map/all_to_all | solution.py:483
  679.6 37.5 %collective-permute-start.12 = (bf16[96,2048]{1,0:T(8,128)(2,1)}, bf16[96,2048]{1,0:T(8,128)(2,1)}, u32[]{:S(2)}, u32[]{:S(2)}) collective-permute-start(bf16[96,2048]{1,0:T(8,128)(2,1)} %get-tuple-element.240), channel_id=1, source_target_pairs={{0,32},{64,96},{128,160},{192,224},{32,0},{96,64},{160,128},{224,1... | collective-permute-start | bytes 1179656 | tf_op jit(solution)/shard_map/ppermute | solution.py:687
  694.2 15.8 %all-to-all-start.29 = ((bf16[32,3,2048]{2,1,0:T(4,128)(2,1)}), bf16[32,3,2048]{2,1,0:T(4,128)(2,1)S(1)}, u32[]{:S(2)}, u32[]{:S(2)}) async-start(bf16[32,3,2048]{2,1,0:T(4,128)(2,1)} %copy-done.27), calls=%async_computation.30 | async-start | bytes 1048576 | tf_op jit(solution)/shard_map/all_to_all | solution.py:483
  729.1 22.1 %all-to-all-start.30 = ((bf16[32,6,2048]{2,1,0:T(8,128)(2,1)}), bf16[32,6,2048]{2,1,0:T(8,128)(2,1)S(1)}, u32[]{:S(2)}, u32[]{:S(2)}) async-start(bf16[32,6,2048]{2,1,0:T(8,128)(2,1)} %shard_map.178), calls=%async_computation.31 | async-start | bytes 2097152 | tf_op jit(solution)/shard_map/all_to_all | solution.py:483
  734.8 19.6 %collective-permute-start.20 = (bf16[96,2048]{1,0:T(8,128)(2,1)}, bf16[96,2048]{1,0:T(8,128)(2,1)}, u32[]{:S(2)}, u32[]{:S(2)}) collective-permute-start(bf16[96,2048]{1,0:T(8,128)(2,1)} %get-tuple-element.238), channel_id=1, source_target_pairs={{0,32},{64,96},{128,160},{192,224},{32,0},{96,64},{160,128},{224,1... | collective-permute-start | bytes 1179656 | tf_op jit(solution)/shard_map/ppermute | solution.py:687
  735.5 21.1 %collective-permute-start.21 = (bf16[96,768]{1,0:T(8,128)(2,1)S(1)}, bf16[96,768]{1,0:T(8,128)(2,1)}, u32[]{:S(2)}, u32[]{:S(2)}) collective-permute-start(bf16[96,768]{1,0:T(8,128)(2,1)S(1)} %get-tuple-element.242), channel_id=1, source_target_pairs={{0,32},{64,96},{128,160},{192,224},{32,0},{96,64},{160,128},{224,1... | collective-permute-start | bytes 442376 | tf_op jit(solution)/shard_map/ppermute | solution.py:687
  (70 other events, 562.4 us)
Sparse Core Ops, SparseCore 0:
  177.4 103.3 all-gather.2
  442.8 105.6 reduce-scatter.1

commit v6 on v5

--- a/solution.py
+++ b/solution.py
@@ -455,28 +455,59 @@
     )(normed, pre, grads, act)
 
 
-def weights_body(kept, slot_grads, narrow, gate, up, down):
+def choose(flag, joint, mine, theirs, chosen):
+    half = mine.shape[0]
+
+    @pl.when(flag[0] == 1)
+    def _():
+        chosen[...] = joint[...]
+
+    @pl.when(flag[0] != 1)
+    def _():
+        chosen[:half, :] = mine[...]
+        chosen[half:, :] = theirs[...]
+
+
+def weights_body(flag, *refs):
+    sources, (gate, up, down), (kept, slot_grads, narrow) = (refs[:9], refs[9:12], refs[12:])
+    choose(flag, *sources[0:3], kept)
+    choose(flag, *sources[3:6], slot_grads)
+
+    @pl.when(pl.program_id(0) == 0)
+    def _():
+        choose(flag, *sources[6:9], narrow)
+
     inner = gate.shape[1]
     gate[...] = dot_tn(kept[...], narrow[:, inner : 2 * inner])
     up[...] = dot_tn(kept[...], narrow[:, 2 * inner :])
     down[...] = dot_tn(narrow[:, :inner], slot_grads[...])
 
 
-def weight_sums(kept, slot_grads, narrow):
-    slots, width = kept.shape
-    inner = narrow.shape[1] // 3
-    wide = pl.BlockSpec((slots, inner), lambda k: (0, k))
-    tall = pl.BlockSpec((inner, inner), lambda k: (k, 0))
+def weight_sums(flag, *triples):
+    slots, width = triples[0][0].shape
+    inner = triples[2][0].shape[1] // 3
+    block = 2 * inner
+    in_specs = [pl.BlockSpec(memory_space=pltpu.SMEM)]
+    for triple in triples[:2]:
+        in_specs += [pl.BlockSpec((part.shape[0], block), lambda k: (0, k)) for part in triple]
+    in_specs += [pl.BlockSpec(part.shape, lambda k: (0, 0)) for part in triples[2]]
+    tall = pl.BlockSpec((block, inner), lambda k: (k, 0))
     return pl.pallas_call(
         weights_body,
-        grid=(width // inner,),
+        grid=(width // block,),
         out_shape=tuple(
             jax.ShapeDtypeStruct(shape, jnp.float32)
             for shape in ((width, inner), (width, inner), (inner, width))
         ),
-        in_specs=[wide, wide, pl.BlockSpec(narrow.shape, lambda k: (0, 0))],
-        out_specs=(tall, tall, pl.BlockSpec((inner, inner), lambda k: (0, k))),
-    )(kept, slot_grads, narrow)
+        in_specs=in_specs,
+        out_specs=(tall, tall, pl.BlockSpec((inner, block), lambda k: (0, k))),
+        scratch_shapes=[
+            pltpu.VMEM((slots, block), jnp.bfloat16),
+            pltpu.VMEM((slots, block), jnp.bfloat16),
+            pltpu.VMEM((slots, 3 * inner), jnp.bfloat16),
+        ],
+        compiler_params=pltpu.CompilerParams(vmem_limit_bytes=16 * 1024 * 1024),
+    )(flag, *(part for triple in triples for part in triple))
 
 
 def exchange(buffer):
@@ -727,7 +758,6 @@
     route_all = route_of(
         joint_slots, expert_count * capacity * micro_count, route_gates[0].reshape(-1)
     )
-    routing = [route_odd if layer % 2 else route_even for layer in range(section_count)]
 
     flags = [(pair == layer // 2).astype(jnp.int32)[None] for layer in range(section_count)]
     always = jnp.ones((1,), jnp.int32)
@@ -735,6 +765,12 @@
     served, kept_all, pre_all = serve(
         always, exchange(send(first_rows, route_all[0])), own, None, None
     )
+    targets = jnp.where(is_even, labels[0], labels[1]).astype(jnp.float32)[:, None]
+    on_first = (section == 0).astype(jnp.int32)[None]
+    served, route_all, route_even, route_odd, flags, targets, on_first = lax.optimization_barrier(
+        (served, route_all, route_even, route_odd, flags, targets, on_first)
+    )
+    routing = [route_odd if layer % 2 else route_even for layer in range(section_count)]
     second_rows, _ = take(always, exchange(served), route_all, first_rows, None)
     second_rows, late = lax.optimization_barrier((second_rows, own[2]))
     crossing = lax.ppermute(second_rows[row_count:], "section", to_odd)
@@ -788,7 +824,6 @@
                 rows = hop(rows, layer)
                 sending = send(rows, routing[layer + 1][0])
 
-    targets = jnp.where(is_even, labels[0], labels[1]).astype(jnp.float32)[:, None]
     grads, low_normed, low_act, low_pre, low_grads = lowrank_layers(
         flags[-1], rows, low_mats, targets, head_weight[None, :]
     )
@@ -839,11 +874,7 @@
     joint = (kept_all,) + tuple(
         serve_last(exchange(send_back(all_grads, route_all)), pre_all, own[2])
     )
-    kept, slot_grads, narrow = (
-        jnp.where(section == 0, both, jnp.concatenate([mine, other], axis=0))
-        for both, mine, other in zip(joint, held, theirs)
-    )
-    sums = weight_sums(kept, slot_grads, narrow)
+    sums = weight_sums(on_first, *zip(joint, held, theirs))
     share = jnp.sum(share[2 * last_pair :].astype(jnp.float32), axis=0)
     return (
         sums[0][None, None],

time: 785 us -> 790 us (level)
  blocking collectives: 286 us -> 349 us
  waiting for transfers between devices: 216 us -> 187 us
  starting transfers between devices: 108 us -> 93.6 us
    all_to_all x18 -> x22, blocking collectives: 286 us -> 349 us  [exchange(): lax.all_to_all(buffer, 'expert', split_axis=0, concat_axis=0, tiled=True)]
    all_to_all x13 -> x9, waiting for transfers between devices: 130 us -> 80.2 us  [exchange(): lax.all_to_all(buffer, 'expert', split_axis=0, concat_axis=0, tiled=True)]
    ppermute x1, waiting for transfers between devices: 3.57 us -> 28.1 us  [local(): crossing = lax.ppermute(second_rows[row_count:], 'section', to_odd)]
    all_to_all x13 -> x9, starting transfers between devices: 69.1 us -> 52.7 us  [exchange(): lax.all_to_all(buffer, 'expert', split_axis=0, concat_axis=0, tiled=True)]
    unnamed x119 -> x105, local copies, waits for them, and re-layouts: 30.5 us -> 25.4 us
  transfers between devices with their start and end apart: 38 -> 34, of which waited for: 28 -> 24; matrix products, arithmetic and copies ran while one was open for 3% -> 3% of each run, Pallas kernels for 7% -> 6%
where the time goes in v6:
time: 790 us; the launch traced here: 779 us
  blocking collectives  349 us (44%)
  waiting for transfers between devices  187 us (24%)
  starting transfers between devices  93.6 us (12%)
  Pallas kernels  82.8 us (10%)
  local copies, waits for them, and re-layouts  30.4 us (4%)
  other arithmetic  20.8 us (3%)
  between operations  15.5 us (2%)
    all_to_all x22, blocking collectives, exchange(): lax.all_to_all(buffer, 'expert', split_axis=0, concat_axis=0, tiled=True)  349 us
    all_to_all x9, waiting for transfers between devices, exchange(): lax.all_to_all(buffer, 'expert', split_axis=0, concat_axis=0, tiled=True)  80.2 us
    pallas_call x42, Pallas kernels, run_kernel(): pl.pallas_call(body, out_shape=jax.tree.unflatten(treedef, leaves), in_sp...  71.5 us
    ppermute x12, waiting for transfers between devices, hop(): lax.ppermute(part, 'section', links)  71.4 us
    all_to_all x9, starting transfers between devices, exchange(): lax.all_to_all(buffer, 'expert', split_axis=0, concat_axis=0, tiled=True)  52.7 us
    ppermute x1, waiting for transfers between devices, local(): crossing = lax.ppermute(second_rows[row_count:], 'section', to_odd)  28.1 us
    unnamed x105, local copies, waits for them, and re-layouts  25.4 us
    ppermute x12, starting transfers between devices, hop(): lax.ppermute(part, 'section', links)  19.9 us
  transfers between devices with their start and end apart: 34, of which 24 were waited for; matrix products, arithmetic and copies ran while one was open for 3% of the time, Pallas kernels for 6%

profile of v6, /device:TPU:1, one launch (start us, length us, event | category | flops | bytes accessed | tf_op | source)
XLA Modules:
  0.0 778.6 jit_solution(3946080445618641387)
XLA Ops:
  50.8 15.6 %all-to-all-done.1.refs_1_ = bf16[32,6,2048]{2,1,0:T(8,128)(2,1)S(1)} async-done(((bf16[32,6,2048]{2,1,0:T(8,128)(2,1)}), bf16[32,6,2048]{2,1,0:T(8,128)(2,1)S(1)}, u32[]{:S(2)}, u32[]{:S(2)}) %all-to-all-start.1) | async-done | bytes 786464 | tf_op jit(solution)/shard_map/all_to_all | solution.py:514
  71.6 28.1 %collective-permute-done.1 = bf16[64,2048]{1,0:T(8,128)(2,1)S(1)} collective-permute-done((bf16[64,2048]{1,0:T(8,128)(2,1)S(1)}, bf16[64,2048]{1,0:T(8,128)(2,1)S(1)}, u32[]{:S(2)}, u32[]{:S(2)}) %collective-permute-start.1) | collective-permute-done | bytes 262176 | tf_op jit(solution)/shard_map/ppermute | solution.py:776
  201.4 15.7 %all_to_all.160.received = bf16[32,3,2048]{2,1,0:T(4,128)(2,1)S(1)} all-to-all(bf16[32,3,2048]{2,1,0:T(4,128)(2,1)} %copy-done.28), channel_id=1, replica_groups=mesh['section'=8,'expert'=32] {'expert'}, dimensions={0} | all-to-all | bytes 786432 | tf_op jit(solution)/shard_map/all_to_all | solution.py:514
  218.0 15.2 %all_to_all.161.returned = bf16[32,3,2048]{2,1,0:T(4,128)(2,1)S(1)} all-to-all(bf16[32,3,2048]{2,1,0:T(4,128)(2,1)S(1)} %get-tuple-element.172), channel_id=1, replica_groups=mesh['section'=8,'expert'=32] {'expert'}, dimensions={0} | all-to-all | bytes 786432 | tf_op jit(solution)/shard_map/all_to_all | solution.py:514
  254.3 16.0 %all_to_all.162.received = bf16[32,3,2048]{2,1,0:T(4,128)(2,1)S(1)} all-to-all(bf16[32,3,2048]{2,1,0:T(4,128)(2,1)S(1)} %shard_map.148), channel_id=1, replica_groups=mesh['section'=8,'expert'=32] {'expert'}, dimensions={0} | all-to-all | bytes 786432 | tf_op jit(solution)/shard_map/all_to_all | solution.py:514
  272.8 15.2 %all_to_all.163.returned = bf16[32,3,2048]{2,1,0:T(4,128)(2,1)S(1)} all-to-all(bf16[32,3,2048]{2,1,0:T(4,128)(2,1)S(1)} %get-tuple-element.182), channel_id=1, replica_groups=mesh['section'=8,'expert'=32] {'expert'}, dimensions={0} | all-to-all | bytes 786432 | tf_op jit(solution)/shard_map/all_to_all | solution.py:514
  289.0 15.2 %all_to_all.164.received = bf16[32,3,2048]{2,1,0:T(4,128)(2,1)S(1)} all-to-all(bf16[32,3,2048]{2,1,0:T(4,128)(2,1)S(1)} %get-tuple-element.184), channel_id=1, replica_groups=mesh['section'=8,'expert'=32] {'expert'}, dimensions={0} | all-to-all | bytes 786432 | tf_op jit(solution)/shard_map/all_to_all | solution.py:514
  305.1 15.2 %all_to_all.165.returned = bf16[32,3,2048]{2,1,0:T(4,128)(2,1)S(1)} all-to-all(bf16[32,3,2048]{2,1,0:T(4,128)(2,1)S(1)} %get-tuple-element.187), channel_id=1, replica_groups=mesh['section'=8,'expert'=32] {'expert'}, dimensions={0} | all-to-all | bytes 786432 | tf_op jit(solution)/shard_map/all_to_all | solution.py:514
  336.9 15.6 %all_to_all.166.received = bf16[32,3,2048]{2,1,0:T(4,128)(2,1)S(1)} all-to-all(bf16[32,3,2048]{2,1,0:T(4,128)(2,1)S(1)} %shard_map.153), channel_id=1, replica_groups=mesh['section'=8,'expert'=32] {'expert'}, dimensions={0} | all-to-all | bytes 786432 | tf_op jit(solution)/shard_map/all_to_all | solution.py:514
  355.0 15.2 %all_to_all.167.returned = bf16[32,3,2048]{2,1,0:T(4,128)(2,1)S(1)} all-to-all(bf16[32,3,2048]{2,1,0:T(4,128)(2,1)S(1)} %get-tuple-element.198), channel_id=1, replica_groups=mesh['section'=8,'expert'=32] {'expert'}, dimensions={0} | all-to-all | bytes 786432 | tf_op jit(solution)/shard_map/all_to_all | solution.py:514
  371.1 15.2 %all_to_all.168.received = bf16[32,3,2048]{2,1,0:T(4,128)(2,1)S(1)} all-to-all(bf16[32,3,2048]{2,1,0:T(4,128)(2,1)S(1)} %get-tuple-element.200), channel_id=1, replica_groups=mesh['section'=8,'expert'=32] {'expert'}, dimensions={0} | all-to-all | bytes 786432 | tf_op jit(solution)/shard_map/all_to_all | solution.py:514
  421.3 15.2 %all_to_all.169.refs_1_ = bf16[32,3,2048]{2,1,0:T(4,128)(2,1)S(1)} all-to-all(bf16[32,3,2048]{2,1,0:T(4,128)(2,1)S(1)} %shard_map.159), channel_id=1, replica_groups=mesh['section'=8,'expert'=32] {'expert'}, dimensions={0} | all-to-all | bytes 786432 | tf_op jit(solution)/shard_map/all_to_all | solution.py:514
  460.4 18.7 %all_to_all.170.refs_1_ = bf16[32,3,2048]{2,1,0:T(4,128)(2,1)S(1)} all-to-all(bf16[32,3,2048]{2,1,0:T(4,128)(2,1)} %copy-done.27), channel_id=1, replica_groups=mesh['section'=8,'expert'=32] {'expert'}, dimensions={0} | all-to-all | bytes 786432 | tf_op jit(solution)/shard_map/all_to_all | solution.py:514
  483.3 15.4 %all_to_all.171.returned = bf16[32,3,2048]{2,1,0:T(4,128)(2,1)S(1)} all-to-all(bf16[32,3,2048]{2,1,0:T(4,128)(2,1)S(1)} %get-tuple-element.230), channel_id=1, replica_groups=mesh['section'=8,'expert'=32] {'expert'}, dimensions={0} | all-to-all | bytes 786432 | tf_op jit(solution)/shard_map/all_to_all | solution.py:514
  513.4 19.4 %all_to_all.172.received = bf16[32,3,2048]{2,1,0:T(4,128)(2,1)S(1)} all-to-all(bf16[32,3,2048]{2,1,0:T(4,128)(2,1)S(1)} %shard_map.165), channel_id=1, replica_groups=mesh['section'=8,'expert'=32] {'expert'}, dimensions={0} | all-to-all | bytes 786432 | tf_op jit(solution)/shard_map/all_to_all | solution.py:514
  534.9 16.7 %all_to_all.173.returned = bf16[32,3,2048]{2,1,0:T(4,128)(2,1)S(1)} all-to-all(bf16[32,3,2048]{2,1,0:T(4,128)(2,1)S(1)} %get-tuple-element.235), channel_id=1, replica_groups=mesh['section'=8,'expert'=32] {'expert'}, dimensions={0} | all-to-all | bytes 786432 | tf_op jit(solution)/shard_map/all_to_all | solution.py:514
  552.7 16.4 %all_to_all.174.received = bf16[32,3,2048]{2,1,0:T(4,128)(2,1)S(1)} all-to-all(bf16[32,3,2048]{2,1,0:T(4,128)(2,1)S(1)} %get-tuple-element.236), channel_id=1, replica_groups=mesh['section'=8,'expert'=32] {'expert'}, dimensions={0} | all-to-all | bytes 786432 | tf_op jit(solution)/shard_map/all_to_all | solution.py:514
  572.2 15.5 %all_to_all.175.returned = bf16[32,3,2048]{2,1,0:T(4,128)(2,1)S(1)} all-to-all(bf16[32,3,2048]{2,1,0:T(4,128)(2,1)S(1)} %get-tuple-element.242), channel_id=1, replica_groups=mesh['section'=8,'expert'=32] {'expert'}, dimensions={0} | all-to-all | bytes 786432 | tf_op jit(solution)/shard_map/all_to_all | solution.py:514
  601.7 16.0 %all_to_all.176.received = bf16[32,3,2048]{2,1,0:T(4,128)(2,1)S(1)} all-to-all(bf16[32,3,2048]{2,1,0:T(4,128)(2,1)S(1)} %shard_map.170), channel_id=1, replica_groups=mesh['section'=8,'expert'=32] {'expert'}, dimensions={0} | all-to-all | bytes 786432 | tf_op jit(solution)/shard_map/all_to_all | solution.py:514
  619.9 15.2 %all_to_all.177.returned = bf16[32,3,2048]{2,1,0:T(4,128)(2,1)S(1)} all-to-all(bf16[32,3,2048]{2,1,0:T(4,128)(2,1)S(1)} %get-tuple-element.246), channel_id=1, replica_groups=mesh['section'=8,'expert'=32] {'expert'}, dimensions={0} | all-to-all | bytes 786432 | tf_op jit(solution)/shard_map/all_to_all | solution.py:514
  636.1 15.5 %all_to_all.178.received = bf16[32,3,2048]{2,1,0:T(4,128)(2,1)S(1)} all-to-all(bf16[32,3,2048]{2,1,0:T(4,128)(2,1)S(1)} %get-tuple-element.247), channel_id=1, replica_groups=mesh['section'=8,'expert'=32] {'expert'}, dimensions={0} | all-to-all | bytes 786432 | tf_op jit(solution)/shard_map/all_to_all | solution.py:514
  654.7 15.2 %all_to_all.179.returned = bf16[32,3,2048]{2,1,0:T(4,128)(2,1)S(1)} all-to-all(bf16[32,3,2048]{2,1,0:T(4,128)(2,1)S(1)} %get-tuple-element.253), channel_id=1, replica_groups=mesh['section'=8,'expert'=32] {'expert'}, dimensions={0} | all-to-all | bytes 786432 | tf_op jit(solution)/shard_map/all_to_all | solution.py:514
  689.2 15.4 %all_to_all.180.received = bf16[32,3,2048]{2,1,0:T(4,128)(2,1)S(1)} all-to-all(bf16[32,3,2048]{2,1,0:T(4,128)(2,1)S(1)} %shard_map.175), channel_id=1, replica_groups=mesh['section'=8,'expert'=32] {'expert'}, dimensions={0} | all-to-all | bytes 786432 | tf_op jit(solution)/shard_map/all_to_all | solution.py:514
  706.8 15.3 %all_to_all.181.returned = bf16[32,3,2048]{2,1,0:T(4,128)(2,1)S(1)} all-to-all(bf16[32,3,2048]{2,1,0:T(4,128)(2,1)S(1)} %get-tuple-element.258), channel_id=1, replica_groups=mesh['section'=8,'expert'=32] {'expert'}, dimensions={0} | all-to-all | bytes 786432 | tf_op jit(solution)/shard_map/all_to_all | solution.py:514
  (274 shorter events, 370.6 us)
Async XLA Ops:
  8.7 16.2 %collective-permute-start = (f32[4,64]{1,0:T(4,128)S(1)}, f32[4,64]{1,0:T(4,128)S(1)}, u32[]{:S(2)}, u32[]{:S(2)}) collective-permute-start(f32[4,64]{1,0:T(4,128)S(1)} %pad_maximum_fusion.2), channel_id=1, source_target_pairs={{0,32},{64,96},{128,160},{192,224},{32,0},{96,64},{160,128},{224,1... | collective-permute-start | bytes 3080 | tf_op jit(solution)/shard_map/ppermute | solution.py:718
  16.1 25.2 %all-to-all-start = ((bf16[32,6,2048]{2,1,0:T(8,128)(2,1)}), bf16[32,6,2048]{2,1,0:T(8,128)(2,1)S(1)}, u32[]{:S(2)}, u32[]{:S(2)}) async-start(bf16[32,6,2048]{2,1,0:T(8,128)(2,1)} %copy-done.9), calls=%async_computation | async-start | bytes 2097152 | tf_op jit(solution)/shard_map/all_to_all | solution.py:514
  45.1 21.3 %all-to-all-start.1 = ((bf16[32,6,2048]{2,1,0:T(8,128)(2,1)}), bf16[32,6,2048]{2,1,0:T(8,128)(2,1)S(1)}, u32[]{:S(2)}, u32[]{:S(2)}) async-start(bf16[32,6,2048]{2,1,0:T(8,128)(2,1)} %copy-done.19), calls=%async_computation.1 | async-start | bytes 2097152 | tf_op jit(solution)/shard_map/all_to_all | solution.py:514
  49.1 51.9 %collective-permute-start.2 = (bf16[2048,256]{1,0:T(8,128)(2,1)S(1)}, bf16[2048,256]{1,0:T(8,128)(2,1)}, u32[]{:S(2)}, u32[]{:S(2)}) collective-permute-start(bf16[2048,256]{1,0:T(8,128)(2,1)S(1)} %bitcast.70), channel_id=1, source_target_pairs={{0,32},{64,96},{128,160},{192,224},{32,0},{96,64},{160,128},{224,1... | collective-permute-start | bytes 3145736 | tf_op jit(solution)/shard_map/ppermute | solution.py:718
  49.2 51.8 %collective-permute-start.3 = (bf16[2048,256]{1,0:T(8,128)(2,1)S(1)}, bf16[2048,256]{1,0:T(8,128)(2,1)}, u32[]{:S(2)}, u32[]{:S(2)}) collective-permute-start(bf16[2048,256]{1,0:T(8,128)(2,1)S(1)} %bitcast.72), channel_id=1, source_target_pairs={{0,32},{64,96},{128,160},{192,224},{32,0},{96,64},{160,128},{224,1... | collective-permute-start | bytes 3145736 | tf_op jit(solution)/shard_map/ppermute | solution.py:718
  68.5 31.2 %collective-permute-start.1 = (bf16[64,2048]{1,0:T(8,128)(2,1)S(1)}, bf16[64,2048]{1,0:T(8,128)(2,1)S(1)}, u32[]{:S(2)}, u32[]{:S(2)}) collective-permute-start(bf16[64,2048]{1,0:T(8,128)(2,1)S(1)} %slice.102), channel_id=1, source_target_pairs={{0,32},{64,96},{128,160},{192,224},{1,33},{65,97},{129,161},{193,2... | collective-permute-start | bytes 786440 | tf_op jit(solution)/shard_map/ppermute | solution.py:776
  70.3 48.7 %collective-permute-start.4 = (bf16[256,2048]{1,0:T(8,128)(2,1)}, bf16[256,2048]{1,0:T(8,128)(2,1)}, u32[]{:S(2)}, u32[]{:S(2)}) collective-permute-start(bf16[256,2048]{1,0:T(8,128)(2,1)} %bitcast.5.refs_4_.down_mat), channel_id=1, source_target_pairs={{32,0},{96,64},{160,128},{224,192},{33,1},{97,65},{161,129},{225,1... | collective-permute-start | bytes 3145736 | tf_op jit(solution)/shard_map/ppermute | solution.py:777
  101.0 19.8 %all-to-all-start.2 = ((bf16[32,3,2048]{2,1,0:T(4,128)(2,1)}), bf16[32,3,2048]{2,1,0:T(4,128)(2,1)}, u32[]{:S(2)}, u32[]{:S(2)}) async-start(bf16[32,3,2048]{2,1,0:T(4,128)(2,1)} %shard_map.140), calls=%async_computation.2 | async-start | bytes 1048576 | tf_op jit(solution)/shard_map/all_to_all | solution.py:514
  109.2 36.2 %collective-permute-start.5 = (bf16[256,2048]{1,0:T(8,128)(2,1)}, bf16[256,2048]{1,0:T(8,128)(2,1)}, u32[]{:S(2)}, u32[]{:S(2)}) collective-permute-start(bf16[256,2048]{1,0:T(8,128)(2,1)} %bitcast.5.refs_4_.down_mat), channel_id=1, source_target_pairs={{0,32},{64,96},{128,160},{192,224},{1,33},{65,97},{129,161},{193,2... | collective-permute-start | bytes 3145736 | tf_op jit(solution)/shard_map/ppermute | solution.py:780
  123.9 19.5 %all-to-all-start.3 = ((bf16[32,3,2048]{2,1,0:T(4,128)(2,1)}), bf16[32,3,2048]{2,1,0:T(4,128)(2,1)}, u32[]{:S(2)}, u32[]{:S(2)}) async-start(bf16[32,3,2048]{2,1,0:T(4,128)(2,1)} %copy-done.29), calls=%async_computation.3 | async-start | bytes 1048576 | tf_op jit(solution)/shard_map/all_to_all | solution.py:514
  160.4 16.4 %all-to-all-start.4 = ((bf16[32,3,2048]{2,1,0:T(4,128)(2,1)}), bf16[32,3,2048]{2,1,0:T(4,128)(2,1)}, u32[]{:S(2)}, u32[]{:S(2)}) async-start(bf16[32,3,2048]{2,1,0:T(4,128)(2,1)} %copy-done.14), calls=%async_computation.4 | async-start | bytes 1048576 | tf_op jit(solution)/shard_map/all_to_all | solution.py:514
  181.1 16.8 %all-to-all-start.5 = ((bf16[32,3,2048]{2,1,0:T(4,128)(2,1)}), bf16[32,3,2048]{2,1,0:T(4,128)(2,1)}, u32[]{:S(2)}, u32[]{:S(2)}) async-start(bf16[32,3,2048]{2,1,0:T(4,128)(2,1)} %copy-done.24), calls=%async_computation.5 | async-start | bytes 1048576 | tf_op jit(solution)/shard_map/all_to_all | solution.py:514
  186.2 220.6 %all-gather.3.cloned.1.call-start = ((), (), s32[]{:S(2)}) async-start(), calls=%async_computation.34 | async-start | bytes 9437184 | tf_op jit(solution)/shard_map/all_gather | solution.py:814
  236.8 17.0 %collective-permute-start.9 = (bf16[32,2048]{1,0:T(8,128)(2,1)S(1)}, bf16[32,2048]{1,0:T(8,128)(2,1)S(1)}, u32[]{:S(2)}, u32[]{:S(2)}) collective-permute-start(bf16[32,2048]{1,0:T(8,128)(2,1)S(1)} %get-tuple-element.289), channel_id=1, source_target_pairs={{64,128},{128,64},{96,160},{160,96},{192,0},{0,192},{224,32},{32,2... | collective-permute-start | bytes 393224 | tf_op jit(solution)/shard_map/ppermute | solution.py:728
  388.1 16.4 %all-to-all-start.15 = ((bf16[32,3,2048]{2,1,0:T(4,128)(2,1)}), bf16[32,3,2048]{2,1,0:T(4,128)(2,1)}, u32[]{:S(2)}, u32[]{:S(2)}) async-start(bf16[32,3,2048]{2,1,0:T(4,128)(2,1)} %copy-done.26), calls=%async_computation.15 | async-start | bytes 1048576 | tf_op jit(solution)/shard_map/all_to_all | solution.py:514
  439.5 16.4 %all-to-all-start.17 = ((bf16[32,3,2048]{2,1,0:T(4,128)(2,1)}), bf16[32,3,2048]{2,1,0:T(4,128)(2,1)}, u32[]{:S(2)}, u32[]{:S(2)}) async-start(bf16[32,3,2048]{2,1,0:T(4,128)(2,1)} %copy-done.25), calls=%async_computation.17 | async-start | bytes 1048576 | tf_op jit(solution)/shard_map/all_to_all | solution.py:514
  444.1 227.1 %reduce-scatter.2.cloned.1.call-start = ((), (), s32[]{:S(2)}) async-start(), calls=%async_computation.33 | async-start | bytes 8650752 | tf_op jit(solution)/shard_map/reduce_scatter | solution.py:860
  499.5 13.3 %collective-permute-start.14 = (bf16[32,2048]{1,0:T(8,128)(2,1)S(1)}, bf16[32,2048]{1,0:T(8,128)(2,1)S(1)}, u32[]{:S(2)}, u32[]{:S(2)}) collective-permute-start(bf16[32,2048]{1,0:T(8,128)(2,1)S(1)} %get-tuple-element.285), channel_id=1, source_target_pairs={{0,64},{64,0},{32,96},{96,32},{128,192},{192,128},{160,224},{224,1... | collective-permute-start | bytes 393224 | tf_op jit(solution)/shard_map/ppermute | solution.py:728
  672.3 12.9 %collective-permute-start.17 = (bf16[32,2048]{1,0:T(8,128)(2,1)S(1)}, bf16[32,2048]{1,0:T(8,128)(2,1)S(1)}, u32[]{:S(2)}, u32[]{:S(2)}) collective-permute-start(bf16[32,2048]{1,0:T(8,128)(2,1)S(1)} %get-tuple-element.282), channel_id=1, source_target_pairs={{0,64},{64,0},{32,96},{96,32},{128,192},{192,128},{160,224},{224,1... | collective-permute-start | bytes 393224 | tf_op jit(solution)/shard_map/ppermute | solution.py:728
  722.2 14.7 %all-to-all-start.31 = ((bf16[8,2,64,128]{3,2,1,0:T(8,128)(2,1)}), bf16[8,2,64,128]{3,2,1,0:T(8,128)(2,1)S(1)}, u32[]{:S(2)}, u32[]{:S(2)}) async-start(bf16[8,2,64,128]{3,2,1,0:T(8,128)(2,1)} %bitcast.79), calls=%async_computation.32 | async-start | bytes 524288 | tf_op jit(solution)/shard_map/all_to_all | solution.py:865
  729.9 36.3 %collective-permute-start.12 = (bf16[96,2048]{1,0:T(8,128)(2,1)}, bf16[96,2048]{1,0:T(8,128)(2,1)S(1)}, u32[]{:S(2)}, u32[]{:S(2)}) collective-permute-start(bf16[96,2048]{1,0:T(8,128)(2,1)} %get-tuple-element.277), channel_id=1, source_target_pairs={{0,32},{64,96},{128,160},{192,224},{32,0},{96,64},{160,128},{224,1... | collective-permute-start | bytes 1179656 | tf_op jit(solution)/shard_map/ppermute | solution.py:718
  741.1 22.9 %all-to-all-start.30 = ((bf16[32,6,2048]{2,1,0:T(8,128)(2,1)}), bf16[32,6,2048]{2,1,0:T(8,128)(2,1)S(1)}, u32[]{:S(2)}, u32[]{:S(2)}) async-start(bf16[32,6,2048]{2,1,0:T(8,128)(2,1)} %shard_map.178), calls=%async_computation.31 | async-start | bytes 2097152 | tf_op jit(solution)/shard_map/all_to_all | solution.py:514
  748.7 17.5 %collective-permute-start.20 = (bf16[96,2048]{1,0:T(8,128)(2,1)}, bf16[96,2048]{1,0:T(8,128)(2,1)}, u32[]{:S(2)}, u32[]{:S(2)}) collective-permute-start(bf16[96,2048]{1,0:T(8,128)(2,1)} %get-tuple-element.275), channel_id=1, source_target_pairs={{0,32},{64,96},{128,160},{192,224},{32,0},{96,64},{160,128},{224,1... | collective-permute-start | bytes 1179656 | tf_op jit(solution)/shard_map/ppermute | solution.py:718
  750.4 15.8 %collective-permute-start.21 = (bf16[96,768]{1,0:T(8,128)(2,1)}, bf16[96,768]{1,0:T(8,128)(2,1)}, u32[]{:S(2)}, u32[]{:S(2)}) collective-permute-start(bf16[96,768]{1,0:T(8,128)(2,1)} %get-tuple-element.279), channel_id=1, source_target_pairs={{0,32},{64,96},{128,160},{192,224},{32,0},{96,64},{160,128},{224,1... | collective-permute-start | bytes 442376 | tf_op jit(solution)/shard_map/ppermute | solution.py:718
  (59 other events, 600.6 us)
Sparse Core Ops, SparseCore 0:
  201.5 103.4 all-gather.2
  460.5 105.5 reduce-scatter.1

commit v7 on v6

--- a/solution.py
+++ b/solution.py
@@ -771,7 +771,10 @@
         (served, route_all, route_even, route_odd, flags, targets, on_first)
     )
     routing = [route_odd if layer % 2 else route_even for layer in range(section_count)]
-    second_rows, _ = take(always, exchange(served), route_all, first_rows, None)
+    returned, gate_other, up_other = lax.optimization_barrier(
+        (exchange(served), gate_other, up_other)
+    )
+    second_rows, _ = take(always, returned, route_all, first_rows, None)
     second_rows, late = lax.optimization_barrier((second_rows, own[2]))
     crossing = lax.ppermute(second_rows[row_count:], "section", to_odd)
     down_back = lax.ppermute(late, "section", to_even)

time: 790 us -> 773 us (0.978)
  waiting for transfers between devices: 187 us -> 168 us
    ppermute x1, waiting for transfers between devices: 28.1 us -> 3.45 us  [local(): crossing = lax.ppermute(second_rows[row_count:], 'section', to_odd)]
    ppermute x6, waiting for transfers between devices: 0.02 us -> 22.1 us  [swap(): return lax.ppermute(value, 'section', to_odd + to_even)]
    all_to_all x9, waiting for transfers between devices: 80.2 us -> 62.8 us  [exchange(): lax.all_to_all(buffer, 'expert', split_axis=0, concat_axis=0, tiled=True)]
  transfers between devices with their start and end apart: 34 -> 34, of which waited for: 24 -> 24; matrix products, arithmetic and copies ran while one was open for 3% -> 3% of each run, Pallas kernels for 6% -> 7%
where the time goes in v7:
time: 773 us; the launch traced here: 762 us
  blocking collectives  349 us (45%)
  waiting for transfers between devices  168 us (22%)
  starting transfers between devices  95.8 us (12%)
  Pallas kernels  82.8 us (11%)
  local copies, waits for them, and re-layouts  30.3 us (4%)
  other arithmetic  20.8 us (3%)
  between operations  15.5 us (2%)
    all_to_all x22, blocking collectives, exchange(): lax.all_to_all(buffer, 'expert', split_axis=0, concat_axis=0, tiled=True)  349 us
    pallas_call x42, Pallas kernels, run_kernel(): pl.pallas_call(body, out_shape=jax.tree.unflatten(treedef, leaves), in_sp...  71.5 us
    ppermute x12, waiting for transfers between devices, hop(): lax.ppermute(part, 'section', links)  71.1 us
    all_to_all x9, waiting for transfers between devices, exchange(): lax.all_to_all(buffer, 'expert', split_axis=0, concat_axis=0, tiled=True)  62.8 us
    all_to_all x9, starting transfers between devices, exchange(): lax.all_to_all(buffer, 'expert', split_axis=0, concat_axis=0, tiled=True)  54.3 us
    unnamed x105, local copies, waits for them, and re-layouts  25.4 us
    ppermute x6, waiting for transfers between devices, swap(): return lax.ppermute(value, 'section', to_odd + to_even)  22.1 us
    ppermute x12, starting transfers between devices, hop(): lax.ppermute(part, 'section', links)  20 us
  transfers between devices with their start and end apart: 34, of which 24 were waited for; matrix products, arithmetic and copies ran while one was open for 3% of the time, Pallas kernels for 7%

profile of v7, /device:TPU:1, one launch (start us, length us, event | category | flops | bytes accessed | tf_op | source)
XLA Modules:
  0.0 761.6 jit_solution(17681766678885089650)
XLA Ops:
  28.2 13.1 %all-to-all-done.refs_1_ = bf16[32,6,2048]{2,1,0:T(8,128)(2,1)S(1)} async-done(((bf16[32,6,2048]{2,1,0:T(8,128)(2,1)}), bf16[32,6,2048]{2,1,0:T(8,128)(2,1)S(1)}, u32[]{:S(2)}, u32[]{:S(2)}) %all-to-all-start) | async-done | bytes 786464 | tf_op jit(solution)/shard_map/all_to_all | solution.py:514
  49.2 22.1 %collective-permute-done.2 = bf16[2048,256]{1,0:T(8,128)(2,1)} collective-permute-done((bf16[2048,256]{1,0:T(8,128)(2,1)S(1)}, bf16[2048,256]{1,0:T(8,128)(2,1)}, u32[]{:S(2)}, u32[]{:S(2)}) %collective-permute-start.2) | collective-permute-done | bytes 1048608 | tf_op jit(solution)/shard_map/ppermute | solution.py:718
  184.6 15.7 %all_to_all.160.received = bf16[32,3,2048]{2,1,0:T(4,128)(2,1)S(1)} all-to-all(bf16[32,3,2048]{2,1,0:T(4,128)(2,1)} %copy-done.28), channel_id=1, replica_groups=mesh['section'=8,'expert'=32] {'expert'}, dimensions={0} | all-to-all | bytes 786432 | tf_op jit(solution)/shard_map/all_to_all | solution.py:514
  201.2 15.2 %all_to_all.161.returned = bf16[32,3,2048]{2,1,0:T(4,128)(2,1)S(1)} all-to-all(bf16[32,3,2048]{2,1,0:T(4,128)(2,1)S(1)} %get-tuple-element.178), channel_id=1, replica_groups=mesh['section'=8,'expert'=32] {'expert'}, dimensions={0} | all-to-all | bytes 786432 | tf_op jit(solution)/shard_map/all_to_all | solution.py:514
  237.4 16.0 %all_to_all.162.received = bf16[32,3,2048]{2,1,0:T(4,128)(2,1)S(1)} all-to-all(bf16[32,3,2048]{2,1,0:T(4,128)(2,1)S(1)} %shard_map.148), channel_id=1, replica_groups=mesh['section'=8,'expert'=32] {'expert'}, dimensions={0} | all-to-all | bytes 786432 | tf_op jit(solution)/shard_map/all_to_all | solution.py:514
  255.8 15.2 %all_to_all.163.returned = bf16[32,3,2048]{2,1,0:T(4,128)(2,1)S(1)} all-to-all(bf16[32,3,2048]{2,1,0:T(4,128)(2,1)S(1)} %get-tuple-element.188), channel_id=1, replica_groups=mesh['section'=8,'expert'=32] {'expert'}, dimensions={0} | all-to-all | bytes 786432 | tf_op jit(solution)/shard_map/all_to_all | solution.py:514
  272.0 15.2 %all_to_all.164.received = bf16[32,3,2048]{2,1,0:T(4,128)(2,1)S(1)} all-to-all(bf16[32,3,2048]{2,1,0:T(4,128)(2,1)S(1)} %get-tuple-element.190), channel_id=1, replica_groups=mesh['section'=8,'expert'=32] {'expert'}, dimensions={0} | all-to-all | bytes 786432 | tf_op jit(solution)/shard_map/all_to_all | solution.py:514
  288.1 15.2 %all_to_all.165.returned = bf16[32,3,2048]{2,1,0:T(4,128)(2,1)S(1)} all-to-all(bf16[32,3,2048]{2,1,0:T(4,128)(2,1)S(1)} %get-tuple-element.193), channel_id=1, replica_groups=mesh['section'=8,'expert'=32] {'expert'}, dimensions={0} | all-to-all | bytes 786432 | tf_op jit(solution)/shard_map/all_to_all | solution.py:514
  320.0 15.6 %all_to_all.166.received = bf16[32,3,2048]{2,1,0:T(4,128)(2,1)S(1)} all-to-all(bf16[32,3,2048]{2,1,0:T(4,128)(2,1)S(1)} %shard_map.153), channel_id=1, replica_groups=mesh['section'=8,'expert'=32] {'expert'}, dimensions={0} | all-to-all | bytes 786432 | tf_op jit(solution)/shard_map/all_to_all | solution.py:514
  338.1 15.2 %all_to_all.167.returned = bf16[32,3,2048]{2,1,0:T(4,128)(2,1)S(1)} all-to-all(bf16[32,3,2048]{2,1,0:T(4,128)(2,1)S(1)} %get-tuple-element.204), channel_id=1, replica_groups=mesh['section'=8,'expert'=32] {'expert'}, dimensions={0} | all-to-all | bytes 786432 | tf_op jit(solution)/shard_map/all_to_all | solution.py:514
  354.2 15.2 %all_to_all.168.received = bf16[32,3,2048]{2,1,0:T(4,128)(2,1)S(1)} all-to-all(bf16[32,3,2048]{2,1,0:T(4,128)(2,1)S(1)} %get-tuple-element.206), channel_id=1, replica_groups=mesh['section'=8,'expert'=32] {'expert'}, dimensions={0} | all-to-all | bytes 786432 | tf_op jit(solution)/shard_map/all_to_all | solution.py:514
  404.4 15.2 %all_to_all.169.refs_1_ = bf16[32,3,2048]{2,1,0:T(4,128)(2,1)S(1)} all-to-all(bf16[32,3,2048]{2,1,0:T(4,128)(2,1)S(1)} %shard_map.159), channel_id=1, replica_groups=mesh['section'=8,'expert'=32] {'expert'}, dimensions={0} | all-to-all | bytes 786432 | tf_op jit(solution)/shard_map/all_to_all | solution.py:514
  443.5 18.7 %all_to_all.170.refs_1_ = bf16[32,3,2048]{2,1,0:T(4,128)(2,1)S(1)} all-to-all(bf16[32,3,2048]{2,1,0:T(4,128)(2,1)} %copy-done.27), channel_id=1, replica_groups=mesh['section'=8,'expert'=32] {'expert'}, dimensions={0} | all-to-all | bytes 786432 | tf_op jit(solution)/shard_map/all_to_all | solution.py:514
  466.3 15.5 %all_to_all.171.returned = bf16[32,3,2048]{2,1,0:T(4,128)(2,1)S(1)} all-to-all(bf16[32,3,2048]{2,1,0:T(4,128)(2,1)S(1)} %get-tuple-element.236), channel_id=1, replica_groups=mesh['section'=8,'expert'=32] {'expert'}, dimensions={0} | all-to-all | bytes 786432 | tf_op jit(solution)/shard_map/all_to_all | solution.py:514
  496.4 19.4 %all_to_all.172.received = bf16[32,3,2048]{2,1,0:T(4,128)(2,1)S(1)} all-to-all(bf16[32,3,2048]{2,1,0:T(4,128)(2,1)S(1)} %shard_map.165), channel_id=1, replica_groups=mesh['section'=8,'expert'=32] {'expert'}, dimensions={0} | all-to-all | bytes 786432 | tf_op jit(solution)/shard_map/all_to_all | solution.py:514
  518.0 16.7 %all_to_all.173.returned = bf16[32,3,2048]{2,1,0:T(4,128)(2,1)S(1)} all-to-all(bf16[32,3,2048]{2,1,0:T(4,128)(2,1)S(1)} %get-tuple-element.241), channel_id=1, replica_groups=mesh['section'=8,'expert'=32] {'expert'}, dimensions={0} | all-to-all | bytes 786432 | tf_op jit(solution)/shard_map/all_to_all | solution.py:514
  535.8 16.1 %all_to_all.174.received = bf16[32,3,2048]{2,1,0:T(4,128)(2,1)S(1)} all-to-all(bf16[32,3,2048]{2,1,0:T(4,128)(2,1)S(1)} %get-tuple-element.242), channel_id=1, replica_groups=mesh['section'=8,'expert'=32] {'expert'}, dimensions={0} | all-to-all | bytes 786432 | tf_op jit(solution)/shard_map/all_to_all | solution.py:514
  555.0 15.6 %all_to_all.175.returned = bf16[32,3,2048]{2,1,0:T(4,128)(2,1)S(1)} all-to-all(bf16[32,3,2048]{2,1,0:T(4,128)(2,1)S(1)} %get-tuple-element.248), channel_id=1, replica_groups=mesh['section'=8,'expert'=32] {'expert'}, dimensions={0} | all-to-all | bytes 786432 | tf_op jit(solution)/shard_map/all_to_all | solution.py:514
  584.7 16.0 %all_to_all.176.received = bf16[32,3,2048]{2,1,0:T(4,128)(2,1)S(1)} all-to-all(bf16[32,3,2048]{2,1,0:T(4,128)(2,1)S(1)} %shard_map.170), channel_id=1, replica_groups=mesh['section'=8,'expert'=32] {'expert'}, dimensions={0} | all-to-all | bytes 786432 | tf_op jit(solution)/shard_map/all_to_all | solution.py:514
  602.9 15.2 %all_to_all.177.returned = bf16[32,3,2048]{2,1,0:T(4,128)(2,1)S(1)} all-to-all(bf16[32,3,2048]{2,1,0:T(4,128)(2,1)S(1)} %get-tuple-element.252), channel_id=1, replica_groups=mesh['section'=8,'expert'=32] {'expert'}, dimensions={0} | all-to-all | bytes 786432 | tf_op jit(solution)/shard_map/all_to_all | solution.py:514
  619.1 15.5 %all_to_all.178.received = bf16[32,3,2048]{2,1,0:T(4,128)(2,1)S(1)} all-to-all(bf16[32,3,2048]{2,1,0:T(4,128)(2,1)S(1)} %get-tuple-element.253), channel_id=1, replica_groups=mesh['section'=8,'expert'=32] {'expert'}, dimensions={0} | all-to-all | bytes 786432 | tf_op jit(solution)/shard_map/all_to_all | solution.py:514
  637.7 15.2 %all_to_all.179.returned = bf16[32,3,2048]{2,1,0:T(4,128)(2,1)S(1)} all-to-all(bf16[32,3,2048]{2,1,0:T(4,128)(2,1)S(1)} %get-tuple-element.259), channel_id=1, replica_groups=mesh['section'=8,'expert'=32] {'expert'}, dimensions={0} | all-to-all | bytes 786432 | tf_op jit(solution)/shard_map/all_to_all | solution.py:514
  672.2 15.4 %all_to_all.180.received = bf16[32,3,2048]{2,1,0:T(4,128)(2,1)S(1)} all-to-all(bf16[32,3,2048]{2,1,0:T(4,128)(2,1)S(1)} %shard_map.175), channel_id=1, replica_groups=mesh['section'=8,'expert'=32] {'expert'}, dimensions={0} | all-to-all | bytes 786432 | tf_op jit(solution)/shard_map/all_to_all | solution.py:514
  689.8 15.3 %all_to_all.181.returned = bf16[32,3,2048]{2,1,0:T(4,128)(2,1)S(1)} all-to-all(bf16[32,3,2048]{2,1,0:T(4,128)(2,1)S(1)} %get-tuple-element.264), channel_id=1, replica_groups=mesh['section'=8,'expert'=32] {'expert'}, dimensions={0} | all-to-all | bytes 786432 | tf_op jit(solution)/shard_map/all_to_all | solution.py:514
  (274 shorter events, 362.2 us)
Async XLA Ops:
  8.7 17.7 %collective-permute-start = (f32[4,64]{1,0:T(4,128)S(1)}, f32[4,64]{1,0:T(4,128)S(1)}, u32[]{:S(2)}, u32[]{:S(2)}) collective-permute-start(f32[4,64]{1,0:T(4,128)S(1)} %pad_maximum_fusion.2), channel_id=1, source_target_pairs={{0,32},{64,96},{128,160},{192,224},{32,0},{96,64},{160,128},{224,1... | collective-permute-start | bytes 3080 | tf_op jit(solution)/shard_map/ppermute | solution.py:718
  16.1 25.2 %all-to-all-start = ((bf16[32,6,2048]{2,1,0:T(8,128)(2,1)}), bf16[32,6,2048]{2,1,0:T(8,128)(2,1)S(1)}, u32[]{:S(2)}, u32[]{:S(2)}) async-start(bf16[32,6,2048]{2,1,0:T(8,128)(2,1)} %copy-done.9), calls=%async_computation | async-start | bytes 2097152 | tf_op jit(solution)/shard_map/all_to_all | solution.py:514
  24.2 25.1 %collective-permute-start.1 = (bf16[2048,256]{1,0:T(8,128)(2,1)S(1)}, bf16[2048,256]{1,0:T(8,128)(2,1)}, u32[]{:S(2)}, u32[]{:S(2)}) collective-permute-start(bf16[2048,256]{1,0:T(8,128)(2,1)S(1)} %bitcast.69), channel_id=1, source_target_pairs={{0,32},{64,96},{128,160},{192,224},{32,0},{96,64},{160,128},{224,1... | collective-permute-start | bytes 3145736 | tf_op jit(solution)/shard_map/ppermute | solution.py:718
  24.3 47.1 %collective-permute-start.2 = (bf16[2048,256]{1,0:T(8,128)(2,1)S(1)}, bf16[2048,256]{1,0:T(8,128)(2,1)}, u32[]{:S(2)}, u32[]{:S(2)}) collective-permute-start(bf16[2048,256]{1,0:T(8,128)(2,1)S(1)} %bitcast.71), channel_id=1, source_target_pairs={{0,32},{64,96},{128,160},{192,224},{32,0},{96,64},{160,128},{224,1... | collective-permute-start | bytes 3145736 | tf_op jit(solution)/shard_map/ppermute | solution.py:718
  45.1 26.2 %all-to-all-start.1 = ((bf16[32,6,2048]{2,1,0:T(8,128)(2,1)}), bf16[32,6,2048]{2,1,0:T(8,128)(2,1)S(1)}, u32[]{:S(2)}, u32[]{:S(2)}) async-start(bf16[32,6,2048]{2,1,0:T(8,128)(2,1)} %copy-done.19), calls=%async_computation.1 | async-start | bytes 2097152 | tf_op jit(solution)/shard_map/all_to_all | solution.py:514
  75.6 25.8 %collective-permute-start.4 = (bf16[256,2048]{1,0:T(8,128)(2,1)}, bf16[256,2048]{1,0:T(8,128)(2,1)}, u32[]{:S(2)}, u32[]{:S(2)}) collective-permute-start(bf16[256,2048]{1,0:T(8,128)(2,1)} %bitcast.5.refs_4_.down_mat), channel_id=1, source_target_pairs={{32,0},{96,64},{160,128},{224,192},{33,1},{97,65},{161,129},{225,1... | collective-permute-start | bytes 3145736 | tf_op jit(solution)/shard_map/ppermute | solution.py:780
  81.7 21.3 %all-to-all-start.2 = ((bf16[32,3,2048]{2,1,0:T(4,128)(2,1)}), bf16[32,3,2048]{2,1,0:T(4,128)(2,1)}, u32[]{:S(2)}, u32[]{:S(2)}) async-start(bf16[32,3,2048]{2,1,0:T(4,128)(2,1)} %shard_map.140), calls=%async_computation.2 | async-start | bytes 1048576 | tf_op jit(solution)/shard_map/all_to_all | solution.py:514
  90.4 38.3 %collective-permute-start.5 = (bf16[256,2048]{1,0:T(8,128)(2,1)}, bf16[256,2048]{1,0:T(8,128)(2,1)}, u32[]{:S(2)}, u32[]{:S(2)}) collective-permute-start(bf16[256,2048]{1,0:T(8,128)(2,1)} %bitcast.5.refs_4_.down_mat), channel_id=1, source_target_pairs={{0,32},{64,96},{128,160},{192,224},{1,33},{65,97},{129,161},{193,2... | collective-permute-start | bytes 3145736 | tf_op jit(solution)/shard_map/ppermute | solution.py:783
  106.1 20.6 %all-to-all-start.3 = ((bf16[32,3,2048]{2,1,0:T(4,128)(2,1)}), bf16[32,3,2048]{2,1,0:T(4,128)(2,1)}, u32[]{:S(2)}, u32[]{:S(2)}) async-start(bf16[32,3,2048]{2,1,0:T(4,128)(2,1)} %copy-done.29), calls=%async_computation.3 | async-start | bytes 1048576 | tf_op jit(solution)/shard_map/all_to_all | solution.py:514
  143.6 16.4 %all-to-all-start.4 = ((bf16[32,3,2048]{2,1,0:T(4,128)(2,1)}), bf16[32,3,2048]{2,1,0:T(4,128)(2,1)}, u32[]{:S(2)}, u32[]{:S(2)}) async-start(bf16[32,3,2048]{2,1,0:T(4,128)(2,1)} %copy-done.14), calls=%async_computation.4 | async-start | bytes 1048576 | tf_op jit(solution)/shard_map/all_to_all | solution.py:514
  164.4 16.8 %all-to-all-start.5 = ((bf16[32,3,2048]{2,1,0:T(4,128)(2,1)}), bf16[32,3,2048]{2,1,0:T(4,128)(2,1)}, u32[]{:S(2)}, u32[]{:S(2)}) async-start(bf16[32,3,2048]{2,1,0:T(4,128)(2,1)} %copy-done.24), calls=%async_computation.5 | async-start | bytes 1048576 | tf_op jit(solution)/shard_map/all_to_all | solution.py:514
  169.5 220.5 %all-gather.3.cloned.1.call-start = ((), (), s32[]{:S(2)}) async-start(), calls=%async_computation.34 | async-start | bytes 9437184 | tf_op jit(solution)/shard_map/all_gather | solution.py:817
  219.8 17.0 %collective-permute-start.9 = (bf16[32,2048]{1,0:T(8,128)(2,1)S(1)}, bf16[32,2048]{1,0:T(8,128)(2,1)S(1)}, u32[]{:S(2)}, u32[]{:S(2)}) collective-permute-start(bf16[32,2048]{1,0:T(8,128)(2,1)S(1)} %get-tuple-element.295), channel_id=1, source_target_pairs={{64,128},{128,64},{96,160},{160,96},{192,0},{0,192},{224,32},{32,2... | collective-permute-start | bytes 393224 | tf_op jit(solution)/shard_map/ppermute | solution.py:728
  303.8 12.9 %collective-permute-start.10 = (bf16[32,2048]{1,0:T(8,128)(2,1)S(1)}, bf16[32,2048]{1,0:T(8,128)(2,1)S(1)}, u32[]{:S(2)}, u32[]{:S(2)}) collective-permute-start(bf16[32,2048]{1,0:T(8,128)(2,1)S(1)} %get-tuple-element.294), channel_id=1, source_target_pairs={{0,64},{64,0},{32,96},{96,32},{128,192},{192,128},{160,224},{224,1... | collective-permute-start | bytes 393224 | tf_op jit(solution)/shard_map/ppermute | solution.py:728
  371.2 16.4 %all-to-all-start.15 = ((bf16[32,3,2048]{2,1,0:T(4,128)(2,1)}), bf16[32,3,2048]{2,1,0:T(4,128)(2,1)}, u32[]{:S(2)}, u32[]{:S(2)}) async-start(bf16[32,3,2048]{2,1,0:T(4,128)(2,1)} %copy-done.26), calls=%async_computation.15 | async-start | bytes 1048576 | tf_op jit(solution)/shard_map/all_to_all | solution.py:514
  422.6 16.4 %all-to-all-start.17 = ((bf16[32,3,2048]{2,1,0:T(4,128)(2,1)}), bf16[32,3,2048]{2,1,0:T(4,128)(2,1)}, u32[]{:S(2)}, u32[]{:S(2)}) async-start(bf16[32,3,2048]{2,1,0:T(4,128)(2,1)} %copy-done.25), calls=%async_computation.17 | async-start | bytes 1048576 | tf_op jit(solution)/shard_map/all_to_all | solution.py:514
  427.2 227.1 %reduce-scatter.2.cloned.1.call-start = ((), (), s32[]{:S(2)}) async-start(), calls=%async_computation.33 | async-start | bytes 8650752 | tf_op jit(solution)/shard_map/reduce_scatter | solution.py:863
  482.6 13.3 %collective-permute-start.14 = (bf16[32,2048]{1,0:T(8,128)(2,1)S(1)}, bf16[32,2048]{1,0:T(8,128)(2,1)S(1)}, u32[]{:S(2)}, u32[]{:S(2)}) collective-permute-start(bf16[32,2048]{1,0:T(8,128)(2,1)S(1)} %get-tuple-element.291), channel_id=1, source_target_pairs={{0,64},{64,0},{32,96},{96,32},{128,192},{192,128},{160,224},{224,1... | collective-permute-start | bytes 393224 | tf_op jit(solution)/shard_map/ppermute | solution.py:728
  655.3 12.9 %collective-permute-start.17 = (bf16[32,2048]{1,0:T(8,128)(2,1)S(1)}, bf16[32,2048]{1,0:T(8,128)(2,1)S(1)}, u32[]{:S(2)}, u32[]{:S(2)}) collective-permute-start(bf16[32,2048]{1,0:T(8,128)(2,1)S(1)} %get-tuple-element.288), channel_id=1, source_target_pairs={{0,64},{64,0},{32,96},{96,32},{128,192},{192,128},{160,224},{224,1... | collective-permute-start | bytes 393224 | tf_op jit(solution)/shard_map/ppermute | solution.py:728
  705.2 14.7 %all-to-all-start.31 = ((bf16[8,2,64,128]{3,2,1,0:T(8,128)(2,1)}), bf16[8,2,64,128]{3,2,1,0:T(8,128)(2,1)S(1)}, u32[]{:S(2)}, u32[]{:S(2)}) async-start(bf16[8,2,64,128]{3,2,1,0:T(8,128)(2,1)} %bitcast.79), calls=%async_computation.32 | async-start | bytes 524288 | tf_op jit(solution)/shard_map/all_to_all | solution.py:868
  712.9 36.3 %collective-permute-start.12 = (bf16[96,2048]{1,0:T(8,128)(2,1)}, bf16[96,2048]{1,0:T(8,128)(2,1)S(1)}, u32[]{:S(2)}, u32[]{:S(2)}) collective-permute-start(bf16[96,2048]{1,0:T(8,128)(2,1)} %get-tuple-element.283), channel_id=1, source_target_pairs={{0,32},{64,96},{128,160},{192,224},{32,0},{96,64},{160,128},{224,1... | collective-permute-start | bytes 1179656 | tf_op jit(solution)/shard_map/ppermute | solution.py:718
  724.1 22.9 %all-to-all-start.30 = ((bf16[32,6,2048]{2,1,0:T(8,128)(2,1)}), bf16[32,6,2048]{2,1,0:T(8,128)(2,1)S(1)}, u32[]{:S(2)}, u32[]{:S(2)}) async-start(bf16[32,6,2048]{2,1,0:T(8,128)(2,1)} %shard_map.178), calls=%async_computation.31 | async-start | bytes 2097152 | tf_op jit(solution)/shard_map/all_to_all | solution.py:514
  731.7 17.5 %collective-permute-start.20 = (bf16[96,2048]{1,0:T(8,128)(2,1)}, bf16[96,2048]{1,0:T(8,128)(2,1)}, u32[]{:S(2)}, u32[]{:S(2)}) collective-permute-start(bf16[96,2048]{1,0:T(8,128)(2,1)} %get-tuple-element.281), channel_id=1, source_target_pairs={{0,32},{64,96},{128,160},{192,224},{32,0},{96,64},{160,128},{224,1... | collective-permute-start | bytes 1179656 | tf_op jit(solution)/shard_map/ppermute | solution.py:718
  733.4 15.8 %collective-permute-start.21 = (bf16[96,768]{1,0:T(8,128)(2,1)}, bf16[96,768]{1,0:T(8,128)(2,1)}, u32[]{:S(2)}, u32[]{:S(2)}) collective-permute-start(bf16[96,768]{1,0:T(8,128)(2,1)} %get-tuple-element.285), channel_id=1, source_target_pairs={{0,32},{64,96},{128,160},{192,224},{32,0},{96,64},{160,128},{224,1... | collective-permute-start | bytes 442376 | tf_op jit(solution)/shard_map/ppermute | solution.py:718
  (59 other events, 570.9 us)
Sparse Core Ops, SparseCore 0:
  184.7 103.1 all-gather.2
  443.6 105.4 reduce-scatter.1
